TPU v7x, 128 devices: a whole 4x4x4 slice. The times are simulated.
128 devices in a mesh: blk: 32 (over z_lo, y, x), tensor: 4 (over z_hi, core).
Axes of the slice: x: 4, y: 4, z: 4 (z_hi: 2, z_lo: 2; z = z_hi * 2 + z_lo), core: 2. Of those that a mesh axis runs over, the one named last changes fastest.
Arguments:
- inputs: bfloat16 [2, 4096, 2304], P(None, 'blk'), may hold values from -6 to 6
- out_grad: bfloat16 [2, 4096, 2304], P(None, 'blk'), may hold values from -6 to 6
- segment_ids: int32 [2, 4096], P(None, 'blk'), may hold values from 0 to 1, never falling along the last dimension, each value on 1 to 3968 neighbouring positions
- keep_mask: int32 [2, 4096], P(None, 'blk'), may hold values 0 or 1
- query_codes: bfloat16 [2304, 2048], P(None, 'tensor'), may hold values from -128 to 127, as said below
- key_codes: bfloat16 [2304, 1024], P(None, 'tensor'), may hold values from -128 to 127, as said below
- value_codes: bfloat16 [2304, 1024], P(None, 'tensor'), may hold values from -128 to 127, as said below
- output_codes: bfloat16 [2048, 2304], P('tensor'), may hold values from -128 to 127, as said below
- gate_codes: bfloat16 [2304, 9216], P(None, 'tensor'), may hold values from -128 to 127, as said below
- up_codes: bfloat16 [2304, 9216], P(None, 'tensor'), may hold values from -128 to 127, as said below
- down_codes: bfloat16 [9216, 2304], P('tensor'), may hold values from -128 to 127, as said below
- norm_attn_in: float32 [2304], replicated, may hold values from 0.25 to 1.75
- norm_attn_out: float32 [2304], replicated, may hold values from 0.25 to 1.75
- norm_ffn_in: float32 [2304], replicated, may hold values from 0.25 to 1.75
- norm_ffn_out: float32 [2304], replicated, may hold values from 0.25 to 1.75
Outputs:
- out_rows: bfloat16 [2, 4096, 2304], P(None, 'blk')
- input_grad: bfloat16 [2, 4096, 2304], P(None, 'blk')
- grad_query: float32 [2304, 2048], P('blk', 'tensor')
- grad_key: float32 [2304, 1024], P('blk', 'tensor')
- grad_value: float32 [2304, 1024], P('blk', 'tensor')
- grad_output: float32 [2048, 2304], P('tensor', 'blk')
- grad_gate: float32 [2304, 9216], P('blk', 'tensor')
- grad_up: float32 [2304, 9216], P('blk', 'tensor')
- grad_down: float32 [9216, 2304], P('tensor', 'blk')
- grad_attn_in: float32 [2304], P('blk')
- grad_attn_out: float32 [2304], P('blk')
- grad_ffn_in: float32 [2304], P('blk')
- grad_ffn_out: float32 [2304], P('blk')
Inputs may be any that keep to these rules, and one draw needn't show every extreme that they name: `segment_ids`: document numbers never fall along a row; a document has at most 3968 tokens. `query_codes`: whole numbers. `key_codes`: whole numbers. `value_codes`: whole numbers. `output_codes`: whole numbers. `gate_codes`: whole numbers. `up_codes`: whole numbers. `down_codes`: whole numbers.
All inputs are finite; a program needn't handle non-finite values. No bound on the sum of `keep_mask` on one device may be relied on, other than what follows from the above.
Results may differ from a plain program's by a relative error of at most 0.035.
Values may be sent and summed in bfloat16 or wider, within the bound.
A program may use at most 320 MiB of HBM per device.

v0:
```python
import jax
import jax.numpy as jnp
from jax import lax
from jax.sharding import PartitionSpec as P

D = 2304
HEADS = 8
HD = 256
FF = 9216


CAP = 50.0
EPS = 1e-06
LEVEL_SCALE = 1.0 / 74.0
WIDTHS = (8, 4, 2)
FLOOR_SCORE = -1e30


def sliced(codes, bits):
    spacing = 2.0 ** (8 - bits)
    upper = 2.0 ** (bits - 1)
    return jnp.clip(jnp.floor(codes / spacing + 0.5), -upper, upper - 1.0) * spacing


def norm_rows(values, gain):
    return values * lax.rsqrt(jnp.mean(values * values, axis=-1, keepdims=True) + EPS) * gain


def norm_back(values, gain, grad):
    return jax.vjp(norm_rows, values, gain)[1](grad)


def rotate(values, cosine, sine):
    half = values.shape[-1] // 2
    first = values[..., :half]
    second = values[..., half:]
    return jnp.concatenate(
        [first * cosine - second * sine, second * cosine + first * sine], axis=-1
    )


def gelu_mix(gate, upper):
    return jax.nn.gelu(gate, approximate=True) * upper


def product(left, right):
    return jnp.dot(left, right, preferred_element_type=jnp.float32)


def cross_rows(left, right):
    return lax.dot_general(
        left, right, (((0,), (0,)), ((), ())), preferred_element_type=jnp.float32
    )


def cross_cols(left, right):
    return lax.dot_general(
        left, right, (((1,), (1,)), ((), ())), preferred_element_type=jnp.float32
    )


def allowed_mask(query_place, query_tag, key_start, key_tags):
    count = key_tags.shape[0]
    key_place = key_start + jnp.arange(count, dtype=jnp.int32)
    earlier = key_place[None, :] <= query_place[:, None]
    same_doc = key_tags.astype(jnp.float32)[None, :] == query_tag[:, None]
    return earlier & same_doc | (key_place[None, :] == query_place[:, None])


def capped_scores(queries, keys, mask):
    raw = jnp.einsum("kgqd,krd->kgqr", queries, keys, preferred_element_type=jnp.float32)
    bent = jnp.tanh(raw * HD ** (-0.5) / CAP)
    capped = jnp.where(mask[None, None], CAP * bent, FLOOR_SCORE)
    return (capped, bent)


def pack_grads(grads, dims, parts):
    flat = []
    for grad, dim in zip(grads, dims):
        leading = grad if dim == 0 else jnp.swapaxes(grad, 0, 1)
        flat.append(leading.reshape(parts, -1))
    return jnp.concatenate(flat, axis=1)


def unpack_grads(packed, grads, dims, parts):
    result = []
    offset = 0
    for grad, dim in zip(grads, dims):
        leading = grad if dim == 0 else jnp.swapaxes(grad, 0, 1)
        shape = (leading.shape[0] // parts,) + leading.shape[1:]
        length = grad.size // parts
        piece = packed[0, offset : offset + length].reshape(shape)
        offset = offset + length
        result.append(piece if dim == 0 else jnp.swapaxes(piece, 0, 1))
    return tuple(result)


def shards(
    inputs,
    out_grad,
    segment_ids,
    keep_mask,
    query_codes,
    key_codes,
    value_codes,
    output_codes,
    gate_codes,
    up_codes,
    down_codes,
    norm_attn_in,
    norm_attn_out,
    norm_ffn_in,
    norm_ffn_out,
):
    batches = inputs.shape[0]
    rows = inputs.shape[1]
    key_heads = key_codes.shape[1] // HD
    group = query_codes.shape[1] // HD // key_heads
    query_heads = key_heads * group
    key_width = key_heads * HD
    parts = lax.axis_size("blk")
    place = lax.axis_index("blk") * rows + jnp.arange(rows, dtype=jnp.int32)
    freqs = 10000.0 ** (-jnp.arange(HD // 2, dtype=jnp.float32) * 2.0 / HD)
    angles = place.astype(jnp.float32)[:, None] * freqs[None, :]
    cosine = jnp.cos(angles)
    sine = jnp.sin(angles)
    in_scale = LEVEL_SCALE * D ** (-0.5)
    mid_scale = LEVEL_SCALE * (HEADS * HD) ** (-0.5)
    ff_scale = LEVEL_SCALE * FF ** (-0.5)
    scatter_dims = (0, 0, 0, 1, 0, 0, 1, 0, 0, 0, 0)
    out_list = []
    grad_list = []
    totals = None
    fresh = None
    for batch in range(batches):
        bits = WIDTHS[batch % 3]
        w_query = (in_scale * sliced(query_codes.astype(jnp.float32), bits)).astype(jnp.bfloat16)
        w_key = (in_scale * sliced(key_codes.astype(jnp.float32), bits)).astype(jnp.bfloat16)
        w_value = (in_scale * sliced(value_codes.astype(jnp.float32), bits)).astype(jnp.bfloat16)
        w_output = (mid_scale * sliced(output_codes.astype(jnp.float32), bits)).astype(jnp.bfloat16)
        w_gate = (in_scale * sliced(gate_codes.astype(jnp.float32), bits)).astype(jnp.bfloat16)
        w_up = (in_scale * sliced(up_codes.astype(jnp.float32), bits)).astype(jnp.bfloat16)
        w_down = (ff_scale * sliced(down_codes.astype(jnp.float32), bits)).astype(jnp.bfloat16)
        tokens = inputs[batch].astype(jnp.float32)
        query_tag = segment_ids[batch].astype(jnp.float32)
        key_tag = jnp.where(keep_mask[batch] == 1, segment_ids[batch], -1).astype(jnp.bfloat16)
        normed = norm_rows(tokens, norm_attn_in).astype(jnp.bfloat16)
        query_raw = product(normed, w_query).reshape(rows, query_heads, HD).transpose(1, 0, 2)
        queries = (
            rotate(query_raw, cosine, sine).astype(jnp.bfloat16).reshape(key_heads, group, rows, HD)
        )
        key_raw = product(normed, w_key).reshape(rows, key_heads, HD).transpose(1, 0, 2)
        key_flat = (
            rotate(key_raw, cosine, sine)
            .astype(jnp.bfloat16)
            .transpose(1, 0, 2)
            .reshape(rows, key_width)
        )
        value_flat = product(normed, w_value).astype(jnp.bfloat16)
        tag_block = jnp.broadcast_to(key_tag[:, None], (rows, HD))
        packed_kv = jnp.concatenate([key_flat, value_flat, tag_block], axis=1)
        start_state = jnp.concatenate(
            [
                jnp.zeros((key_heads, group, rows, HD), jnp.float32),
                jnp.full((key_heads, group, rows, 1), FLOOR_SCORE, jnp.float32),
                jnp.zeros((key_heads, group, rows, 1), jnp.float32),
            ],
            axis=-1,
        )
        piece = lax.all_gather(packed_kv, "blk", axis=0, tiled=True)
        accum = start_state[..., :HD]
        best = start_state[..., HD]
        total = start_state[..., HD + 1]
        count = piece.shape[0]
        keys = piece[:, :key_width].reshape(count, key_heads, HD).transpose(1, 0, 2)
        values = (
            piece[:, key_width : 2 * key_width].reshape(count, key_heads, HD).transpose(1, 0, 2)
        )
        tag_piece = piece[:, 2 * key_width]
        mask = allowed_mask(place, query_tag, jnp.int32(0), tag_piece)
        capped, bent = capped_scores(queries, keys, mask)
        new_best = jnp.maximum(best, jnp.max(capped, axis=-1))
        weights_here = jnp.exp(capped - new_best[..., None])
        fade = jnp.exp(best - new_best)
        total = total * fade + jnp.sum(weights_here, axis=-1)
        accum = accum * fade[..., None] + jnp.einsum(
            "kgqr,krd->kgqd",
            weights_here.astype(jnp.bfloat16),
            values,
            preferred_element_type=jnp.float32,
        )
        folded = jnp.concatenate([accum, new_best[..., None], total[..., None]], axis=-1)
        accum = folded[..., :HD]
        best = folded[..., HD]
        total = folded[..., HD + 1]
        attended = accum / total[..., None]
        log_total = best + jnp.log(total)
        attended_flat = (
            attended.astype(jnp.bfloat16)
            .reshape(query_heads, rows, HD)
            .transpose(1, 0, 2)
            .reshape(rows, query_heads * HD)
        )
        branch = lax.psum(product(attended_flat, w_output).astype(jnp.bfloat16), "tensor").astype(
            jnp.float32
        )
        middle = tokens + norm_rows(branch, norm_attn_out)
        ffn_in = norm_rows(middle, norm_ffn_in).astype(jnp.bfloat16)
        gate = product(ffn_in, w_gate)
        upper = product(ffn_in, w_up)
        hidden = gelu_mix(gate, upper).astype(jnp.bfloat16)
        down = lax.psum(product(hidden, w_down).astype(jnp.bfloat16), "tensor").astype(jnp.float32)
        out_list.append((middle + norm_rows(down, norm_ffn_out)).astype(jnp.bfloat16))
        upstream = out_grad[batch].astype(jnp.float32)
        down_grad, gain_ffn_out = norm_back(down, norm_ffn_out, upstream)
        down_low = down_grad.astype(jnp.bfloat16)
        grad_down = cross_rows(hidden, down_low)
        hidden_grad = cross_cols(down_low, w_down)
        gate_grad, up_grad = jax.vjp(gelu_mix, gate, upper)[1](hidden_grad)
        gate_low = gate_grad.astype(jnp.bfloat16)
        up_low = up_grad.astype(jnp.bfloat16)
        grad_gate = cross_rows(ffn_in, gate_low)
        grad_up = cross_rows(ffn_in, up_low)
        ffn_in_grad = lax.psum(
            (cross_cols(gate_low, w_gate) + cross_cols(up_low, w_up)).astype(jnp.bfloat16), "tensor"
        ).astype(jnp.float32)
        middle_part, gain_ffn_in = norm_back(middle, norm_ffn_in, ffn_in_grad)
        middle_grad = upstream + middle_part
        branch_grad, gain_attn_out = norm_back(branch, norm_attn_out, middle_grad)
        branch_low = branch_grad.astype(jnp.bfloat16)
        grad_output = cross_rows(attended_flat, branch_low)
        attended_grad = cross_cols(branch_low, w_output).astype(jnp.bfloat16)
        attended_heads = (
            attended_grad.reshape(rows, query_heads, HD)
            .transpose(1, 0, 2)
            .reshape(key_heads, group, rows, HD)
        )
        offset = jnp.sum(attended_heads.astype(jnp.float32) * attended, axis=-1)
        packed_all = lax.all_gather(packed_kv, "blk", axis=0, tiled=True)

        def score_parts(start, count):
            keys = packed_all[:, :key_width].reshape(count, key_heads, HD).transpose(1, 0, 2)
            values = (
                packed_all[:, key_width : 2 * key_width]
                .reshape(count, key_heads, HD)
                .transpose(1, 0, 2)
            )
            tag_piece = packed_all[:, 2 * key_width]
            mask = allowed_mask(place, query_tag, start, tag_piece)
            capped, bent = capped_scores(queries, keys, mask)
            probs = jnp.exp(capped - log_total[..., None])
            prob_grad = jnp.einsum(
                "kgqd,krd->kgqr", attended_heads, values, preferred_element_type=jnp.float32
            )
            score_grad = (
                probs * (prob_grad - offset[..., None]) * (1.0 - bent * bent) * HD ** (-0.5)
            ).astype(jnp.bfloat16)
            return (keys, probs, score_grad)

        keys, probs, score_grad = score_parts(0, packed_all.shape[0])
        query_rot_grad = jnp.einsum(
            "kgqr,krd->kgqd", score_grad, keys, preferred_element_type=jnp.float32
        )
        unused, probs_here, grad_here = score_parts(jnp.int32(0), rows * lax.axis_size("blk"))
        key_part = jnp.einsum(
            "kgqr,kgqd->rkd", grad_here, queries, preferred_element_type=jnp.float32
        ).reshape(rows * lax.axis_size("blk"), key_width)
        value_part = jnp.einsum(
            "kgqr,kgqd->rkd",
            probs_here.astype(jnp.bfloat16),
            attended_heads,
            preferred_element_type=jnp.float32,
        ).reshape(rows * lax.axis_size("blk"), key_width)
        key_value_grad = lax.psum_scatter(
            jnp.concatenate([key_part, value_part], axis=1).astype(jnp.bfloat16),
            "blk",
            scatter_dimension=0,
            tiled=True,
        ).astype(jnp.float32)
        key_rot_grad = key_value_grad[:, :key_width].reshape(rows, key_heads, HD).transpose(1, 0, 2)
        key_low = (
            rotate(key_rot_grad, cosine, -sine)
            .transpose(1, 0, 2)
            .reshape(rows, key_width)
            .astype(jnp.bfloat16)
        )
        value_low = key_value_grad[:, key_width:].astype(jnp.bfloat16)
        query_low = (
            rotate(query_rot_grad.reshape(query_heads, rows, HD), cosine, -sine)
            .transpose(1, 0, 2)
            .reshape(rows, query_heads * HD)
            .astype(jnp.bfloat16)
        )
        grad_query = cross_rows(normed, query_low)
        grad_key = cross_rows(normed, key_low)
        grad_value = cross_rows(normed, value_low)
        normed_grad = lax.psum(
            (
                cross_cols(query_low, w_query)
                + cross_cols(key_low, w_key)
                + cross_cols(value_low, w_value)
            ).astype(jnp.bfloat16),
            "tensor",
        ).astype(jnp.float32)
        token_part, gain_attn_in = norm_back(tokens, norm_attn_in, normed_grad)
        grad_list.append((middle_grad + token_part).astype(jnp.bfloat16))
        fresh = (
            in_scale * grad_query,
            in_scale * grad_key,
            in_scale * grad_value,
            mid_scale * grad_output,
            in_scale * grad_gate,
            in_scale * grad_up,
            ff_scale * grad_down,
            gain_attn_in,
            gain_attn_out,
            gain_ffn_in,
            gain_ffn_out,
        )
        totals = (
            fresh if totals is None else tuple((left + right for left, right in zip(totals, fresh)))
        )
    packed_total = pack_grads(totals, scatter_dims, parts)
    summed = lax.psum_scatter(
        packed_total.astype(jnp.bfloat16), "blk", scatter_dimension=0, tiled=True
    ).astype(jnp.float32)
    result = unpack_grads(summed, totals, scatter_dims, parts)
    return (
        jnp.stack(out_list),
        jnp.stack(grad_list),
        result[0],
        result[1],
        result[2],
        result[3],
        result[4],
        result[5],
        result[6],
        result[7],
        result[8],
        result[9],
        result[10],
    )


def solution(mesh):
    placed = (
        P(None, "blk", None),
        P(None, "blk", None),
        P(None, "blk"),
        P(None, "blk"),
        P(None, "tensor"),
        P(None, "tensor"),
        P(None, "tensor"),
        P("tensor", None),
        P(None, "tensor"),
        P(None, "tensor"),
        P("tensor", None),
        P(),
        P(),
        P(),
        P(),
    )
    return jax.shard_map(
        shards,
        mesh=mesh,
        in_specs=placed,
        out_specs=(
            P(None, "blk", None),
            P(None, "blk", None),
            P("blk", "tensor"),
            P("blk", "tensor"),
            P("blk", "tensor"),
            P("tensor", "blk"),
            P("blk", "tensor"),
            P("blk", "tensor"),
            P("tensor", "blk"),
            P("blk"),
            P("blk"),
            P("blk"),
            P("blk"),
        ),
        check_vma=False,
    )
```

profile of v0, /device:TPU:1, one launch (start us, length us, event | category | flops | bytes accessed | tf_op | source)
XLA Modules:
  0.0 1920.8 jit_solution(18215908121158382337)
XLA Ops:
  8.9 2.4 convolution_convert_fusion.3
  17.4 4.1 fusion.266
  21.5 4.3 copy.83
  25.8 2.7 copy.82
  30.3 2.6 convolution_bitcast_fusion.4
  34.0 127.7 %all-gather.5.cloned.1.call-done = bf16[4096,768]{1,0:T(8,128)(2,1)} async-done(((bf16[128,768]{1,0:T(8,128)(2,1)}), bf16[4096,768]{1,0:T(8,128)(2,1)}) %all-gather.5.cloned.1.call-update) | async-done | bytes 6291472 | tf_op jit(solution)/shard_map/all_gather | solution.py:170
  163.2 164.4 %all-gather.3.cloned.1.call-done = bf16[4096,768]{1,0:T(8,128)(2,1)} async-done(((bf16[128,768]{1,0:T(8,128)(2,1)}), bf16[4096,768]{1,0:T(8,128)(2,1)}) %all-gather.3.cloned.1.call-update) | async-done | bytes 6291472 | tf_op jit(solution)/shard_map/all_gather | solution.py:170
  330.4 3.4 fusion.114
  335.8 3.0 fusion.116
  341.5 3.5 fusion.296
  345.1 4.8 fusion.294
  350.1 4.2 convolution_convert_fusion.1
  356.6 66.4 %all-reduce.19.cloned.1.call-done = (bf16[128,2304]{1,0:T(8,128)(2,1)}, bf16[128,2304]{1,0:T(8,128)(2,1)}) async-done(((bf16[128,2304]{1,0:T(8,128)(2,1)}, bf16[128,2304]{1,0:T(8,128)(2,1)}), (bf16[128,2304]{1,0:T(8,128)(2,1)}, bf16[128,2304]{1,0:T(8,128)(2,1)})) %all-reduce.19.cloned.1.call-update) | async-done | bytes 1179664 | tf_op jit(solution)/shard_map/psum | solution.py:204
  430.0 9.4 fusion.95
  439.5 4.9 fusion.43
  444.6 6.6 multiply_convert_fusion.2
  451.1 5.9 multiply_convert_fusion.4
  457.1 6.4 fusion.123
  463.5 5.7 fusion.126
  469.4 46.2 %all-reduce.17.cloned.1.call-done = (bf16[128,2304]{1,0:T(8,128)(2,1)}, bf16[128,2304]{1,0:T(8,128)(2,1)}) async-done(((bf16[128,2304]{1,0:T(8,128)(2,1)}, bf16[128,2304]{1,0:T(8,128)(2,1)}), (bf16[128,2304]{1,0:T(8,128)(2,1)}, bf16[128,2304]{1,0:T(8,128)(2,1)})) %all-reduce.17.cloned.1.call-update) | async-done | bytes 1179664 | tf_op jit(solution)/shard_map/psum | solution.py:212
  518.2 3.1 fusion.252
  521.4 10.9 fusion.243
  532.4 10.1 fusion.89
  542.6 5.7 fusion.236
  548.5 5.0 fusion.37
  553.6 9.5 fusion.120
  563.1 5.7 fusion.117
  569.0 46.4 %all-reduce.15.cloned.1.call-done = (bf16[128,2304]{1,0:T(8,128)(2,1)}, bf16[128,2304]{1,0:T(8,128)(2,1)}) async-done(((bf16[128,2304]{1,0:T(8,128)(2,1)}, bf16[128,2304]{1,0:T(8,128)(2,1)}), (bf16[128,2304]{1,0:T(8,128)(2,1)}, bf16[128,2304]{1,0:T(8,128)(2,1)})) %all-reduce.15.cloned.1.call-update) | async-done | bytes 1179664 | tf_op jit(solution)/shard_map/psum | solution.py:224
  615.4 5.0 fusion.218
  620.6 2.3 fusion.213
  627.3 3.9 fusion.63
  631.4 4.1 fusion.53
  637.9 2.4 pad_maximum_fusion
  641.4 10.0 fusion.524
  651.4 12.3 fusion.30
  663.7 10.5 reshape.1020
  674.3 9.8 fusion.525
  684.1 12.5 fusion.31
  696.6 10.6 reshape.1021
  707.3 10.1 fusion.520
  721.7 5.1 fusion.54
  731.8 2.3 pad_maximum_fusion.1
  735.4 12.0 fusion.32
  747.4 10.8 reshape.1022
  758.9 2.5 fusion.175
  761.4 2.4 fusion.176
  766.7 2.5 reshape.1016
  771.2 2.3 fusion.83
  773.4 3.0 reshape.1019
  781.9 3.2 constant_dynamic-update-slice_fusion.6
  788.1 164.5 %reduce-scatter.5.cloned.1.call-done = bf16[128,512]{1,0:T(8,128)(2,1)} async-done(((bf16[4096,512]{1,0:T(8,128)(2,1)}), bf16[128,512]{1,0:T(8,128)(2,1)}) %reduce-scatter.5.cloned.1.call-update) | async-done | bytes 131088 | tf_op jit(solution)/shard_map/reduce_scatter | solution.py:274
  954.8 3.0 fusion.290
  961.7 2.4 reshape.1017
  967.2 2.6 reshape.1018
  977.9 2.5 constant_dynamic-update-slice_fusion.5
  983.2 11.2 constant_dynamic-update-slice_fusion.2
  994.4 5.1 constant_dynamic-update-slice_fusion.1
  999.5 4.8 constant_dynamic-update-slice_fusion
  1004.2 40.3 %all-reduce.13.cloned.1.call-done = (bf16[128,2304]{1,0:T(8,128)(2,1)}, bf16[128,2304]{1,0:T(8,128)(2,1)}) async-done(((bf16[128,2304]{1,0:T(8,128)(2,1)}, bf16[128,2304]{1,0:T(8,128)(2,1)}), (bf16[128,2304]{1,0:T(8,128)(2,1)}, bf16[128,2304]{1,0:T(8,128)(2,1)})) %all-reduce.13.cloned.1.call-update) | async-done | bytes 1179664 | tf_op jit(solution)/shard_map/psum | solution.py:297
  1044.5 3.0 fusion.219
  1054.9 2.4 pad_maximum_fusion.2
  1061.1 832.1 %all-reduce.11.cloned.1.call-done = bf16[32,608544]{1,0:T(8,128)(2,1)} async-done(((bf16[32,608544]{1,0:T(8,128)(2,1)}), bf16[32,608544]{1,0:T(8,128)(2,1)}) %all-reduce.11.cloned.1.call-update) | async-done | bytes 38946832
  1893.2 6.5 dynamic-slice_convert_fusion
  1900.9 7.0 slice_reduce_fusion
  (451 shorter events, 102.6 us)
Async XLA Ops:
  7.2 154.5 %all-gather.5.cloned.1.call-start = ((), (), s32[]{:S(2)}) async-start(), calls=%async_computation.3 | async-start | bytes 6488064 | tf_op jit(solution)/shard_map/all_gather | solution.py:170
  8.8 21.4 %copy-start.80 = (f32[128]{0:T(128)}, f32[128]{0:T(128)S(1)}, u32[]{:S(2)}) copy-start(f32[128]{0:T(128)S(1)} %fusion.364) | copy-start | bytes 1540
  14.5 313.1 %all-gather.3.cloned.1.call-start = ((), (), s32[]{:S(2)}) async-start(), calls=%async_computation.2 | async-start | bytes 6488064 | tf_op jit(solution)/shard_map/all_gather | solution.py:170
  17.3 405.6 %all-reduce.19.cloned.1.call-start = ((), (), s32[]{:S(2)}) async-start(), calls=%async_computation.10 | async-start | bytes 2359296 | tf_op jit(solution)/shard_map/psum | solution.py:204
  33.8 295.4 %copy-start.107 = (f32[128]{0:T(128)S(1)}, f32[128]{0:T(128)}, u32[]{:S(2)}) copy-start(f32[128]{0:T(128)} %get-tuple-element.116) | copy-start | bytes 1540
  33.8 295.4 %copy-start.108 = (f32[128]{0:T(128)S(1)}, f32[128]{0:T(128)}, u32[]{:S(2)}) copy-start(f32[128]{0:T(128)} %get-tuple-element.117) | copy-start | bytes 1540
  33.9 299.9 %copy-start.65 = (bf16[2,128,128]{2,1,0:T(8,128)(2,1)}, bf16[2,128,128]{2,1,0:T(8,128)(2,1)S(1)}, u32[]{:S(2)}) copy-start(bf16[2,128,128]{2,1,0:T(8,128)(2,1)S(1)} %get-tuple-element.93) | copy-start | bytes 196612
  33.9 299.9 %copy-start.67 = (bf16[2,128,128]{2,1,0:T(8,128)(2,1)}, bf16[2,128,128]{2,1,0:T(8,128)(2,1)S(1)}, u32[]{:S(2)}) copy-start(bf16[2,128,128]{2,1,0:T(8,128)(2,1)S(1)} %get-tuple-element.94) | copy-start | bytes 196612
  33.9 301.9 %copy-start.61 = (bf16[2,128,128]{2,1,0:T(8,128)(2,1)}, bf16[2,128,128]{2,1,0:T(8,128)(2,1)S(1)}, u32[]{:S(2)}) copy-start(bf16[2,128,128]{2,1,0:T(8,128)(2,1)S(1)} %get-tuple-element.79) | copy-start | bytes 196612
  33.9 301.9 %copy-start.63 = (bf16[2,128,128]{2,1,0:T(8,128)(2,1)}, bf16[2,128,128]{2,1,0:T(8,128)(2,1)S(1)}, u32[]{:S(2)}) copy-start(bf16[2,128,128]{2,1,0:T(8,128)(2,1)S(1)} %get-tuple-element.80) | copy-start | bytes 196612
  330.4 11.1 copy-start.33
  330.4 14.7 copy-start.31
  356.5 70.2 %copy-start.57 = (f32[2304]{0:T(1024)S(1)}, f32[2304]{0:T(1024)}, u32[]{:S(2)}) copy-start(f32[2304]{0:T(1024)} %param.27) | copy-start | bytes 27652
  356.5 72.7 %copy-start.73 = (f32[2304]{0:T(1024)S(1)}, f32[2304]{0:T(1024)}, u32[]{:S(2)}) copy-start(f32[2304]{0:T(1024)} %param.28) | copy-start | bytes 27652
  356.5 159.1 %all-reduce.17.cloned.1.call-start = ((), (), s32[]{:S(2)}) async-start(), calls=%async_computation.9 | async-start | bytes 2359296 | tf_op jit(solution)/shard_map/psum | solution.py:212
  429.2 10.3 slice-start.18
  430.0 14.5 copy-start.17
  430.0 21.2 %copy-start.15 = (bf16[128,2304]{1,0:T(8,128)(2,1)}, bf16[128,2304]{1,0:T(8,128)(2,1)S(1)}, u32[]{:S(2)}) copy-start(bf16[128,2304]{1,0:T(8,128)(2,1)S(1)} %get-tuple-element.71) | copy-start | bytes 1769476
  430.0 14.5 slice-start.12
  430.0 14.5 slice-start.13
  444.5 12.5 slice-start.6
  444.5 12.5 slice-start.7
  469.1 49.1 %copy-start.6 = (bf16[2,128,2304]{2,1,0:T(8,128)(2,1)S(1)}, bf16[2,128,2304]{2,1,0:T(8,128)(2,1)}, u32[]{:S(2)}) copy-start(bf16[2,128,2304]{2,1,0:T(8,128)(2,1)} %param.16) | copy-start | bytes 3538948
  469.1 49.1 %copy-start.59 = (f32[2304]{0:T(1024)S(1)}, f32[2304]{0:T(1024)}, u32[]{:S(2)}) copy-start(f32[2304]{0:T(1024)} %param.29) | copy-start | bytes 27652
  469.2 146.2 %all-reduce.15.cloned.1.call-start = ((), (), s32[]{:S(2)}) async-start(), calls=%async_computation.8 | async-start | bytes 2359296 | tf_op jit(solution)/shard_map/psum | solution.py:224
  516.9 25.6 %copy-start.91 = (f32[128]{0:T(128)}, f32[128]{0:T(128)S(1)}, u32[]{:S(2)}) copy-start(f32[128]{0:T(128)S(1)} %fusion.363) | copy-start | bytes 1540
  518.2 14.1 copy-start.99
  521.3 11.0 copy-start.113
  521.3 21.2 %slice-start.9 = ((s8[10616832]{0:T(1024)(128)(4,1)}), s8[4194304]{0:T(1024)(128)(4,1)S(1)}, s32[]{:S(2)}) async-start(s8[10616832]{0:T(1024)(128)(4,1)} %bitcast.385), calls=%async_computation.20 | async-start | bytes 8388608
  521.3 21.2 %slice-start.10 = ((s8[10616832]{0:T(1024)(128)(4,1)}), s8[4194304]{0:T(1024)(128)(4,1)S(1)}, s32[]{:S(2)}) async-start(s8[10616832]{0:T(1024)(128)(4,1)} %bitcast.385), calls=%async_computation.21 | async-start | bytes 8388608
  532.3 21.2 %copy-start.49 = (bf16[128,2304]{1,0:T(8,128)(2,1)}, bf16[128,2304]{1,0:T(8,128)(2,1)S(1)}, u32[]{:S(2)}) copy-start(bf16[128,2304]{1,0:T(8,128)(2,1)S(1)} %get-tuple-element.65) | copy-start | bytes 1769476
  532.3 10.3 copy-start.11
  532.3 10.3 slice-start.11
  532.3 10.3 copy-start.130
  532.4 16.0 slice-start.15
  532.4 16.0 slice-start.16
  548.4 14.7 copy-start.45
  548.5 14.6 slice-start.21
  548.5 14.6 slice-start.22
  563.1 52.3 %copy-start.1 = (bf16[2,128,2304]{2,1,0:T(8,128)(2,1)S(1)}, bf16[2,128,2304]{2,1,0:T(8,128)(2,1)}, u32[]{:S(2)}) copy-start(bf16[2,128,2304]{2,1,0:T(8,128)(2,1)} %param.15) | copy-start | bytes 3538948
  563.1 52.3 %copy-start.3 = (bf16[128,2304]{1,0:T(8,128)(2,1)S(1)}, bf16[128,2304]{1,0:T(8,128)(2,1)}, u32[]{:S(2)}) copy-start(bf16[128,2304]{1,0:T(8,128)(2,1)} %get-tuple-element.52) | copy-start | bytes 1769476
  563.1 52.2 %copy-start.5 = (bf16[128,2304]{1,0:T(8,128)(2,1)S(1)}, bf16[128,2304]{1,0:T(8,128)(2,1)}, u32[]{:S(2)}) copy-start(bf16[128,2304]{1,0:T(8,128)(2,1)} %get-tuple-element.53) | copy-start | bytes 1769476
  563.1 52.2 %copy-start.58 = (f32[2304]{0:T(1024)S(1)}, f32[2304]{0:T(1024)}, u32[]{:S(2)}) copy-start(f32[2304]{0:T(1024)} %param.27) | copy-start | bytes 27652
  563.1 52.2 %copy-start.88 = (f32[128]{0:T(128)S(1)}, f32[128]{0:T(128)}, u32[]{:S(2)}) copy-start(f32[128]{0:T(128)} %copy-done.87) | copy-start | bytes 1540
  568.9 217.7 %reduce-scatter.3.cloned.1.call-start = ((), (), s32[]{:S(2)}) async-start(), calls=%async_computation.4 | async-start | bytes 4325376 | tf_op jit(solution)/shard_map/reduce_scatter | solution.py:274
  640.4 11.1 copy-start.18
  640.4 312.2 %reduce-scatter.5.cloned.1.call-start = ((), (), s32[]{:S(2)}) async-start(), calls=%async_computation.5 | async-start | bytes 4325376 | tf_op jit(solution)/shard_map/reduce_scatter | solution.py:274
  696.6 10.6 copy-start.12
  696.6 10.6 copy-start.60
  696.6 10.6 copy-start.92
  734.2 310.3 %all-reduce.13.cloned.1.call-start = ((), (), s32[]{:S(2)}) async-start(), calls=%async_computation.7 | async-start | bytes 2359296 | tf_op jit(solution)/shard_map/psum | solution.py:297
  747.4 10.8 copy-start.75
  747.4 10.8 copy-start.76
  747.4 11.5 copy-start.36
  977.9 915.4 %all-reduce.11.cloned.1.call-start = ((), (), s32[]{:S(2)}) async-start(), calls=%async_computation.6 | async-start | bytes 77905920
  981.5 12.8 slice-start
  983.2 11.2 slice-start.1
  983.2 11.2 slice-start.2
  983.2 16.2 slice-start.3
  983.2 16.2 slice-start.4
  999.5 45.0 %copy-start.86 = (f32[128]{0:T(128)S(1)}, f32[128]{0:T(128)}, u32[]{:S(2)}) copy-start(f32[128]{0:T(128)} %copy-done.82) | copy-start | bytes 1540
  1004.2 44.7 %copy-start.78 = (bf16[32,72]{1,0:T(8,128)(2,1)S(1)}, bf16[32,72]{1,0:T(8,128)(2,1)}, u32[]{:S(2)}) copy-start(bf16[32,72]{1,0:T(8,128)(2,1)} %add.434) | copy-start | bytes 13828
  1004.2 46.2 %copy-start.79 = (bf16[32,72]{1,0:T(8,128)(2,1)S(1)}, bf16[32,72]{1,0:T(8,128)(2,1)}, u32[]{:S(2)}) copy-start(bf16[32,72]{1,0:T(8,128)(2,1)} %add.436) | copy-start | bytes 13828
  1004.2 47.7 %copy-start.77 = (bf16[32,72]{1,0:T(8,128)(2,1)S(1)}, bf16[32,72]{1,0:T(8,128)(2,1)}, u32[]{:S(2)}) copy-start(bf16[32,72]{1,0:T(8,128)(2,1)} %add.438) | copy-start | bytes 13828
  (102 other events, 373.8 us)
Sparse Core Ops, SparseCore 0:
  14.6 146.9 all-gather.4
  163.8 163.7 all-gather.2
  356.6 66.2 all-reduce.18
  469.3 46.2 all-reduce.16
  569.0 46.2 all-reduce.14
  640.5 146.0 reduce-scatter.2
  789.0 163.5 reduce-scatter.4
  978.0 66.4 all-reduce.12
  1053.6 839.5 all-reduce.10
where the time goes:
time: 1930 us; the launch traced here: 1920 us
  waiting for transfers between devices  1490 us (77%)
  matrix products  231 us (12%)
  local copies, waits for them, and re-layouts  118 us (6%)
  other arithmetic  65.7 us (3%)
    unnamed x10, waiting for transfers between devices  832 us
    all_gather x2, waiting for transfers between devices, shards(): piece = lax.all_gather(packed_kv, 'blk', axis=0, tiled=True)  292 us
    reduce_scatter x2, waiting for transfers between devices, shards(): lax.psum_scatter(jnp.concatenate([key_part, value_part], axis=1).astype(j...  166 us
    dot_general x14, matrix products, cross_rows(): lax.dot_general(left, right, (((0,), (0,)), ((), ())), preferred_element_...  78 us
    psum x1, waiting for transfers between devices, shards(): lax.psum(product(attended_flat, w_output).astype(jnp.bfloat16), 'tensor')  66.4 us
    dot_general x14, matrix products, cross_cols(): lax.dot_general(left, right, (((1,), (1,)), ((), ())), preferred_element_...  62 us
    dot_general x14, matrix products, product(): return jnp.dot(left, right, preferred_element_type=jnp.float32)  54.5 us
    unnamed x325, local copies, waits for them, and re-layouts  46.9 us
  transfers between devices with their start and end apart: 9, of which 9 were waited for; matrix products, arithmetic and copies ran while one was open for 10% of the time, Pallas kernels for 0%

commit v1 on v0

v1 whole, which is shorter than its diff:
```python
import functools

import jax
import jax.numpy as jnp
from jax import lax
from jax.experimental import pallas as pl
from jax.experimental.pallas import tpu as pltpu
from jax.sharding import PartitionSpec as P

D = 2304
HEADS = 8
HD = 256
FF = 9216

CAP = 50.0
EPS = 1e-06
LEVEL_SCALE = 1.0 / 74.0
WIDTHS = (8, 4, 2)

MESH = pl.DeviceIdType.MESH
VMEM = pltpu.VMEM
BF = jnp.bfloat16
F32 = jnp.float32
SEQ = 4096
ROWS = 128
TAGROW = 256
MASKED = -2.0


def place_of():
    b = lax.axis_index("blk")
    t = lax.axis_index("tensor")
    return b % 4, (b // 4) % 4, b // 16, t // 2, t % 2


def device_at(x, y, z, zh, c):
    return ((z * 4 + y) * 4 + x, zh * 2 + c)


def greet(peers):
    barrier = pltpu.get_barrier_semaphore()
    for peer in peers:
        pl.semaphore_signal(barrier, inc=1, device_id=peer, device_id_type=MESH)
    pl.semaphore_wait(barrier, len(peers))


def send(src, dst, ssem, rsem, peer):
    copy = pltpu.make_async_remote_copy(
        src_ref=src, dst_ref=dst, send_sem=ssem, recv_sem=rsem, device_id=peer, device_id_type=MESH
    )
    copy.start()
    return copy


def params(collective_id=None, limit=60):
    if collective_id is None:
        return pltpu.CompilerParams(vmem_limit_bytes=limit << 20)
    return pltpu.CompilerParams(
        vmem_limit_bytes=limit << 20, collective_id=collective_id, has_side_effects=True
    )


def whole(space=VMEM):
    return pl.BlockSpec(memory_space=space)


def gather_kernel(a_ref, b_ref, oa, ob, lsem, ssem, rsem):
    x, y, z, zh, c = place_of()
    xs = [device_at((x + j) % 4, y, z, zh, c) for j in (1, 2, 3)]
    ys = [device_at(x, (y + j) % 4, z, zh, c) for j in (1, 2, 3)]
    zp = device_at(x, y, 1 - z, zh, c)
    greet(xs + ys + [zp])
    mine_a = pltpu.make_async_copy(a_ref, oa.at[z, y, x], lsem.at[0])
    mine_b = pltpu.make_async_copy(b_ref, ob.at[z, y, x], lsem.at[1])
    mine_a.start()
    mine_b.start()
    za = send(a_ref, oa.at[z, y, x], ssem.at[0], rsem.at[0], zp)
    zb = send(b_ref, ob.at[z, y, x], ssem.at[1], rsem.at[1], zp)
    done = [za, zb]
    first_a = [send(a_ref, oa.at[z, y, x], ssem.at[2 + j], rsem.at[2 + j], xs[j]) for j in range(3)]
    first_b = [send(b_ref, ob.at[z, y, x], ssem.at[5 + j], rsem.at[5 + j], ys[j]) for j in range(3)]
    za.wait_recv()
    other = 1 - z
    next_a = [
        send(oa.at[other, y, x], oa.at[other, y, x], ssem.at[8 + j], rsem.at[8 + j], xs[j])
        for j in range(3)
    ]
    zb.wait_recv()
    next_b = [
        send(ob.at[other, y, x], ob.at[other, y, x], ssem.at[11 + j], rsem.at[11 + j], ys[j])
        for j in range(3)
    ]
    mine_a.wait()
    mine_b.wait()
    last = []
    for step, (level, copies_a, copies_b) in enumerate(((z, first_a, first_b), (other, next_a, next_b))):
        for copy in copies_a:
            copy.wait_recv()
        for j in range(3):
            k = 14 + 6 * step + j
            last.append(send(oa.at[level, y], oa.at[level, y], ssem.at[k], rsem.at[k], ys[j]))
        for copy in copies_b:
            copy.wait_recv()
        for j in range(3):
            k = 17 + 6 * step + j
            last.append(send(ob.at[level, :, x], ob.at[level, :, x], ssem.at[k], rsem.at[k], xs[j]))
    for copy in last:
        copy.wait_recv()
    for copy in done + first_a + first_b + next_a + next_b + last:
        copy.wait_send()


def gather(a, b):
    return pl.pallas_call(
        gather_kernel,
        out_shape=(
            jax.ShapeDtypeStruct((2, 4, 4) + a.shape, a.dtype),
            jax.ShapeDtypeStruct((2, 4, 4) + b.shape, b.dtype),
        ),
        in_specs=[whole(), whole()],
        out_specs=(whole(), whole()),
        scratch_shapes=[
            pltpu.SemaphoreType.DMA((2,)),
            pltpu.SemaphoreType.DMA((26,)),
            pltpu.SemaphoreType.DMA((26,)),
        ],
        compiler_params=params(1, 30),
    )(a, b)


def scatter_kernel(a_ref, b_ref, oa, ob, r1a, r1b, s1a, s1b, r2a, r2b, s2a, s2b, r3a, r3b, ssem, rsem):
    x, y, z, zh, c = place_of()
    xi = [(x + j) % 4 for j in (1, 2, 3)]
    yi = [(y + j) % 4 for j in (1, 2, 3)]
    xs = [device_at(i, y, z, zh, c) for i in xi]
    ys = [device_at(x, i, z, zh, c) for i in yi]
    zp = device_at(x, y, 1 - z, zh, c)
    greet(xs + ys + [zp])
    one_a = [send(a_ref.at[:, :, xi[j]], r1a.at[j], ssem.at[j], rsem.at[j], xs[j]) for j in range(3)]
    one_b = [send(b_ref.at[:, yi[j]], r1b.at[j], ssem.at[3 + j], rsem.at[3 + j], ys[j]) for j in range(3)]
    for copy in one_a:
        copy.wait_recv()

    def add_a(i, carry):
        zi, k = i // 4, i % 4
        total = a_ref[zi, k, x].astype(F32)
        for j in range(3):
            total = total + r1a[j, zi, k].astype(F32)
        s1a[zi, k] = total.astype(BF)
        return carry

    lax.fori_loop(0, 8, add_a, 0)
    two_a = [send(s1a.at[:, yi[j]], r2a.at[j], ssem.at[6 + j], rsem.at[6 + j], ys[j]) for j in range(3)]
    for copy in one_b:
        copy.wait_recv()

    def add_b(i, carry):
        zi, k = i // 4, i % 4
        total = b_ref[zi, y, k].astype(F32)
        for j in range(3):
            total = total + r1b[j, zi, k].astype(F32)
        s1b[zi, k] = total.astype(BF)
        return carry

    lax.fori_loop(0, 8, add_b, 0)
    two_b = [send(s1b.at[:, xi[j]], r2b.at[j], ssem.at[9 + j], rsem.at[9 + j], xs[j]) for j in range(3)]
    for copy in two_a:
        copy.wait_recv()
    for zi in range(2):
        total = s1a[zi, y].astype(F32)
        for j in range(3):
            total = total + r2a[j, zi].astype(F32)
        s2a[zi] = total.astype(BF)
    three_a = send(s2a.at[1 - z], r3a, ssem.at[12], rsem.at[12], zp)
    for copy in two_b:
        copy.wait_recv()
    for zi in range(2):
        total = s1b[zi, x].astype(F32)
        for j in range(3):
            total = total + r2b[j, zi].astype(F32)
        s2b[zi] = total.astype(BF)
    three_b = send(s2b.at[1 - z], r3b, ssem.at[13], rsem.at[13], zp)
    three_a.wait_recv()
    oa[...] = s2a[z].astype(F32) + r3a[...].astype(F32)
    three_b.wait_recv()
    ob[...] = s2b[z].astype(F32) + r3b[...].astype(F32)
    for copy in one_a + one_b + two_a + two_b + [three_a, three_b]:
        copy.wait_send()


def scatter(a, b):
    ta, tb = a.shape[3:], b.shape[3:]
    return pl.pallas_call(
        scatter_kernel,
        out_shape=(jax.ShapeDtypeStruct(ta, F32), jax.ShapeDtypeStruct(tb, F32)),
        in_specs=[whole(), whole()],
        out_specs=(whole(), whole()),
        scratch_shapes=[
            VMEM((3, 2, 4) + ta, BF),
            VMEM((3, 2, 4) + tb, BF),
            VMEM((2, 4) + ta, BF),
            VMEM((2, 4) + tb, BF),
            VMEM((3, 2) + ta, BF),
            VMEM((3, 2) + tb, BF),
            VMEM((2,) + ta, BF),
            VMEM((2,) + tb, BF),
            VMEM(ta, BF),
            VMEM(tb, BF),
            pltpu.SemaphoreType.DMA((14,)),
            pltpu.SemaphoreType.DMA((14,)),
        ],
        compiler_params=params(2, 40),
    )(a, b)


PIECES = 4


def total_kernel(p_ref, o_ref, r1, h, r2, ssem, rsem):
    x, y, z, zh, c = place_of()
    mate = device_at(x, y, z, zh, 1 - c)
    far = device_at(x, y, z, 1 - zh, c)
    greet([mate, far])
    size = p_ref.shape[1] // PIECES
    rows = [pl.ds(k * size, size) for k in range(PIECES)]
    one = [
        send(p_ref.at[1 - c, rows[k]], r1.at[rows[k]], ssem.at[k], rsem.at[k], mate)
        for k in range(PIECES)
    ]
    two, three = [], []
    for k in range(PIECES):
        one[k].wait_recv()
        h[rows[k]] = (p_ref[c, rows[k]].astype(F32) + r1[rows[k]].astype(F32)).astype(BF)
        i = PIECES + k
        two.append(send(h.at[rows[k]], r2.at[rows[k]], ssem.at[i], rsem.at[i], far))
    for k in range(PIECES):
        two[k].wait_recv()
        o_ref[c, rows[k]] = (h[rows[k]].astype(F32) + r2[rows[k]].astype(F32)).astype(BF)
        i = 2 * PIECES + k
        three.append(send(o_ref.at[c, rows[k]], o_ref.at[c, rows[k]], ssem.at[i], rsem.at[i], mate))
    for k in range(PIECES):
        three[k].wait_recv()
    for copy in one + two + three:
        copy.wait_send()


def total(p, collective_id):
    half = p.shape[1:]
    return pl.pallas_call(
        total_kernel,
        out_shape=jax.ShapeDtypeStruct(p.shape, BF),
        in_specs=[whole()],
        out_specs=whole(),
        scratch_shapes=[
            VMEM(half, BF),
            VMEM(half, BF),
            VMEM(half, BF),
            pltpu.SemaphoreType.DMA((3 * PIECES,)),
            pltpu.SemaphoreType.DMA((3 * PIECES,)),
        ],
        compiler_params=params(collective_id, 30),
    )(p)


CHUNK = 4
KEYS = CHUNK * ROWS


def nt(left, right):
    return lax.dot_general(left, right, (((1,), (1,)), ((), ())), preferred_element_type=F32)


def tn(left, right):
    return lax.dot_general(left, right, (((0,), (0,)), ((), ())), preferred_element_type=F32)


def nn(left, right):
    return jnp.dot(left, right, preferred_element_type=F32)


def load_chunk(k_ref, v_ref, step, m):
    blocks = pl.ds(step * CHUNK, CHUNK)
    keys = k_ref[blocks, m * ROWS : (m + 1) * ROWS, :].reshape(KEYS, HD)
    values = v_ref[blocks, m * ROWS : (m + 1) * ROWS, :].reshape(KEYS, HD)
    tags = k_ref[blocks, TAGROW : TAGROW + 16, m * ROWS : (m + 1) * ROWS].astype(F32)
    tag_row = jnp.concatenate([tags[i, 0:1, :] for i in range(CHUNK)], axis=1)
    return keys, values, tag_row


def allowed(step, tag_row, query_tag, query_place):
    key_place = step * KEYS + lax.broadcasted_iota(jnp.int32, (2 * ROWS, KEYS), 1)
    ok = (key_place <= query_place) & (tag_row == query_tag)
    return ok | (key_place == query_place)


def query_places():
    row = lax.broadcasted_iota(jnp.int32, (2 * ROWS, 1), 0)
    return lax.axis_index("blk") * ROWS + row % ROWS


def attend_kernel(q_ref, t_ref, k_ref, v_ref, o_ref, lse_ref):
    limit = lax.axis_index("blk") // CHUNK + 1
    where = query_places()
    for m in range(2):
        q = q_ref[m]
        tag = t_ref[m]

        def step(i, carry):
            acc, mass = carry
            keys, values, tag_row = load_chunk(k_ref, v_ref, i, m)
            bent = jnp.tanh(nt(q, keys) * (HD ** (-0.5) / CAP))
            e = jnp.where(allowed(i, tag_row, tag, where), jnp.exp(CAP * bent), 0.0)
            mass = mass + jnp.sum(e, axis=-1, keepdims=True)
            return acc + nn(e.astype(BF), values), mass

        acc, mass = lax.fori_loop(
            0, limit, step, (jnp.zeros((2 * ROWS, HD), F32), jnp.zeros((2 * ROWS, 1), F32))
        )
        o_ref[m] = acc / mass
        lse_ref[m] = jnp.log(mass)


def attend(q, tag, k, v):
    return pl.pallas_call(
        attend_kernel,
        out_shape=(
            jax.ShapeDtypeStruct((2, 2 * ROWS, HD), F32),
            jax.ShapeDtypeStruct((2, 2 * ROWS, 1), F32),
        ),
        in_specs=[whole()] * 4,
        out_specs=(whole(), whole()),
        compiler_params=params(None, 40),
    )(q, tag, k, v)


def attend_back_kernel(q_ref, g_ref, lse_ref, off_ref, t_ref, k_ref, v_ref, dq_ref, dk_ref, dv_ref):
    limit = lax.axis_index("blk") // CHUNK + 1
    where = query_places()
    for m in range(2):
        q = q_ref[m]
        g = g_ref[m]
        tag = t_ref[m]
        lse = lse_ref[m]
        off = off_ref[m]
        part = slice(m * ROWS, (m + 1) * ROWS)

        def step(i, dq):
            keys, values, tag_row = load_chunk(k_ref, v_ref, i, m)
            bent = jnp.tanh(nt(q, keys) * (HD ** (-0.5) / CAP))
            p = jnp.where(allowed(i, tag_row, tag, where), jnp.exp(CAP * bent - lse), 0.0)
            dp = nt(g, values)
            ds = (p * (dp - off) * (1.0 - bent * bent) * HD ** (-0.5)).astype(BF)
            blocks = pl.ds(i * CHUNK, CHUNK)
            dk_ref[blocks, part, :] = tn(ds, q).astype(BF).reshape(CHUNK, ROWS, HD)
            dv_ref[blocks, part, :] = tn(p.astype(BF), g).astype(BF).reshape(CHUNK, ROWS, HD)
            return dq + nn(ds, keys)

        dq_ref[m] = lax.fori_loop(0, limit, step, jnp.zeros((2 * ROWS, HD), F32))

        def blank(i, carry):
            blocks = pl.ds(i * CHUNK, CHUNK)
            dk_ref[blocks, part, :] = jnp.zeros((CHUNK, ROWS, HD), BF)
            dv_ref[blocks, part, :] = jnp.zeros((CHUNK, ROWS, HD), BF)
            return carry

        lax.fori_loop(limit, SEQ // KEYS, blank, 0)


def attend_back(q, g, lse, off, tag, k, v):
    return pl.pallas_call(
        attend_back_kernel,
        out_shape=(
            jax.ShapeDtypeStruct((2, 2 * ROWS, HD), F32),
            jax.ShapeDtypeStruct((32, 2 * ROWS, HD), BF),
            jax.ShapeDtypeStruct((32, 2 * ROWS, HD), BF),
        ),
        in_specs=[whole()] * 7,
        out_specs=(whole(),) * 3,
        compiler_params=params(None, 40),
    )(q, g, lse, off, tag, k, v)


PART = 576
SHARE = 72
TILE_A = 512
TILE_B = 256
COLS_A = 4608
COLS_B = 3840
SPANS_B = ((0, 9), (9, 13), (13, 15))
COLS_G = COLS_B + 128


def grads_kernel(
    da, ca, db, gb, cb, oa, ob,
    rda, rca, rdb, rgb, rcb, pa, pb, r2a, r2b, sa, sb, r3a, r3b, ssem, rsem,
):
    x, y, z, zh, c = place_of()
    xi = [(x + j) % 4 for j in (1, 2, 3)]
    yi = [(y + j) % 4 for j in (1, 2, 3)]
    xs = [device_at(i, y, z, zh, c) for i in xi]
    ys = [device_at(x, i, z, zh, c) for i in yi]
    zp = device_at(x, y, 1 - z, zh, c)
    greet(xs + ys + [zp])
    copies = []

    def post(src, dst, peer):
        k = len(copies)
        copies.append(send(src, dst, ssem.at[k], rsem.at[k], peer))
        return copies[k]

    got_a, got_b = [], []
    for j in range(3):
        got_a.append(post(da.at[xi[j]], rda.at[j], xs[j]))
        got_a.append(post(ca, rca.at[j], xs[j]))
        got_b.append(post(db.at[yi[j]], rdb.at[j], ys[j]))
        got_b.append(post(gb.at[yi[j]], rgb.at[j], ys[j]))
        got_b.append(post(cb, rcb.at[j], ys[j]))
    for copy in got_a:
        copy.wait_recv()

    def rows_a(t, carry):
        cols = pl.ds(pl.multiple_of(t * TILE_A, TILE_A), TILE_A)
        out = nn(da[x], ca[:, cols])
        for j in range(3):
            out = out + nn(rda[j], rca[j, :, cols])
        pa[:, :, :, cols] = out.reshape(2, 4, SHARE, TILE_A).astype(BF)
        return carry

    lax.fori_loop(0, COLS_A // TILE_A, rows_a, 0)
    two_a = [post(pa.at[:, yi[j]], r2a.at[j], ys[j]) for j in range(3)]
    for copy in got_b:
        copy.wait_recv()
    for which in range(3):

        def rows_b(t, carry):
            cols = pl.ds(pl.multiple_of(t * TILE_B, TILE_B), TILE_B)
            out = nn(db[y, which], cb[:, cols])
            for j in range(3):
                out = out + nn(rdb[j, which], rcb[j, :, cols])
            pb[:, :, :, cols] = out.reshape(2, 4, SHARE, TILE_B).astype(BF)
            return carry

        lax.fori_loop(*SPANS_B[which], rows_b, 0)
    gains = gb[y].astype(F32)
    for j in range(3):
        gains = gains + rgb[j].astype(F32)
    pb[:, :, :, COLS_B:] = gains.reshape(2, 4, SHARE, 128).astype(BF)
    two_b = [post(pb.at[:, xi[j]], r2b.at[j], xs[j]) for j in range(3)]

    for copy in two_a:
        copy.wait_recv()

    def adds_a(t, carry):
        cols = pl.ds(pl.multiple_of(t * TILE_A, TILE_A), TILE_A)
        for zi in range(2):
            out = pa[zi, y, :, cols].astype(F32)
            for j in range(3):
                out = out + r2a[j, zi, :, cols].astype(F32)
            sa[zi, :, cols] = out.astype(BF)
        return carry

    lax.fori_loop(0, COLS_A // TILE_A, adds_a, 0)
    three_a = post(sa.at[1 - z], r3a, zp)
    for copy in two_b:
        copy.wait_recv()

    def adds_b(t, carry):
        cols = pl.ds(pl.multiple_of(t * 128, 128), 128)
        for zi in range(2):
            out = pb[zi, x, :, cols].astype(F32)
            for j in range(3):
                out = out + r2b[j, zi, :, cols].astype(F32)
            sb[zi, :, cols] = out.astype(BF)
        return carry

    lax.fori_loop(0, COLS_G // 128, adds_b, 0)
    three_b = post(sb.at[1 - z], r3b, zp)
    three_a.wait_recv()
    oa[...] = sa[z].astype(F32) + r3a[...].astype(F32)
    three_b.wait_recv()
    ob[...] = sb[z].astype(F32) + r3b[...].astype(F32)
    for copy in copies:
        copy.wait_send()


def grads(da, ca, db, gb, cb):
    return pl.pallas_call(
        grads_kernel,
        out_shape=(
            jax.ShapeDtypeStruct((SHARE, COLS_A), F32),
            jax.ShapeDtypeStruct((SHARE, COLS_G), F32),
        ),
        in_specs=[whole()] * 5,
        out_specs=(whole(), whole()),
        scratch_shapes=[
            VMEM((3,) + da.shape[1:], BF),
            VMEM((3,) + ca.shape, BF),
            VMEM((3,) + db.shape[1:], BF),
            VMEM((3,) + gb.shape[1:], BF),
            VMEM((3,) + cb.shape, BF),
            VMEM((2, 4, SHARE, COLS_A), BF),
            VMEM((2, 4, SHARE, COLS_G), BF),
            VMEM((3, 2, SHARE, COLS_A), BF),
            VMEM((3, 2, SHARE, COLS_G), BF),
            VMEM((2, SHARE, COLS_A), BF),
            VMEM((2, SHARE, COLS_G), BF),
            VMEM((SHARE, COLS_A), BF),
            VMEM((SHARE, COLS_G), BF),
            pltpu.SemaphoreType.DMA((23,)),
            pltpu.SemaphoreType.DMA((23,)),
        ],
        compiler_params=params(3, 62),
    )(da, ca, db, gb, cb)


def rows_for_x(left):
    t = left.T.reshape(2, 4, 4, SHARE, left.shape[0])
    return t.transpose(2, 0, 1, 3, 4).reshape(4, PART, left.shape[0])


def rows_for_y(left):
    t = left.T.reshape(2, 4, 4, SHARE, left.shape[0])
    return t.transpose(1, 0, 2, 3, 4).reshape(4, PART, left.shape[0])


def sliced(codes, bits):
    if bits == 8:
        return codes
    spacing = 2.0 ** (8 - bits)
    upper = 2.0 ** (bits - 1)
    wide = codes.astype(F32)
    return (jnp.clip(jnp.floor(wide / spacing + 0.5), -upper, upper - 1.0) * spacing).astype(BF)


def norm_rows(values, gain):
    return values * lax.rsqrt(jnp.mean(values * values, axis=-1, keepdims=True) + EPS) * gain


def norm_back(values, gain, grad):
    q = lax.rsqrt(jnp.mean(values * values, axis=-1, keepdims=True) + EPS)
    lifted = grad * gain
    back = q * lifted - values * (q * q * q) * jnp.mean(lifted * values, axis=-1, keepdims=True)
    return back, jnp.sum(grad * values * q, axis=(0, 1))


def rotate(values, cosine, sine):
    half = values.shape[-1] // 2
    first = values[..., :half]
    second = values[..., half:]
    return jnp.concatenate(
        [first * cosine - second * sine, second * cosine + first * sine], axis=-1
    )


def gelu_mix(gate, upper):
    return jax.nn.gelu(gate, approximate=True) * upper


def shards(
    inputs,
    out_grad,
    segment_ids,
    keep_mask,
    query_codes,
    key_codes,
    value_codes,
    output_codes,
    gate_codes,
    up_codes,
    down_codes,
    norm_attn_in,
    norm_attn_out,
    norm_ffn_in,
    norm_ffn_out,
):
    rows = inputs.shape[1]
    place = lax.axis_index("blk") * rows + jnp.arange(rows, dtype=jnp.int32)
    freqs = 10000.0 ** (-jnp.arange(HD // 2, dtype=F32) * 2.0 / HD)
    angles = place.astype(F32)[:, None] * freqs[None, :]
    cosine = jnp.cos(angles)
    sine = jnp.sin(angles)
    in_scale = LEVEL_SCALE * D ** (-0.5)
    mid_scale = LEVEL_SCALE * (HEADS * HD) ** (-0.5)
    ff_scale = LEVEL_SCALE * FF ** (-0.5)

    def by_batch(left, codes, scale, back=False):
        parts = []
        for m in range(2):
            weight = sliced(codes, WIDTHS[m])
            parts.append((nt if back else nn)(left[m], weight) * scale)
        return jnp.stack(parts)

    tokens = inputs.astype(F32)
    normed = norm_rows(tokens, norm_attn_in).astype(BF)
    q_raw = by_batch(normed, query_codes, in_scale).reshape(2, rows, 2, HD).transpose(0, 2, 1, 3)
    queries = rotate(q_raw, cosine, sine).astype(BF).reshape(2, 2 * rows, HD)
    key_own = rotate(by_batch(normed, key_codes, in_scale), cosine, sine).astype(BF)
    value_own = by_batch(normed, value_codes, in_scale).astype(BF)
    key_tag = jnp.where(keep_mask == 1, segment_ids, -1).astype(BF).reshape(1, 2 * rows)
    packed = jnp.concatenate(
        [key_own.reshape(2 * rows, HD), jnp.broadcast_to(key_tag, (16, 2 * rows))], axis=0
    )
    keys, values = gather(packed, value_own.reshape(2 * rows, HD))
    keys = keys.reshape(32, 2 * rows + 16, HD)
    values = values.reshape(32, 2 * rows, HD)
    tag = segment_ids.astype(F32)
    tag = jnp.concatenate([tag, tag], axis=1)[:, :, None]
    attended, lse = attend(queries, tag, keys, values)

    def flat(heads):
        return heads.reshape(2, 2, rows, HD).transpose(0, 2, 1, 3).reshape(2, rows, 2 * HD)

    def headed(wide):
        return wide.reshape(2, rows, 2, HD).transpose(0, 2, 1, 3).reshape(2, 2 * rows, HD)

    attended_flat = flat(attended).astype(BF)
    branch = total(by_batch(attended_flat, output_codes, mid_scale).astype(BF), 4).astype(F32)
    middle = tokens + norm_rows(branch, norm_attn_out)
    ffn_in = norm_rows(middle, norm_ffn_in).astype(BF)
    gate = by_batch(ffn_in, gate_codes, in_scale)
    upper = by_batch(ffn_in, up_codes, in_scale)
    hidden = gelu_mix(gate, upper).astype(BF)
    down = total(by_batch(hidden, down_codes, ff_scale).astype(BF), 5).astype(F32)
    out_rows = (middle + norm_rows(down, norm_ffn_out)).astype(BF)

    upstream = out_grad.astype(F32)
    down_grad, gain_ffn_out = norm_back(down, norm_ffn_out, upstream)
    down_low = down_grad.astype(BF)
    hidden_grad = by_batch(down_low, down_codes, ff_scale, True)
    gate_grad, up_grad = jax.vjp(gelu_mix, gate, upper)[1](hidden_grad)
    gate_low = gate_grad.astype(BF)
    up_low = up_grad.astype(BF)
    ffn_in_grad = total(
        (
            by_batch(gate_low, gate_codes, in_scale, True)
            + by_batch(up_low, up_codes, in_scale, True)
        ).astype(BF),
        6,
    ).astype(F32)
    middle_part, gain_ffn_in = norm_back(middle, norm_ffn_in, ffn_in_grad)
    middle_grad = upstream + middle_part
    branch_grad, gain_attn_out = norm_back(branch, norm_attn_out, middle_grad)
    branch_low = branch_grad.astype(BF)
    attended_grad = headed(by_batch(branch_low, output_codes, mid_scale, True).astype(BF))
    offset = jnp.sum(attended_grad.astype(F32) * attended, axis=-1, keepdims=True)
    query_rot, key_part, value_part = attend_back(
        queries, attended_grad, lse, offset, tag, keys, values
    )
    box = (2, 4, 4, 2 * rows, HD)
    key_rot, value_grad = scatter(key_part.reshape(box), value_part.reshape(box))
    key_low = rotate(key_rot.reshape(2, rows, HD), cosine, -sine).astype(BF)
    value_low = value_grad.reshape(2, rows, HD).astype(BF)
    query_low = rotate(query_rot.reshape(2, 2, rows, HD), cosine, -sine)
    query_low = flat(query_low.reshape(2, 2 * rows, HD)).astype(BF)
    normed_grad = total(
        (
            by_batch(query_low, query_codes, in_scale, True)
            + by_batch(key_low, key_codes, in_scale, True)
            + by_batch(value_low, value_codes, in_scale, True)
        ).astype(BF),
        7,
    ).astype(F32)
    token_part, gain_attn_in = norm_back(tokens, norm_attn_in, normed_grad)
    input_grad = (middle_grad + token_part).astype(BF)

    def both(left):
        return left.reshape(2 * rows, left.shape[-1])

    gains = jnp.stack([gain_attn_in, gain_attn_out, gain_ffn_in, gain_ffn_out]).astype(BF)
    gains = jnp.concatenate([gains, jnp.zeros((124, D), BF)])
    da = rows_for_x(both(ffn_in))
    ca = jnp.concatenate([both(gate_low), both(up_low)], axis=1)
    db = jnp.stack([rows_for_y(both(v)) for v in (down_low, normed, branch_low)], axis=1)
    cb = jnp.concatenate(
        [both(hidden), both(query_low), both(key_low), both(value_low), both(attended_flat)], axis=1
    )
    ga, gb = grads(da, ca, db, rows_for_y(gains), cb)
    g_down = gb[:, :2304].T * ff_scale
    g_query = gb[:, 2304:2816] * in_scale
    g_key = gb[:, 2816:3072] * in_scale
    g_value = gb[:, 3072:3328] * in_scale
    g_output = gb[:, 3328:3840].T * mid_scale
    return (
        out_rows,
        input_grad,
        g_query,
        g_key,
        g_value,
        g_output,
        ga[:, :2304] * in_scale,
        ga[:, 2304:] * in_scale,
        g_down,
        gb[:, 3840],
        gb[:, 3841],
        gb[:, 3842],
        gb[:, 3843],
    )


def solution(mesh):
    placed = (
        P(None, "blk", None),
        P(None, "blk", None),
        P(None, "blk"),
        P(None, "blk"),
        P(None, "tensor"),
        P(None, "tensor"),
        P(None, "tensor"),
        P("tensor", None),
        P(None, "tensor"),
        P(None, "tensor"),
        P("tensor", None),
        P(),
        P(),
        P(),
        P(),
    )
    return jax.shard_map(
        shards,
        mesh=mesh,
        in_specs=placed,
        out_specs=(
            P(None, "blk", None),
            P(None, "blk", None),
            P("blk", "tensor"),
            P("blk", "tensor"),
            P("blk", "tensor"),
            P("tensor", "blk"),
            P("blk", "tensor"),
            P("blk", "tensor"),
            P("tensor", "blk"),
            P("blk"),
            P("blk"),
            P("blk"),
            P("blk"),
        ),
        check_vma=False,
    )
```

time: 1930 us -> 658 us (0.34)
  waiting for transfers between devices: 1490 us -> 0 us
  Pallas kernels: 0 us -> 466 us
  matrix products: 231 us -> 95.1 us
  local copies, waits for them, and re-layouts: 118 us -> 50.3 us
  other arithmetic: 65.7 us -> 43.9 us
    unnamed x10 -> x0, waiting for transfers between devices: 832 us -> none
    pallas_call x0 -> x9, Pallas kernels: none -> 466 us  [the longest x1 223 us: grads(): pl.pallas_call(grads_kernel, out_shape=(jax.ShapeDtypeStruct((SHARE, COLS...]
    all_gather x2 -> x0, waiting for transfers between devices: 292 us -> none  [shards(): piece = lax.all_gather(packed_kv, 'blk', axis=0, tiled=True)]
    psum x4 -> x0, waiting for transfers between devices: 199 us -> none  [the longest x1 66.4 us: shards(): lax.psum(product(attended_flat, w_output).astype(jnp.bfloat16), 'tensor')]
    reduce_scatter x2 -> x0, waiting for transfers between devices: 166 us -> none  [shards(): lax.psum_scatter(jnp.concatenate([key_part, value_part], axis=1).astype(j...]
    dot_general x54 -> x28, matrix products: 231 us -> 95.1 us  [the longest x14 54 us: nt(): lax.dot_general(left, right, (((1,), (1,)), ((), ())), preferred_element_...]
    reshape x9 -> x4, local copies, waits for them, and re-layouts: 42.7 us -> 7.66 us  [both(): return left.reshape(2 * rows, left.shape[-1])]
    unnamed x325 -> x204, local copies, waits for them, and re-layouts: 46.9 us -> 19.8 us
  transfers between devices with their start and end apart: 9 -> 0, of which waited for: 9 -> 0; matrix products, arithmetic and copies ran while one was open for 10% -> 0% of each run, Pallas kernels for 0% -> 0%
where the time goes in v1:
time: 658 us; the launch traced here: 657 us
  Pallas kernels  466 us (71%)
  matrix products  95.1 us (14%)
  local copies, waits for them, and re-layouts  50.3 us (8%)
  other arithmetic  43.9 us (7%)
    pallas_call x1, Pallas kernels, grads(): pl.pallas_call(grads_kernel, out_shape=(jax.ShapeDtypeStruct((SHARE, COLS...  223 us
    pallas_call x1, Pallas kernels, scatter(): pl.pallas_call(scatter_kernel, out_shape=(jax.ShapeDtypeStruct(ta, F32),...  84.8 us
    pallas_call x4, Pallas kernels, total(): pl.pallas_call(total_kernel, out_shape=jax.ShapeDtypeStruct(p.shape, BF),...  83.4 us
    pallas_call x1, Pallas kernels, gather(): pl.pallas_call(gather_kernel, out_shape=(jax.ShapeDtypeStruct((2, 4, 4) +...  67.7 us
    dot_general x14, matrix products, nt(): lax.dot_general(left, right, (((1,), (1,)), ((), ())), preferred_element_...  54 us
    dot_general x14, matrix products, nn(): return jnp.dot(left, right, preferred_element_type=F32)  41 us
    unnamed x204, local copies, waits for them, and re-layouts  19.8 us

profile of v1, /device:TPU:1, one launch (start us, length us, event | category | flops | bytes accessed | tf_op | source)
XLA Modules:
  0.0 657.1 jit_solution(2674254830699899819)
XLA Ops:
  0.7 1.7 fusion.79
  4.8 1.2 fusion.81
  8.6 1.2 copy-done.27
  9.8 1.3 convolution_multiply_fusion.16
  11.3 2.1 convolution_multiply_fusion.17
  14.3 1.2 maximum_bitcast_fusion
  15.9 1.4 copy.68
  17.4 2.4 copy.69
  19.7 67.7 %shard_map.246 = (bf16[2,4,4,272,256]{4,3,2,1,0:T(8,128)(2,1)S(1)}, bf16[2,4,4,256,256]{4,3,2,1,0:T(8,128)(2,1)S(1)}) custom-call(bf16[272,256]{1,0:T(8,128)(2,1)S(1)} %pad_maximum_fusion.9.a_ref, bf16[256,256]{1,0:T(8,128)(2,1)S(1)} %bitcast.246), custom_call_target="tpu_custom_call" | custom-call | tf_op jit(solution)/shard_map/pallas_call | solution.py:114
  87.5 1.5 shard_map.247
  89.6 1.3 copy-done.3
  92.9 1.3 fusion.32
  94.9 21.9 %shard_map.248 = bf16[2,128,2304]{2,1,0:T(8,128)(2,1)S(1)} custom-call(bf16[2,128,2304]{2,1,0:T(8,128)(2,1)S(1)} %pad_maximum_fusion.5.p_ref), custom_call_target="tpu_custom_call" | custom-call | tf_op jit(solution)/shard_map/pallas_call | solution.py:249
  119.8 5.4 fusion.15
  125.3 1.6 fusion.24
  126.9 17.9 %fusion.13 = f32[1,128,2304]{2,1,0:T(8,128)S(1)} fusion(bf16[2304,2304]{1,0:T(8,128)(2,1)S(1)} %bitcast.255, bf16[2,128,2304]{2,1,0:T(8,128)(2,1)S(1)} %multiply_convert_fusion.39), kind=kOutput, calls=%fused_computation.48 | convolution fusion | flops 1396408320 | bytes 12386304 | tf_op jit(solution)/shard_map/dot_general | solution.py:278
  144.8 1.6 fusion.23
  146.5 1.0 copy-done.23
  148.3 5.7 fusion.35
  154.0 1.6 fusion.34
  155.7 19.8 %shard_map.249 = bf16[2,128,2304]{2,1,0:T(8,128)(2,1)S(1)} custom-call(bf16[2,128,2304]{2,1,0:T(8,128)(2,1)S(1)} %pad_maximum_fusion.6.p_ref), custom_call_target="tpu_custom_call" | custom-call | tf_op jit(solution)/shard_map/pallas_call | solution.py:249
  177.2 1.6 fusion.41
  178.9 2.4 copy.66
  181.3 2.5 copy.67
  183.8 9.0 %fusion.16 = f32[1,128,2304]{2,1,0:T(8,128)} fusion(bf16[2304,2304]{1,0:T(8,128)(2,1)} %param.25, bf16[2,128,2304]{2,1,0:T(8,128)(2,1)S(1)} %copy-done.29), kind=kOutput, calls=%fused_computation.51 | convolution fusion | flops 1396408320 | bytes 12386304 | tf_op jit(solution)/shard_map/dot_general | solution.py:270
  192.8 8.5 %fusion.25 = f32[1,128,2304]{2,1,0:T(8,128)} fusion(bf16[2304,2304]{1,0:T(8,128)(2,1)} %param.25, bf16[2,128,2304]{2,1,0:T(8,128)(2,1)S(1)} %copy-done.29), kind=kOutput, calls=%fused_computation.60 | convolution fusion | flops 1359249408 | bytes 12386304 | tf_op jit(solution)/shard_map/dot_general | solution.py:270
  201.3 1.4 copy.64
  202.7 2.6 copy.65
  205.4 3.6 multiply_convert_fusion.37
  209.0 3.7 fusion.62
  212.7 1.5 pad_maximum_fusion.4.ca
  214.2 5.4 fusion.14
  219.7 4.8 fusion.27
  224.4 8.5 %fusion.12 = f32[1,128,2304]{2,1,0:T(8,128)S(1)} fusion(bf16[2304,2304]{1,0:T(8,128)(2,1)} %param.23, bf16[2,128,2304]{2,1,0:T(8,128)(2,1)S(1)} %get-tuple-element.52), kind=kOutput, calls=%fused_computation.47 | convolution fusion | flops 1396408320 | bytes 12386304 | tf_op jit(solution)/shard_map/dot_general | solution.py:270
  233.0 3.5 fusion.26
  236.8 19.8 %shard_map.250 = bf16[2,128,2304]{2,1,0:T(8,128)(2,1)S(1)} custom-call(bf16[2,128,2304]{2,1,0:T(8,128)(2,1)S(1)} %fusion.86.p_ref), custom_call_target="tpu_custom_call" | custom-call | tf_op jit(solution)/shard_map/pallas_call | solution.py:249
  258.0 2.4 fusion.70
  261.6 1.7 fusion.67
  263.3 1.0 copy-done.30
  264.3 2.0 fusion.98
  266.3 1.6 stack.195
  267.9 1.6 copy.59
  269.5 3.4 fusion.97
  272.9 1.6 stack.194
  276.3 1.8 multiply_reduce_fusion.1
  278.8 1.5 copy.60.off_ref
  280.3 2.2 copy-done.4
  282.5 0.9 copy-done.6
  287.3 4.7 shard_map.251
  292.0 84.8 %shard_map.252 = (f32[256,256]{1,0:T(8,128)S(1)}, f32[256,256]{1,0:T(8,128)S(1)}) custom-call(bf16[2,4,4,256,256]{4,3,2,1,0:T(8,128)(2,1)S(1)} %bitcast.242, bf16[2,4,4,256,256]{4,3,2,1,0:T(8,128)(2,1)S(1)} %bitcast.243), custom_call_target="tpu_custom_call" | custom-call | tf_op jit(solution)/shard_map/pallas_call | solution.py:193
  378.9 2.3 fusion.18
  381.3 2.0 fusion.17
  383.3 1.8 fusion.20
  385.0 1.6 fusion.19
  386.6 2.4 copy.70
  389.0 1.5 copy.71
  391.0 2.0 pad_maximum_fusion.db
  398.1 21.9 %shard_map.253 = bf16[2,128,2304]{2,1,0:T(8,128)(2,1)S(1)} custom-call(bf16[2,128,2304]{2,1,0:T(8,128)(2,1)S(1)} %fusion.88.p_ref), custom_call_target="tpu_custom_call" | custom-call | tf_op jit(solution)/shard_map/pallas_call | solution.py:249
  420.9 3.4 fusion.44
  425.6 223.4 %shard_map.254 = (f32[72,4608]{1,0:T(8,128)}, f32[72,3968]{1,0:T(8,128)}) custom-call(bf16[4,576,256]{2,1,0:T(8,128)(2,1)} %bitcast.262, bf16[256,4608]{1,0:T(8,128)(2,1)} %pad_maximum_fusion.4.ca, bf16[4,3,576,256]{3,2,1,0:T(8,128)(2,1)} %pad_maximum_fusion.db, bf16[4,576,128]{2,1,0:T(8,128)(2,1)} %bitcast.270, bf16[256,3840]{1,0:T(8,128)(2,1)} %copy-done.31), custom_call_target="tpu_custom_call" | custom-call | tf_op jit(solution)/shard_map/pallas_call | solution.py:487
  649.0 1.7 slice_reduce_fusion
  650.7 1.6 slice_multiply_fusion.3
  652.3 1.7 multiply_bitcast_fusion.1
  654.1 2.8 slice_multiply_fusion
  (266 shorter events, 33.8 us)
Async XLA Ops:
  0.6 4.2 copy-start.17
  2.9 4.0 copy-start.72
  4.6 10.9 %copy-start.45 = (f32[128,128]{1,0:T(8,128)}, f32[128,128]{1,0:T(8,128)S(1)}, u32[]{:S(2)}) copy-start(f32[128,128]{1,0:T(8,128)S(1)} %get-tuple-element.84) | copy-start | bytes 196612
  4.8 82.7 %copy-start.5 = (f32[2,256,1]{2,1,0:T(8,128)}, f32[2,256,1]{2,1,0:T(8,128)S(1)}, u32[]{:S(2)}) copy-start(f32[2,256,1]{2,1,0:T(8,128)S(1)} %copy.56.t_ref) | copy-start | bytes 6148
  15.9 71.6 %copy-start.7 = (bf16[2,256,256]{2,1,0:T(8,128)(2,1)}, bf16[2,256,256]{2,1,0:T(8,128)(2,1)S(1)}, u32[]{:S(2)}) copy-start(bf16[2,256,256]{2,1,0:T(8,128)(2,1)S(1)} %pad_maximum_fusion.7.q_ref) | copy-start | bytes 786436
  87.5 3.4 copy-start.3
  90.9 3.4 copy-start.11
  90.9 3.4 copy-start.13
  92.9 26.9 %slice-start.3 = ((s8[10616832]{0:T(1024)(128)(4,1)}), s8[4194304]{0:T(1024)(128)(4,1)S(1)}, s32[]{:S(2)}) async-start(s8[10616832]{0:T(1024)(128)(4,1)} %bitcast.250), calls=%async_computation.3 | async-start | bytes 8388608
  92.9 26.9 %slice-start.4 = ((s8[10616832]{0:T(1024)(128)(4,1)}), s8[2228224]{0:T(1024)(128)(4,1)S(1)}, s32[]{:S(2)}) async-start(s8[10616832]{0:T(1024)(128)(4,1)} %bitcast.250), calls=%async_computation.4 | async-start | bytes 4456448
  94.8 23.0 %copy-start.56 = (f32[2304]{0:T(1024)S(1)}, f32[2304]{0:T(1024)}, u32[]{:S(2)}) copy-start(f32[2304]{0:T(1024)} %param.27) | copy-start | bytes 27652
  94.9 24.9 %slice-start.5 = ((s8[10616832]{0:T(1024)(128)(4,1)}), s8[4194304]{0:T(1024)(128)(4,1)S(1)}, s32[]{:S(2)}) async-start(s8[10616832]{0:T(1024)(128)(4,1)} %bitcast.250), calls=%async_computation.5 | async-start | bytes 8388608
  116.9 2.9 copy-start
  116.9 2.2 copy-start.58
  119.1 6.2 copy-start.69
  119.1 7.8 %slice-start.9 = ((s8[10616832]{0:T(1024)(128)(4,1)}), s8[4194304]{0:T(1024)(128)(4,1)S(1)}, s32[]{:S(2)}) async-start(s8[10616832]{0:T(1024)(128)(4,1)} %bitcast.254), calls=%async_computation.9 | async-start | bytes 8388608
  119.8 7.0 %slice-start.10 = ((s8[10616832]{0:T(1024)(128)(4,1)}), s8[4194304]{0:T(1024)(128)(4,1)S(1)}, s32[]{:S(2)}) async-start(s8[10616832]{0:T(1024)(128)(4,1)} %bitcast.254), calls=%async_computation.10 | async-start | bytes 8388608
  119.8 7.0 %slice-start.11 = ((s8[10616832]{0:T(1024)(128)(4,1)}), s8[2228224]{0:T(1024)(128)(4,1)S(1)}, s32[]{:S(2)}) async-start(s8[10616832]{0:T(1024)(128)(4,1)} %bitcast.254), calls=%async_computation.11 | async-start | bytes 4456448
  125.2 21.2 %copy-start.33 = (f32[1,128,2304]{2,1,0:T(8,128)}, f32[1,128,2304]{2,1,0:T(8,128)S(1)}, u32[]{:S(2)}) copy-start(f32[1,128,2304]{2,1,0:T(8,128)S(1)} %fusion.15) | copy-start | bytes 3538948
  125.2 23.0 %slice-start = ((s8[10616832]{0:T(1024)(128)(4,1)}), s8[4194304]{0:T(1024)(128)(4,1)S(1)}, s32[]{:S(2)}) async-start(s8[10616832]{0:T(1024)(128)(4,1)} %bitcast.248), calls=%async_computation | async-start | bytes 8388608
  126.9 21.4 %slice-start.1 = ((s8[10616832]{0:T(1024)(128)(4,1)}), s8[4194304]{0:T(1024)(128)(4,1)S(1)}, s32[]{:S(2)}) async-start(s8[10616832]{0:T(1024)(128)(4,1)} %bitcast.248), calls=%async_computation.1 | async-start | bytes 8388608
  126.9 21.4 %slice-start.2 = ((s8[10616832]{0:T(1024)(128)(4,1)}), s8[2228224]{0:T(1024)(128)(4,1)S(1)}, s32[]{:S(2)}) async-start(s8[10616832]{0:T(1024)(128)(4,1)} %bitcast.248), calls=%async_computation.2 | async-start | bytes 4456448
  155.7 20.2 %copy-start.20 = (bf16[2,128,2304]{2,1,0:T(8,128)(2,1)S(1)}, bf16[2,128,2304]{2,1,0:T(8,128)(2,1)}, u32[]{:S(2)}) copy-start(bf16[2,128,2304]{2,1,0:T(8,128)(2,1)} %param.16) | copy-start | bytes 3538948
  155.7 20.2 %copy-start.62 = (f32[2304]{0:T(1024)S(1)}, f32[2304]{0:T(1024)}, u32[]{:S(2)}) copy-start(f32[2304]{0:T(1024)} %param.29) | copy-start | bytes 27652
  175.9 3.0 copy-start.74
  181.3 2.5 copy-start.29
  202.7 2.6 copy-start.24
  202.7 2.6 copy-start.32
  205.3 8.8 %slice-start.6 = ((s8[10616832]{0:T(1024)(128)(4,1)}), s8[4194304]{0:T(1024)(128)(4,1)S(1)}, s32[]{:S(2)}) async-start(s8[10616832]{0:T(1024)(128)(4,1)} %bitcast.252), calls=%async_computation.6 | async-start | bytes 8388608
  205.3 8.8 %slice-start.7 = ((s8[10616832]{0:T(1024)(128)(4,1)}), s8[4194304]{0:T(1024)(128)(4,1)S(1)}, s32[]{:S(2)}) async-start(s8[10616832]{0:T(1024)(128)(4,1)} %bitcast.252), calls=%async_computation.7 | async-start | bytes 8388608
  209.0 5.2 copy-start.44
  209.0 5.2 slice-start.8
  219.7 13.3 %slice-start.12 = ((s8[10616832]{0:T(1024)(128)(4,1)}), s8[2228224]{0:T(1024)(128)(4,1)S(1)}, s32[]{:S(2)}) async-start(s8[10616832]{0:T(1024)(128)(4,1)} %bitcast.256), calls=%async_computation.12 | async-start | bytes 4456448
  224.4 8.5 %slice-start.13 = ((s8[10616832]{0:T(1024)(128)(4,1)}), s8[4194304]{0:T(1024)(128)(4,1)S(1)}, s32[]{:S(2)}) async-start(s8[10616832]{0:T(1024)(128)(4,1)} %bitcast.256), calls=%async_computation.13 | async-start | bytes 8388608
  224.4 8.5 %slice-start.14 = ((s8[10616832]{0:T(1024)(128)(4,1)}), s8[4194304]{0:T(1024)(128)(4,1)S(1)}, s32[]{:S(2)}) async-start(s8[10616832]{0:T(1024)(128)(4,1)} %bitcast.256), calls=%async_computation.14 | async-start | bytes 8388608
  236.5 20.2 %copy-start.57 = (f32[2304]{0:T(1024)S(1)}, f32[2304]{0:T(1024)}, u32[]{:S(2)}) copy-start(f32[2304]{0:T(1024)} %param.27) | copy-start | bytes 27652
  236.5 20.2 %copy-start.59 = (f32[2304]{0:T(1024)S(1)}, f32[2304]{0:T(1024)}, u32[]{:S(2)}) copy-start(f32[2304]{0:T(1024)} %param.28) | copy-start | bytes 27652
  236.5 20.2 %copy-start.65 = (f32[2,128]{1,0:T(2,128)S(1)}, f32[2,128]{1,0:T(2,128)}, u32[]{:S(2)}) copy-start(f32[2,128]{1,0:T(2,128)} %copy-done.64) | copy-start | bytes 3076
  236.8 19.9 %copy-start.1 = (bf16[2,128,2304]{2,1,0:T(8,128)(2,1)S(1)}, bf16[2,128,2304]{2,1,0:T(8,128)(2,1)}, u32[]{:S(2)}) copy-start(bf16[2,128,2304]{2,1,0:T(8,128)(2,1)} %copy-done) | copy-start | bytes 3538948
  236.8 19.9 %copy-start.18 = (bf16[2,128,2304]{2,1,0:T(8,128)(2,1)S(1)}, bf16[2,128,2304]{2,1,0:T(8,128)(2,1)}, u32[]{:S(2)}) copy-start(bf16[2,128,2304]{2,1,0:T(8,128)(2,1)} %param.15) | copy-start | bytes 3538948
  258.0 3.6 copy-start.78
  258.0 3.6 copy-start.80
  261.6 2.7 copy-start.26
  292.0 84.8 %copy-start.46 = (f32[128,128]{1,0:T(8,128)S(1)}, f32[128,128]{1,0:T(8,128)}, u32[]{:S(2)}) copy-start(f32[128,128]{1,0:T(8,128)} %copy-done.45) | copy-start | bytes 196612
  292.0 84.8 %copy-start.51 = (f32[128,128]{1,0:T(8,128)S(1)}, f32[128,128]{1,0:T(8,128)}, u32[]{:S(2)}) copy-start(f32[128,128]{1,0:T(8,128)} %get-tuple-element.82) | copy-start | bytes 196612
  376.8 8.2 %copy-start.52 = (bf16[2,128,128]{2,1,0:T(8,128)(2,1)}, bf16[2,128,128]{2,1,0:T(8,128)(2,1)S(1)}, u32[]{:S(2)}) copy-start(bf16[2,128,128]{2,1,0:T(8,128)(2,1)S(1)} %get-tuple-element.71) | copy-start | bytes 196612
  376.9 8.2 %copy-start.54 = (bf16[2,128,128]{2,1,0:T(8,128)(2,1)}, bf16[2,128,128]{2,1,0:T(8,128)(2,1)S(1)}, u32[]{:S(2)}) copy-start(bf16[2,128,128]{2,1,0:T(8,128)(2,1)S(1)} %get-tuple-element.70) | copy-start | bytes 196612
  394.6 2.3 copy-start.43
  394.6 2.7 copy-start.47
  394.6 3.0 copy-start.48
  397.6 22.4 %copy-start.61 = (f32[2304]{0:T(1024)S(1)}, f32[2304]{0:T(1024)}, u32[]{:S(2)}) copy-start(f32[2304]{0:T(1024)} %param.26) | copy-start | bytes 27652
  397.6 22.4 %copy-start.73 = (f32[2,128]{1,0:T(2,128)S(1)}, f32[2,128]{1,0:T(2,128)}, u32[]{:S(2)}) copy-start(f32[2,128]{1,0:T(2,128)} %copy-done.72) | copy-start | bytes 3076
  398.0 22.0 %copy-start.19 = (bf16[2,128,2304]{2,1,0:T(8,128)(2,1)S(1)}, bf16[2,128,2304]{2,1,0:T(8,128)(2,1)}, u32[]{:S(2)}) copy-start(bf16[2,128,2304]{2,1,0:T(8,128)(2,1)} %param.15) | copy-start | bytes 3538948
  398.0 22.7 %copy-start.22 = (bf16[2,128,2304]{2,1,0:T(8,128)(2,1)S(1)}, bf16[2,128,2304]{2,1,0:T(8,128)(2,1)}, u32[]{:S(2)}) copy-start(bf16[2,128,2304]{2,1,0:T(8,128)(2,1)} %param.16) | copy-start | bytes 3538948
  398.0 22.7 %copy-start.60 = (f32[2304]{0:T(1024)S(1)}, f32[2304]{0:T(1024)}, u32[]{:S(2)}) copy-start(f32[2304]{0:T(1024)} %param.28) | copy-start | bytes 27652
  398.1 22.7 %copy-start.63 = (f32[2304]{0:T(1024)S(1)}, f32[2304]{0:T(1024)}, u32[]{:S(2)}) copy-start(f32[2304]{0:T(1024)} %param.29) | copy-start | bytes 27652
  398.1 22.7 %copy-start.71 = (f32[2,128]{1,0:T(2,128)S(1)}, f32[2,128]{1,0:T(2,128)}, u32[]{:S(2)}) copy-start(f32[2,128]{1,0:T(2,128)} %copy-done.69) | copy-start | bytes 3076
  398.1 22.7 %copy-start.75 = (f32[2,128]{1,0:T(2,128)S(1)}, f32[2,128]{1,0:T(2,128)}, u32[]{:S(2)}) copy-start(f32[2,128]{1,0:T(2,128)} %copy-done.74) | copy-start | bytes 3076
  398.1 22.7 %copy-start.77 = (f32[2,128]{1,0:T(2,128)S(1)}, f32[2,128]{1,0:T(2,128)}, u32[]{:S(2)}) copy-start(f32[2,128]{1,0:T(2,128)} %get-tuple-element.87) | copy-start | bytes 3076
  398.1 22.7 %copy-start.79 = (f32[2,128]{1,0:T(2,128)S(1)}, f32[2,128]{1,0:T(2,128)}, u32[]{:S(2)}) copy-start(f32[2,128]{1,0:T(2,128)} %copy-done.78) | copy-start | bytes 3076
  398.1 22.7 %copy-start.81 = (f32[2,128]{1,0:T(2,128)S(1)}, f32[2,128]{1,0:T(2,128)}, u32[]{:S(2)}) copy-start(f32[2,128]{1,0:T(2,128)} %get-tuple-element.80) | copy-start | bytes 3076
  420.8 3.5 copy-start.66
  420.8 3.5 copy-start.67
  420.8 3.5 copy-start.68
  (33 other events, 47.3 us)

commit v2 on v1

v2 whole, which is shorter than its diff:
```python
import functools

import jax
import jax.numpy as jnp
from jax import lax
from jax.experimental import pallas as pl
from jax.experimental.pallas import tpu as pltpu
from jax.sharding import PartitionSpec as P

D = 2304
HEADS = 8
HD = 256
FF = 9216

CAP = 50.0
EPS = 1e-06
LEVEL_SCALE = 1.0 / 74.0
WIDTHS = (8, 4, 2)

MESH = pl.DeviceIdType.MESH
VMEM = pltpu.VMEM
BF = jnp.bfloat16
F32 = jnp.float32
SEQ = 4096
ROWS = 128
TAGROW = 256
MASKED = -2.0


def place_of():
    b = lax.axis_index("blk")
    t = lax.axis_index("tensor")
    return b % 4, (b // 4) % 4, b // 16, t // 2, t % 2


def device_at(x, y, z, zh, c):
    return ((z * 4 + y) * 4 + x, zh * 2 + c)


def greet(peers):
    barrier = pltpu.get_barrier_semaphore()
    for peer in peers:
        pl.semaphore_signal(barrier, inc=1, device_id=peer, device_id_type=MESH)
    pl.semaphore_wait(barrier, len(peers))


def send(src, dst, ssem, rsem, peer):
    copy = pltpu.make_async_remote_copy(
        src_ref=src, dst_ref=dst, send_sem=ssem, recv_sem=rsem, device_id=peer, device_id_type=MESH
    )
    copy.start()
    return copy


def params(collective_id=None, limit=60):
    if collective_id is None:
        return pltpu.CompilerParams(vmem_limit_bytes=limit << 20)
    return pltpu.CompilerParams(
        vmem_limit_bytes=limit << 20, collective_id=collective_id, has_side_effects=True
    )


def whole(space=VMEM):
    return pl.BlockSpec(memory_space=space)


def gather_kernel(a_ref, b_ref, oa, ob, lsem, ssem, rsem):
    x, y, z, zh, c = place_of()
    xs = [device_at((x + j) % 4, y, z, zh, c) for j in (1, 2, 3)]
    ys = [device_at(x, (y + j) % 4, z, zh, c) for j in (1, 2, 3)]
    zp = device_at(x, y, 1 - z, zh, c)
    greet(xs + ys + [zp])
    mine_a = pltpu.make_async_copy(a_ref, oa.at[z, y, x], lsem.at[0])
    mine_b = pltpu.make_async_copy(b_ref, ob.at[z, y, x], lsem.at[1])
    mine_a.start()
    mine_b.start()
    za = send(a_ref, oa.at[z, y, x], ssem.at[0], rsem.at[0], zp)
    zb = send(b_ref, ob.at[z, y, x], ssem.at[1], rsem.at[1], zp)
    done = [za, zb]
    first_a = [send(a_ref, oa.at[z, y, x], ssem.at[2 + j], rsem.at[2 + j], xs[j]) for j in range(3)]
    first_b = [send(b_ref, ob.at[z, y, x], ssem.at[5 + j], rsem.at[5 + j], ys[j]) for j in range(3)]
    za.wait_recv()
    other = 1 - z
    next_a = [
        send(oa.at[other, y, x], oa.at[other, y, x], ssem.at[8 + j], rsem.at[8 + j], xs[j])
        for j in range(3)
    ]
    zb.wait_recv()
    next_b = [
        send(ob.at[other, y, x], ob.at[other, y, x], ssem.at[11 + j], rsem.at[11 + j], ys[j])
        for j in range(3)
    ]
    mine_a.wait()
    mine_b.wait()
    last = []
    for step, (level, copies_a, copies_b) in enumerate(((z, first_a, first_b), (other, next_a, next_b))):
        for copy in copies_a:
            copy.wait_recv()
        for j in range(3):
            k = 14 + 6 * step + j
            last.append(send(oa.at[level, y], oa.at[level, y], ssem.at[k], rsem.at[k], ys[j]))
        for copy in copies_b:
            copy.wait_recv()
        for j in range(3):
            k = 17 + 6 * step + j
            last.append(send(ob.at[level, :, x], ob.at[level, :, x], ssem.at[k], rsem.at[k], xs[j]))
    for copy in last:
        copy.wait_recv()
    for copy in done + first_a + first_b + next_a + next_b + last:
        copy.wait_send()


def gather(a, b):
    return pl.pallas_call(
        gather_kernel,
        out_shape=(
            jax.ShapeDtypeStruct((2, 4, 4) + a.shape, a.dtype),
            jax.ShapeDtypeStruct((2, 4, 4) + b.shape, b.dtype),
        ),
        in_specs=[whole(), whole()],
        out_specs=(whole(), whole()),
        scratch_shapes=[
            pltpu.SemaphoreType.DMA((2,)),
            pltpu.SemaphoreType.DMA((26,)),
            pltpu.SemaphoreType.DMA((26,)),
        ],
        compiler_params=params(1, 30),
    )(a, b)


PIECES = 4


def total_kernel(kinds, *refs):
    n = len(kinds)
    p_ref, extras = refs[0], refs[1 : 1 + n]
    o_ref, lands = refs[1 + n], refs[2 + n : 2 + 2 * n]
    r1, h, r2, lsem, ssem, rsem = refs[2 + 2 * n :]
    x, y, z, zh, c = place_of()
    peers = {
        "x": [((x + j) % 4, device_at((x + j) % 4, y, z, zh, c)) for j in (1, 2, 3)],
        "y": [((y + j) % 4, device_at(x, (y + j) % 4, z, zh, c)) for j in (1, 2, 3)],
    }
    mine = {"x": x, "y": y}
    mate = device_at(x, y, z, zh, 1 - c)
    far = device_at(x, y, z, 1 - zh, c)
    axes = sorted({axis for _, axis in kinds})
    greet([mate, far] + [device for axis in axes for _, device in peers[axis]])
    size = p_ref.shape[1] // PIECES
    rows = [pl.ds(k * size, size) for k in range(PIECES)]
    one = [
        send(p_ref.at[1 - c, rows[k]], r1.at[rows[k]], ssem.at[k], rsem.at[k], mate)
        for k in range(PIECES)
    ]
    carried, kept = [], []
    for e, (kind, axis) in enumerate(kinds):
        band = pl.ds(pl.multiple_of(mine[axis] * 256, 256), 256)
        land = lands[e].at[:, band] if kind == "swap" else lands[e].at[band]
        for j, (place, device) in enumerate(peers[axis]):
            i = 3 * PIECES + 3 * e + j
            src = extras[e].at[place] if kind == "swap" else extras[e]
            carried.append(send(src, land, ssem.at[i], rsem.at[i], device))
        own = extras[e].at[mine[axis]] if kind == "swap" else extras[e]
        copy = pltpu.make_async_copy(own, land, lsem.at[e])
        copy.start()
        kept.append(copy)
    two, three = [], []
    for k in range(PIECES):
        one[k].wait_recv()
        h[rows[k]] = (p_ref[c, rows[k]].astype(F32) + r1[rows[k]].astype(F32)).astype(BF)
        i = PIECES + k
        two.append(send(h.at[rows[k]], r2.at[rows[k]], ssem.at[i], rsem.at[i], far))
    for k in range(PIECES):
        two[k].wait_recv()
        o_ref[c, rows[k]] = (h[rows[k]].astype(F32) + r2[rows[k]].astype(F32)).astype(BF)
        i = 2 * PIECES + k
        three.append(send(o_ref.at[c, rows[k]], o_ref.at[c, rows[k]], ssem.at[i], rsem.at[i], mate))
    for copy in three + carried:
        copy.wait_recv()
    for copy in one + two + three + carried:
        copy.wait_send()
    for copy in kept:
        copy.wait()


def total(p, collective_id, carry=()):
    half = p.shape[1:]
    kinds = tuple((kind, axis) for kind, axis, _ in carry)
    extras = [array for _, _, array in carry]
    lands = [
        jax.ShapeDtypeStruct((PART, 1024) if kind == "swap" else (1024, array.shape[1]), BF)
        for kind, _, array in carry
    ]
    sems = 3 * PIECES + 3 * len(carry)
    out = pl.pallas_call(
        functools.partial(total_kernel, kinds),
        out_shape=[jax.ShapeDtypeStruct(p.shape, BF)] + lands,
        in_specs=[whole()] + [whole(pl.ANY)] * len(carry),
        out_specs=[whole()] + [whole(pl.ANY)] * len(carry),
        scratch_shapes=[
            VMEM(half, BF),
            VMEM(half, BF),
            VMEM(half, BF),
            pltpu.SemaphoreType.DMA((max(1, len(carry)),)),
            pltpu.SemaphoreType.DMA((sems,)),
            pltpu.SemaphoreType.DMA((sems,)),
        ],
        compiler_params=params(collective_id, 30),
        cost_estimate=pl.CostEstimate(flops=1000, bytes_accessed=1000, transcendentals=0),
    )(p, *extras)
    return out[0], out[1:]


CHUNK = 4
KEYS = CHUNK * ROWS


def nt(left, right):
    return lax.dot_general(left, right, (((1,), (1,)), ((), ())), preferred_element_type=F32)


def tn(left, right):
    return lax.dot_general(left, right, (((0,), (0,)), ((), ())), preferred_element_type=F32)


def nn(left, right):
    return jnp.dot(left, right, preferred_element_type=F32)


def load_chunk(k_ref, v_ref, step, m):
    blocks = pl.ds(step * CHUNK, CHUNK)
    keys = k_ref[blocks, m * ROWS : (m + 1) * ROWS, :].reshape(KEYS, HD)
    values = v_ref[blocks, m * ROWS : (m + 1) * ROWS, :].reshape(KEYS, HD)
    tags = k_ref[blocks, TAGROW : TAGROW + 16, m * ROWS : (m + 1) * ROWS].astype(F32)
    tag_row = jnp.concatenate([tags[i, 0:1, :] for i in range(CHUNK)], axis=1)
    return keys, values, tag_row


def allowed(step, tag_row, query_tag, query_place):
    key_place = step * KEYS + lax.broadcasted_iota(jnp.int32, (2 * ROWS, KEYS), 1)
    ok = (key_place <= query_place) & (tag_row == query_tag)
    return ok | (key_place == query_place)


def query_places():
    row = lax.broadcasted_iota(jnp.int32, (2 * ROWS, 1), 0)
    return lax.axis_index("blk") * ROWS + row % ROWS


def attend_kernel(q_ref, t_ref, k_ref, v_ref, o_ref, lse_ref):
    limit = lax.axis_index("blk") // CHUNK + 1
    where = query_places()
    for m in range(2):
        q = q_ref[m]
        tag = t_ref[m]

        def step(i, carry):
            acc, mass = carry
            keys, values, tag_row = load_chunk(k_ref, v_ref, i, m)
            bent = jnp.tanh(nt(q, keys) * (HD ** (-0.5) / CAP))
            e = jnp.where(allowed(i, tag_row, tag, where), jnp.exp(CAP * bent), 0.0)
            mass = mass + jnp.sum(e, axis=-1, keepdims=True)
            return acc + nn(e.astype(BF), values), mass

        acc, mass = lax.fori_loop(
            0, limit, step, (jnp.zeros((2 * ROWS, HD), F32), jnp.zeros((2 * ROWS, 1), F32))
        )
        o_ref[m] = acc / mass
        lse_ref[m] = jnp.log(mass)


def attend(q, tag, k, v):
    return pl.pallas_call(
        attend_kernel,
        out_shape=(
            jax.ShapeDtypeStruct((2, 2 * ROWS, HD), F32),
            jax.ShapeDtypeStruct((2, 2 * ROWS, 1), F32),
        ),
        in_specs=[whole()] * 4,
        out_specs=(whole(), whole()),
        compiler_params=params(None, 40),
    )(q, tag, k, v)


FTILE = 256
ROOT = (2.0 / 3.141592653589793) ** 0.5
CUBE = 0.044715


def narrow(codes):
    level = codes * BF(1.0 / 16.0) + BF(1.0 / 32.0)
    level = (level + BF(192.0)) - BF(192.0)
    return jnp.minimum(level, BF(7.0)) * BF(16.0)


def ffn_kernel(x_ref, wg_ref, wu_ref, wd_ref, gate_ref, up_ref, hid_ref, down_ref, acc, scale_in, scale_out):
    i = pl.program_id(0)

    @pl.when(i == 0)
    def _():
        acc[...] = jnp.zeros_like(acc)

    for m in range(2):
        wg, wu, wd = wg_ref[...], wu_ref[...], wd_ref[...]
        if m == 1:
            wg, wu, wd = narrow(wg), narrow(wu), narrow(wd)
        gate = nn(x_ref[m], wg) * scale_in
        up = nn(x_ref[m], wu) * scale_in
        gate_ref[m] = gate
        up_ref[m] = up
        bent = jnp.tanh(ROOT * (gate + CUBE * gate * gate * gate))
        hidden = (0.5 * gate * (1.0 + bent) * up).astype(BF)
        hid_ref[m] = hidden
        acc[m] += nn(hidden, wd)

    @pl.when(i == pl.num_programs(0) - 1)
    def _():
        down_ref[...] = (acc[...] * scale_out).astype(BF)


def ffn(x, wg, wu, wd, scale_in, scale_out):
    def kernel(x_ref, wg_ref, wu_ref, wd_ref, gate_ref, up_ref, hid_ref, down_ref, acc):
        ffn_kernel(x_ref, wg_ref, wu_ref, wd_ref, gate_ref, up_ref, hid_ref, down_ref, acc, scale_in, scale_out)

    full = pl.BlockSpec((2, ROWS, D), lambda i: (0, 0, 0))
    wide = pl.BlockSpec((2, ROWS, FTILE), lambda i: (0, 0, i))
    width = wg.shape[1]
    return pl.pallas_call(
        kernel,
        grid=(width // FTILE,),
        out_shape=(
            jax.ShapeDtypeStruct((2, ROWS, width), F32),
            jax.ShapeDtypeStruct((2, ROWS, width), F32),
            jax.ShapeDtypeStruct((2, ROWS, width), BF),
            jax.ShapeDtypeStruct((2, ROWS, D), BF),
        ),
        in_specs=[
            full,
            pl.BlockSpec((D, FTILE), lambda i: (0, i)),
            pl.BlockSpec((D, FTILE), lambda i: (0, i)),
            pl.BlockSpec((FTILE, D), lambda i: (i, 0)),
        ],
        out_specs=(wide, wide, wide, full),
        scratch_shapes=[VMEM((2, ROWS, D), F32)],
        compiler_params=params(None, 40),
        cost_estimate=pl.CostEstimate(flops=1000, bytes_accessed=1000, transcendentals=0),
    )(x, wg, wu, wd)


def ffn_back(g, gate, up, wg, wu, wd, scale_in, scale_out):
    def kernel(g_ref, gate_ref, up_ref, wg_ref, wu_ref, wd_ref, dgate_ref, dup_ref, dx_ref, acc):
        i = pl.program_id(0)

        @pl.when(i == 0)
        def _():
            acc[...] = jnp.zeros_like(acc)

        for m in range(2):
            wg, wu, wd = wg_ref[...], wu_ref[...], wd_ref[...]
            if m == 1:
                wg, wu, wd = narrow(wg), narrow(wu), narrow(wd)
            grad = nt(g_ref[m], wd) * scale_out
            v, u = gate_ref[m], up_ref[m]
            bent = jnp.tanh(ROOT * (v + CUBE * v * v * v))
            half = 0.5 * (1.0 + bent)
            slope = half + 0.5 * v * (1.0 - bent * bent) * (ROOT * (1.0 + 3.0 * CUBE * v * v))
            dgate = (grad * u * slope).astype(BF)
            dup = (grad * (v * half)).astype(BF)
            dgate_ref[m] = dgate
            dup_ref[m] = dup
            acc[m] += nt(dgate, wg) + nt(dup, wu)

        @pl.when(i == pl.num_programs(0) - 1)
        def _():
            dx_ref[...] = (acc[...] * scale_in).astype(BF)

    full = pl.BlockSpec((2, ROWS, D), lambda i: (0, 0, 0))
    wide = pl.BlockSpec((2, ROWS, FTILE), lambda i: (0, 0, i))
    width = wg.shape[1]
    return pl.pallas_call(
        kernel,
        grid=(width // FTILE,),
        out_shape=(
            jax.ShapeDtypeStruct((2, ROWS, width), BF),
            jax.ShapeDtypeStruct((2, ROWS, width), BF),
            jax.ShapeDtypeStruct((2, ROWS, D), BF),
        ),
        in_specs=[
            full,
            wide,
            wide,
            pl.BlockSpec((D, FTILE), lambda i: (0, i)),
            pl.BlockSpec((D, FTILE), lambda i: (0, i)),
            pl.BlockSpec((FTILE, D), lambda i: (i, 0)),
        ],
        out_specs=(wide, wide, full),
        scratch_shapes=[VMEM((2, ROWS, D), F32)],
        compiler_params=params(None, 40),
        cost_estimate=pl.CostEstimate(flops=1000, bytes_accessed=1000, transcendentals=0),
    )(g, gate, up, wg, wu, wd)


PART = 576
SHARE = 72


def poster(ssem, rsem, copies):
    def post(src, dst, peer):
        k = len(copies)
        copies.append(send(src, dst, ssem.at[k], rsem.at[k], peer))
        return copies[k]

    return post


def total_start(post, p_ref, r1, rows, c, mate):
    return [post(p_ref.at[1 - c, r], r1.at[r], mate) for r in rows]


def total_across(post, p_ref, r1, h, r2, rows, c, far, one):
    two = []
    for k, r in enumerate(rows):
        one[k].wait_recv()
        h[r] = (p_ref[c, r].astype(F32) + r1[r].astype(F32)).astype(BF)
        two.append(post(h.at[r], r2.at[r], far))
    return two


def total_end(post, o_ref, h, r2, rows, c, mate, two):
    three = []
    for k, r in enumerate(rows):
        two[k].wait_recv()
        o_ref[c, r] = (h[r].astype(F32) + r2[r].astype(F32)).astype(BF)
        three.append(post(o_ref.at[c, r], o_ref.at[c, r], mate))
    for copy in three:
        copy.wait_recv()


def piece_rows():
    size = ROWS // PIECES
    return [pl.ds(k * size, size) for k in range(PIECES)]


def norm_grad(v, gain, grad):
    q = lax.rsqrt(jnp.mean(v * v, axis=-1, keepdims=True) + EPS)
    lifted = grad * gain
    back = q * lifted - v * (q * q * q * jnp.mean(lifted * v, axis=-1, keepdims=True))
    return back, jnp.sum(grad * v * q, axis=0, keepdims=True)


def mid_kernel(
    part, gain_mid, gain_out, q_ref, lse_ref, tag_ref, att_ref,
    middle_in, branch_in, up_in, wo_in, k_in, v_in, cg_own, cu_own, ch_own, da, dd,
    key_out, value_out, dq_ref, mgrad, bt, gains, cg, cu, ch, dg_land, dd_land,
    middle, branch, upstream, wo, k_ref, v_ref, blow, g_ref, dk, dv,
    t1, th, t2, total_ref, r1a, r1b, s1a, s1b, r2a, r2b, s2a, s2b, r3a, r3b,
    lsem, ssem, rsem,
    scale,
):
    x, y, z, zh, c = place_of()
    xi = [(x + j) % 4 for j in (1, 2, 3)]
    yi = [(y + j) % 4 for j in (1, 2, 3)]
    xs = [device_at(i, y, z, zh, c) for i in xi]
    ys = [device_at(x, i, z, zh, c) for i in yi]
    zp = device_at(x, y, 1 - z, zh, c)
    mate = device_at(x, y, z, zh, 1 - c)
    far = device_at(x, y, z, 1 - zh, c)
    copies, local = [], []
    post = poster(ssem, rsem, copies)

    def load(src, dst):
        copy = pltpu.make_async_copy(src, dst, lsem.at[len(local)])
        copy.start()
        local.append(copy)
        return copy

    loads = [
        load(*pair)
        for pair in (
            (middle_in, middle), (branch_in, branch), (up_in, upstream), (wo_in, wo), (k_in, k_ref), (v_in, v_ref),
        )
    ]
    greet(xs + ys + [zp, mate, far])
    rows = piece_rows()
    one = total_start(post, part, t1, rows, c, mate)
    band_x = pl.ds(pl.multiple_of(x * 256, 256), 256)
    band_y = pl.ds(pl.multiple_of(y * 256, 256), 256)
    for j in (0, 2, 1):
        post(da.at[xi[j]], dg_land.at[:, band_x], xs[j])
        post(dd.at[yi[j]], dd_land.at[:, band_y], ys[j])
    for j in (0, 2, 1):
        post(cg_own, cg.at[band_x], xs[j])
        post(ch_own, ch.at[band_y], ys[j])
    for j in (0, 2, 1):
        post(cu_own, cu.at[band_x], xs[j])
    carried = copies[len(one) :]
    for pair in (
        (da.at[x], dg_land.at[:, band_x]), (dd.at[y], dd_land.at[:, band_y]),
        (cg_own, cg.at[band_x]), (cu_own, cu.at[band_x]), (ch_own, ch.at[band_y]),
    ):
        load(*pair)
    two = total_across(post, part, t1, th, t2, rows, c, far, one)
    total_end(post, total_ref, th, t2, rows, c, mate, two)
    for copy in loads[:4]:
        copy.wait()

    zero = jnp.zeros((1, D), F32)
    for m in range(2):

        def slab(i, carry):
            sum_mid, sum_out = carry
            r = pl.ds(pl.multiple_of(i * 16, 16), 16)
            back, more = norm_grad(middle[m, r], gain_mid[...], total_ref[m, r].astype(F32))
            grad = upstream[m, r].astype(F32) + back
            mgrad[m, r] = grad
            back, most = norm_grad(branch[m, r].astype(F32), gain_out[...], grad)
            blow[m, r] = back.astype(BF)
            return sum_mid + more, sum_out + most

        sums = lax.fori_loop(0, ROWS // 16, slab, (zero, zero) if m == 0 else sums)
    gains[0:1] = sums[1]
    gains[1:2] = sums[0]
    for m in range(2):
        weight = wo[...] if m == 0 else narrow(wo[...])
        wide = (nt(blow[m], weight) * scale).astype(BF)
        g_ref[m, :ROWS] = wide[:, :HD]
        g_ref[m, ROWS:] = wide[:, HD:]
        turned = blow[m].T
        for zi in range(2):
            for k in range(4):
                at = (zi * 4 + k) * 288
                bt[zi, k, :, m * ROWS : (m + 1) * ROWS] = turned[at : at + 288]

    loads[4].wait()
    loads[5].wait()
    limit = lax.axis_index("blk") // CHUNK + 1
    where = query_places()
    for m in range(2):
        q = q_ref[m]
        g = g_ref[m]
        tag = tag_ref[m]
        lse = lse_ref[m]
        off = jnp.sum(g.astype(F32) * att_ref[m], axis=-1, keepdims=True)
        span = slice(m * ROWS, (m + 1) * ROWS)

        def step(i, dq):
            keys, values, tag_row = load_chunk(k_ref, v_ref, i, m)
            bent = jnp.tanh(nt(q, keys) * (HD ** (-0.5) / CAP))
            p = jnp.where(allowed(i, tag_row, tag, where), jnp.exp(CAP * bent - lse), 0.0)
            dp = nt(g, values)
            ds = (p * (dp - off) * (1.0 - bent * bent) * HD ** (-0.5)).astype(BF)
            dk[i // 4, i % 4, :, span, :] = tn(ds, q).astype(BF).reshape(CHUNK, ROWS, HD)
            dv[i // 4, i % 4, :, span, :] = tn(p.astype(BF), g).astype(BF).reshape(CHUNK, ROWS, HD)
            return dq + nn(ds, keys)

        dq_ref[m] = lax.fori_loop(0, limit, step, jnp.zeros((2 * ROWS, HD), F32))

        def blank(i, carry):
            dk[i // 4, i % 4, :, span, :] = jnp.zeros((CHUNK, ROWS, HD), BF)
            dv[i // 4, i % 4, :, span, :] = jnp.zeros((CHUNK, ROWS, HD), BF)
            return carry

        lax.fori_loop(limit, SEQ // KEYS, blank, 0)

    one_a = [post(dk.at[:, :, xi[j]], r1a.at[j], xs[j]) for j in range(3)]
    one_b = [post(dv.at[:, yi[j]], r1b.at[j], ys[j]) for j in range(3)]
    for copy in one_a:
        copy.wait_recv()

    def add_a(i, carry):
        zi, k = i // 4, i % 4
        out = dk[zi, k, x].astype(F32)
        for j in range(3):
            out = out + r1a[j, zi, k].astype(F32)
        s1a[zi, k] = out.astype(BF)
        return carry

    lax.fori_loop(0, 8, add_a, 0)
    two_a = [post(s1a.at[:, yi[j]], r2a.at[j], ys[j]) for j in range(3)]
    for copy in one_b:
        copy.wait_recv()

    def add_b(i, carry):
        zi, k = i // 4, i % 4
        out = dv[zi, y, k].astype(F32)
        for j in range(3):
            out = out + r1b[j, zi, k].astype(F32)
        s1b[zi, k] = out.astype(BF)
        return carry

    lax.fori_loop(0, 8, add_b, 0)
    two_b = [post(s1b.at[:, xi[j]], r2b.at[j], xs[j]) for j in range(3)]

    def second(arrivals, own, mine, land, half):
        for copy in arrivals:
            copy.wait_recv()
        for zi in range(2):
            out = own[zi, mine].astype(F32)
            for j in range(3):
                out = out + land[j, zi].astype(F32)
            half[zi] = out.astype(BF)

    second(two_a, s1a, y, r2a, s2a)
    three_a = post(s2a.at[1 - z], r3a, zp)
    second(two_b, s1b, x, r2b, s2b)
    three_b = post(s2b.at[1 - z], r3b, zp)
    three_a.wait_recv()
    key_out[...] = s2a[z].astype(F32) + r3a[...].astype(F32)
    three_b.wait_recv()
    value_out[...] = s2b[z].astype(F32) + r3b[...].astype(F32)
    for copy in carried:
        copy.wait_recv()
    for copy in local[6:]:
        copy.wait()
    for copy in copies:
        copy.wait_send()


def mid(part, gain_mid, gain_out, q, lse, tag, att, middle, branch, up, wo, k, v, cg, cu, ch, da, dd, scale):
    def kernel(*refs):
        mid_kernel(*refs, scale)

    any_ = whole(pl.ANY)
    tile = (2 * ROWS, HD)
    wide = (4 * 2 * ROWS, D)
    sems = 4 + 15 + 4 + 4 + 6 + 6 + 2
    return pl.pallas_call(
        kernel,
        out_shape=[
            jax.ShapeDtypeStruct(tile, F32),
            jax.ShapeDtypeStruct(tile, F32),
            jax.ShapeDtypeStruct((2,) + tile, F32),
            jax.ShapeDtypeStruct((2, ROWS, D), F32),
            jax.ShapeDtypeStruct((2, 4, 288, 2 * ROWS), BF),
            jax.ShapeDtypeStruct((2, D), F32),
            jax.ShapeDtypeStruct(wide, BF),
            jax.ShapeDtypeStruct(wide, BF),
            jax.ShapeDtypeStruct(wide, BF),
            jax.ShapeDtypeStruct((PART, 1024), BF),
            jax.ShapeDtypeStruct((PART, 1024), BF),
        ],
        in_specs=[whole()] * 7 + [any_] * 11,
        out_specs=[whole()] * 6 + [any_] * 5,
        scratch_shapes=[
            VMEM(middle.shape, F32),
            VMEM(branch.shape, BF),
            VMEM(up.shape, BF),
            VMEM(wo.shape, BF),
            VMEM(k.shape, BF),
            VMEM(v.shape, BF),
            VMEM((2, ROWS, D), BF),
            VMEM((2,) + tile, BF),
            VMEM((2, 4, 4) + tile, BF),
            VMEM((2, 4, 4) + tile, BF),
            VMEM((ROWS, D), BF),
            VMEM((ROWS, D), BF),
            VMEM((ROWS, D), BF),
            VMEM((2, ROWS, D), BF),
            VMEM((3, 2, 4) + tile, BF),
            VMEM((3, 2, 4) + tile, BF),
            VMEM((2, 4) + tile, BF),
            VMEM((2, 4) + tile, BF),
            VMEM((3, 2) + tile, BF),
            VMEM((3, 2) + tile, BF),
            VMEM((2,) + tile, BF),
            VMEM((2,) + tile, BF),
            VMEM(tile, BF),
            VMEM(tile, BF),
            pltpu.SemaphoreType.DMA((11,)),
            pltpu.SemaphoreType.DMA((sems,)),
            pltpu.SemaphoreType.DMA((sems,)),
        ],
        compiler_params=params(2, 62),
    )(part, gain_mid, gain_out, q, lse, tag, att, middle, branch, up, wo, k, v, cg, cu, ch, da, dd)


def turn(values, cosine, sine):
    half = HD // 2
    first, second = values[:, :half], values[:, half:]
    return jnp.concatenate([first * cosine - second * sine, second * cosine + first * sine], axis=1)


def end_kernel(
    key_ref, value_ref, dq_ref, cos_ref, sin_ref, gain_in, gains_in,
    bt, wq_in, wk_in, wv_in, tok_in, mgrad_in, dg_in, cg_in, dd_in, ch_in, cu_in, dn_in, ca_in,
    igrad, og, ou, od, oq, on,
    wq, wk, wv, tok, mgrad, dg, c0, dd, c1, dn, ca, db, cq,
    part, t1, th, t2, total_ref, gpad, gb, rgb,
    pg, pu, pd, pq, pn, rg, ru, rd, rq, rn, sg, su, sd, sq, sn, zg, zu, zd, zq, zn,
    lsem, ssem, rsem,
    scale,
):
    x, y, z, zh, c = place_of()
    xi = [(x + j) % 4 for j in (1, 2, 3)]
    yi = [(y + j) % 4 for j in (1, 2, 3)]
    xs = [device_at(i, y, z, zh, c) for i in xi]
    ys = [device_at(x, i, z, zh, c) for i in yi]
    zp = device_at(x, y, 1 - z, zh, c)
    mate = device_at(x, y, z, zh, 1 - c)
    far = device_at(x, y, z, 1 - zh, c)
    copies, local = [], []
    post = poster(ssem, rsem, copies)

    def load(src, dst):
        copy = pltpu.make_async_copy(src, dst, lsem.at[len(local)])
        copy.start()
        local.append(copy)
        return copy

    band_y = pl.ds(pl.multiple_of(y * 256, 256), 256)
    weights = [load(*pair) for pair in ((wq_in, wq), (wk_in, wk), (wv_in, wv))]
    got_g = [load(dg_in, dg), load(cg_in, c0)]
    got_d = [load(dd_in, dd), load(ch_in, c1)]
    got_t = [load(tok_in, tok), load(mgrad_in, mgrad)]
    got_q = [load(dn_in, dn), load(ca_in, ca), load(bt.at[:, y], db.at[:, :, band_y])]
    greet(xs + ys + [zp, mate, far])
    got_q_far = [post(bt.at[:, yi[j]], db.at[:, :, band_y], ys[j]) for j in range(3)]

    for m in range(2):
        r = slice(m * ROWS, (m + 1) * ROWS)
        own = pl.ds(pl.multiple_of(y * 256, 256) + m * ROWS, ROWS)
        cosine, sine = cos_ref[...], -sin_ref[...]
        for h in range(2):
            turned = turn(dq_ref[m, h * ROWS : (h + 1) * ROWS], cosine, sine)
            cq[own, h * HD : (h + 1) * HD] = turned.astype(BF)
        cq[own, 2 * HD : 3 * HD] = turn(key_ref[r], cosine, sine).astype(BF)
        cq[own, 3 * HD :] = value_ref[r].astype(BF)
    got_q_far += [post(cq.at[band_y], cq.at[band_y], ys[j]) for j in range(3)]
    for copy in weights:
        copy.wait()
    for m in range(2):
        own = pl.ds(pl.multiple_of(y * 256, 256) + m * ROWS, ROWS)
        a, b, v = wq[...], wk[...], wv[...]
        if m == 1:
            a, b, v = narrow(a), narrow(b), narrow(v)
        out = nt(cq[own, : 2 * HD], a) + nt(cq[own, 2 * HD : 3 * HD], b) + nt(cq[own, 3 * HD :], v)
        part[m] = (out * scale).astype(BF)
    rows = piece_rows()
    one = total_start(post, part, t1, rows, c, mate)
    two = total_across(post, part, t1, th, t2, rows, c, far, one)

    def multiply(left, right, out_ref, width, base, tile):
        def body(t, carry):
            cols = pl.ds(pl.multiple_of(t * tile, tile), tile)
            outs = pl.ds(pl.multiple_of(base + t * tile, 256), tile)
            out = nn(left[...].reshape(PART, 1024), right[:, cols])
            out_ref[:, :, :, outs] = out.reshape(2, 4, SHARE, tile).astype(BF)
            return carry

        lax.fori_loop(0, width // tile, body, 0)

    def spread(p, land, along):
        if along == "y":
            return [post(p.at[:, yi[j]], land.at[j], ys[j]) for j in range(3)]
        return [post(p.at[:, xi[j]], land.at[j], xs[j]) for j in range(3)]

    def reduce(p, land, half, own, arrivals, across):
        for copy in arrivals:
            copy.wait_recv()

        def body(t, carry):
            cols = pl.ds(pl.multiple_of(t * 128, 128), 128)
            for zi in range(2):
                out = p[zi, own, :, cols].astype(F32)
                for j in range(3):
                    out = out + land[j, zi, :, cols].astype(F32)
                half[zi, :, cols] = out.astype(BF)
            return carry

        lax.fori_loop(0, half.shape[-1] // 128, body, 0)
        return post(half.at[1 - z], across, zp)

    def finish(copy, half, across, out):
        copy.wait_recv()
        out[...] = half[z].astype(F32) + across[...].astype(F32)

    for copy in got_g:
        copy.wait()
    multiply(dg, c0, pg, D, 0, 768)
    two_g = spread(pg, rg, "y")
    got_u = load(cu_in, c0)
    for copy in got_d:
        copy.wait()
    multiply(dd, c1, pd, D, 0, 768)
    two_d = spread(pd, rd, "x")
    total_end(post, total_ref, th, t2, rows, c, mate, two)

    for copy in got_t:
        copy.wait()
    sums = jnp.zeros((1, D), F32)
    for m in range(2):

        def slab(i, carry):
            r = pl.ds(pl.multiple_of(i * 16, 16), 16)
            back, more = norm_grad(tok[m, r].astype(F32), gain_in[...], total_ref[m, r].astype(F32))
            igrad[m, r] = (mgrad[m, r] + back).astype(BF)
            return carry + more

        sums = lax.fori_loop(0, ROWS // 16, slab, sums)
    gpad[...] = jnp.zeros_like(gpad)
    gpad[0:1] = sums
    gpad[1:4] = gains_in[...]
    turned = gpad[...].T.astype(BF)
    for zi in range(2):
        for k in range(4):
            at = (zi * 4 + k) * 288
            gb[zi, k] = turned[at : at + 288]
    gains_far = [post(gb.at[:, yi[j]], rgb.at[j], ys[j]) for j in range(3)]

    got_u.wait()
    multiply(dg, c0, pu, D, 0, 768)
    two_u = spread(pu, ru, "y")
    for copy in got_q:
        copy.wait()
    for copy in got_q_far:
        copy.wait_recv()
    multiply(dn, cq, pq, 1024, 0, 512)
    multiply(db, ca, pq, 512, 1024, 512)
    two_q = spread(pq, rq, "x")
    out = gb[:, y].astype(F32)
    for j in range(3):
        gains_far[j].wait_recv()
        out = out + rgb[j].astype(F32)
    pn[...] = out.reshape(2, 4, SHARE, 128).astype(BF)
    two_n = spread(pn, rn, "x")
    three_g = reduce(pg, rg, sg, y, two_g, zg)
    three_d = reduce(pd, rd, sd, x, two_d, zd)
    finish(three_g, sg, zg, og)
    finish(three_d, sd, zd, od)
    three_u = reduce(pu, ru, su, y, two_u, zu)
    three_q = reduce(pq, rq, sq, x, two_q, zq)
    three_n = reduce(pn, rn, sn, x, two_n, zn)
    finish(three_u, su, zu, ou)
    finish(three_q, sq, zq, oq)
    finish(three_n, sn, zn, on)
    for copy in copies:
        copy.wait_send()


def end(key, value, dq, cosine, sine, gain_in, gains, bt, wq, wk, wv, tok, mgrad, dg, cg, dd, ch, cu, dn, ca, scale):
    def kernel(*refs):
        end_kernel(*refs, scale)

    widths = (D, D, D, 1536, 128)
    sems = 6 + 12 + 3 + 15 + 5
    return pl.pallas_call(
        kernel,
        out_shape=[jax.ShapeDtypeStruct((2, ROWS, D), BF)]
        + [jax.ShapeDtypeStruct((SHARE, w), F32) for w in widths],
        in_specs=[whole()] * 7 + [whole(pl.ANY)] * 13,
        out_specs=[whole()] * 6,
        scratch_shapes=[
            VMEM(wq.shape, BF),
            VMEM(wk.shape, BF),
            VMEM(wv.shape, BF),
            VMEM(tok.shape, BF),
            VMEM(mgrad.shape, F32),
            VMEM(dg.shape, BF),
            VMEM(cg.shape, BF),
            VMEM(dd.shape, BF),
            VMEM(ch.shape, BF),
            VMEM(dn.shape, BF),
            VMEM(ca.shape, BF),
            VMEM((2, 288, 1024), BF),
            VMEM((1024, 1024), BF),
            VMEM((2, ROWS, D), BF),
            VMEM((ROWS, D), BF),
            VMEM((ROWS, D), BF),
            VMEM((ROWS, D), BF),
            VMEM((2, ROWS, D), BF),
            VMEM((128, D), F32),
            VMEM((2, 4, 288, 128), BF),
            VMEM((3, 2, 288, 128), BF),
        ]
        + [VMEM((2, 4, SHARE, w), BF) for w in widths]
        + [VMEM((3, 2, SHARE, w), BF) for w in widths]
        + [VMEM((2, SHARE, w), BF) for w in widths]
        + [VMEM((SHARE, w), BF) for w in widths]
        + [
            pltpu.SemaphoreType.DMA((13,)),
            pltpu.SemaphoreType.DMA((sems,)),
            pltpu.SemaphoreType.DMA((sems,)),
        ],
        compiler_params=params(3, 63),
    )(key, value, dq, cosine, sine, gain_in, gains, bt, wq, wk, wv, tok, mgrad, dg, cg, dd, ch, cu, dn, ca)


def rows_for_x(left):
    t = left.T.reshape(2, 4, 4, SHARE, left.shape[0])
    return t.transpose(2, 0, 1, 3, 4).reshape(4, PART, left.shape[0])


def rows_for_y(left):
    t = left.T.reshape(2, 4, 4, SHARE, left.shape[0])
    return t.transpose(1, 0, 2, 3, 4).reshape(4, PART, left.shape[0])


def sliced(codes, bits):
    if bits == 8:
        return codes
    spacing = 2.0 ** (8 - bits)
    upper = 2.0 ** (bits - 1)
    wide = codes.astype(F32)
    return (jnp.clip(jnp.floor(wide / spacing + 0.5), -upper, upper - 1.0) * spacing).astype(BF)


def norm_rows(values, gain):
    return values * lax.rsqrt(jnp.mean(values * values, axis=-1, keepdims=True) + EPS) * gain


def norm_back(values, gain, grad):
    q = lax.rsqrt(jnp.mean(values * values, axis=-1, keepdims=True) + EPS)
    lifted = grad * gain
    back = q * lifted - values * (q * q * q) * jnp.mean(lifted * values, axis=-1, keepdims=True)
    return back, jnp.sum(grad * values * q, axis=(0, 1))


def rotate(values, cosine, sine):
    half = values.shape[-1] // 2
    first = values[..., :half]
    second = values[..., half:]
    return jnp.concatenate(
        [first * cosine - second * sine, second * cosine + first * sine], axis=-1
    )


def shards(
    inputs,
    out_grad,
    segment_ids,
    keep_mask,
    query_codes,
    key_codes,
    value_codes,
    output_codes,
    gate_codes,
    up_codes,
    down_codes,
    norm_attn_in,
    norm_attn_out,
    norm_ffn_in,
    norm_ffn_out,
):
    rows = inputs.shape[1]
    place = lax.axis_index("blk") * rows + jnp.arange(rows, dtype=jnp.int32)
    freqs = 10000.0 ** (-jnp.arange(HD // 2, dtype=F32) * 2.0 / HD)
    angles = place.astype(F32)[:, None] * freqs[None, :]
    cosine = jnp.cos(angles)
    sine = jnp.sin(angles)
    in_scale = LEVEL_SCALE * D ** (-0.5)
    mid_scale = LEVEL_SCALE * (HEADS * HD) ** (-0.5)
    ff_scale = LEVEL_SCALE * FF ** (-0.5)

    def by_batch(left, codes, scale, back=False):
        parts = []
        for m in range(2):
            weight = sliced(codes, WIDTHS[m])
            parts.append((nt if back else nn)(left[m], weight) * scale)
        return jnp.stack(parts)

    tokens = inputs.astype(F32)
    normed = norm_rows(tokens, norm_attn_in).astype(BF)
    q_raw = by_batch(normed, query_codes, in_scale).reshape(2, rows, 2, HD).transpose(0, 2, 1, 3)
    queries = rotate(q_raw, cosine, sine).astype(BF).reshape(2, 2 * rows, HD)
    key_own = rotate(by_batch(normed, key_codes, in_scale), cosine, sine).astype(BF)
    value_own = by_batch(normed, value_codes, in_scale).astype(BF)
    key_tag = jnp.where(keep_mask == 1, segment_ids, -1).astype(BF).reshape(1, 2 * rows)
    packed = jnp.concatenate(
        [key_own.reshape(2 * rows, HD), jnp.broadcast_to(key_tag, (16, 2 * rows))], axis=0
    )
    keys, values = gather(packed, value_own.reshape(2 * rows, HD))
    keys = keys.reshape(32, 2 * rows + 16, HD)
    values = values.reshape(32, 2 * rows, HD)
    tag = segment_ids.astype(F32)
    tag = jnp.concatenate([tag, tag], axis=1)[:, :, None]
    attended, lse = attend(queries, tag, keys, values)

    def flat(heads):
        return heads.reshape(2, 2, rows, HD).transpose(0, 2, 1, 3).reshape(2, rows, 2 * HD)

    def both(left):
        return left.reshape(2 * rows, left.shape[-1])

    attended_flat = flat(attended).astype(BF)
    branch, (d_normed,) = total(
        by_batch(attended_flat, output_codes, mid_scale).astype(BF),
        4,
        [("swap", "y", rows_for_y(both(normed)))],
    )
    branch_low = branch
    branch = branch.astype(F32)
    middle = tokens + norm_rows(branch, norm_attn_out)
    ffn_in = norm_rows(middle, norm_ffn_in).astype(BF)
    gate, upper, hidden, down_part = ffn(
        ffn_in, gate_codes, up_codes, down_codes, in_scale, ff_scale
    )
    down, (all_attended,) = total(down_part, 5, [("copy", "y", both(attended_flat))])
    down = down.astype(F32)
    out_rows = (middle + norm_rows(down, norm_ffn_out)).astype(BF)

    upstream = out_grad.astype(F32)
    down_grad, gain_ffn_out = norm_back(down, norm_ffn_out, upstream)
    down_low = down_grad.astype(BF)
    gate_low, up_low, ffn_part = ffn_back(
        down_low, gate, upper, gate_codes, up_codes, down_codes, in_scale, ff_scale
    )
    key_rot, value_grad, query_rot, middle_grad, d_branch, gains, cg, cu, ch, d_ffn_in, d_down = mid(
        ffn_part, norm_ffn_in[None], norm_attn_out[None], queries, lse, tag, attended,
        middle, branch_low, out_grad, output_codes, keys, values,
        both(gate_low), both(up_low), both(hidden),
        rows_for_x(both(ffn_in)), rows_for_y(both(down_low)), mid_scale,
    )
    gains = jnp.concatenate([gains, gain_ffn_out[None]])
    input_grad, g_gate, g_up, g_down, g_rest, g_gains = end(
        key_rot, value_grad, query_rot, cosine, sine, norm_attn_in[None], gains,
        d_branch, query_codes, key_codes, value_codes, inputs, middle_grad,
        d_ffn_in, cg, d_down, ch, cu, d_normed, all_attended, in_scale,
    )
    return (
        out_rows,
        input_grad,
        g_rest[:, :512] * in_scale,
        g_rest[:, 512:768] * in_scale,
        g_rest[:, 768:1024] * in_scale,
        g_rest[:, 1024:1536].T * mid_scale,
        g_gate * in_scale,
        g_up * in_scale,
        g_down.T * ff_scale,
        g_gains[:, 0],
        g_gains[:, 1],
        g_gains[:, 2],
        g_gains[:, 3],
    )


def solution(mesh):
    placed = (
        P(None, "blk", None),
        P(None, "blk", None),
        P(None, "blk"),
        P(None, "blk"),
        P(None, "tensor"),
        P(None, "tensor"),
        P(None, "tensor"),
        P("tensor", None),
        P(None, "tensor"),
        P(None, "tensor"),
        P("tensor", None),
        P(),
        P(),
        P(),
        P(),
    )
    return jax.shard_map(
        shards,
        mesh=mesh,
        in_specs=placed,
        out_specs=(
            P(None, "blk", None),
            P(None, "blk", None),
            P("blk", "tensor"),
            P("blk", "tensor"),
            P("blk", "tensor"),
            P("tensor", "blk"),
            P("blk", "tensor"),
            P("blk", "tensor"),
            P("tensor", "blk"),
            P("blk"),
            P("blk"),
            P("blk"),
            P("blk"),
        ),
        check_vma=False,
    )
```

time: 658 us -> 516 us (0.78)
  matrix products: 95.1 us -> 7.08 us
  local copies, waits for them, and re-layouts: 50.3 us -> 19.9 us
  other arithmetic: 43.9 us -> 17.4 us
    dot_general x14 -> x0, matrix products: 54 us -> none  [nt(): lax.dot_general(left, right, (((1,), (1,)), ((), ())), preferred_element_...]
    dot_general x14 -> x8, matrix products: 41 us -> 7.08 us  [nn(): return jnp.dot(left, right, preferred_element_type=F32)]
    convert_element_type x9 -> x0, other arithmetic: 14.5 us -> none  [the longest x1 3.65 us: shards(): gate_low = gate_grad.astype(BF)]
    unnamed x204 -> x72, local copies, waits for them, and re-layouts: 19.8 us -> 7.7 us
    pallas_call x7 -> x6, Pallas kernels: 396 us -> 398 us  [the longest x1 191 us: mid(): pl.pallas_call(kernel, out_shape=[jax.ShapeDtypeStruct(tile, F32), jax.Sh...]
where the time goes in v2:
time: 516 us; the launch traced here: 513 us
  Pallas kernels  467 us (91%)
  local copies, waits for them, and re-layouts  19.9 us (4%)
  other arithmetic  17.4 us (3%)
  matrix products  7.08 us (1%)
    pallas_call x1, Pallas kernels, mid(): pl.pallas_call(kernel, out_shape=[jax.ShapeDtypeStruct(tile, F32), jax.Sh...  191 us
    pallas_call x1, Pallas kernels, end(): pl.pallas_call(kernel, out_shape=[jax.ShapeDtypeStruct((2, ROWS, D), BF)]...  117 us
    pallas_call x1, Pallas kernels, gather(): pl.pallas_call(gather_kernel, out_shape=(jax.ShapeDtypeStruct((2, 4, 4) +...  67.8 us
    pallas_call x2, Pallas kernels, total(): pl.pallas_call(functools.partial(total_kernel, kinds), out_shape=[jax.Sha...  42.3 us
    pallas_call x1, Pallas kernels, ffn_back(): pl.pallas_call(kernel, grid=(width // FTILE,), out_shape=(jax.ShapeDtypeS...  26.3 us
    pallas_call x1, Pallas kernels, ffn(): pl.pallas_call(kernel, grid=(width // FTILE,), out_shape=(jax.ShapeDtypeS...  21.2 us

profile of v2, /device:TPU:1, one launch (start us, length us, event | category | flops | bytes accessed | tf_op | source)
XLA Modules:
  0.0 513.0 jit_solution(1158246999342615169)
XLA Ops:
  0.6 0.0 copy-start.16
  0.7 1.7 fusion.9
  2.4 1.6 fusion.11
  4.0 2.0 fusion.27
  6.0 1.8 stack.43
  7.8 1.7 copy.33
  9.5 1.2 convolution_multiply_fusion.2
  10.7 1.2 stack.42
  11.9 1.0 maximum_bitcast_fusion
  13.0 0.3 multiply_cosine_fusion
  13.3 0.0 copy-start.23
  13.3 0.0 copy-start.24
  13.3 0.1 subtract_convert_fusion
  13.4 0.0 copy-start.3
  13.5 0.1 copy.34.t_ref.refs_5_
  13.7 0.7 fusion.30
  14.4 0.0 copy-start.18
  14.4 0.3 fusion.31
  14.8 0.8 copy-done.18
  15.6 0.7 fusion.34
  16.4 0.3 fusion.35
  16.7 67.8 %shard_map.246 = (bf16[2,4,4,272,256]{4,3,2,1,0:T(8,128)(2,1)S(1)}, bf16[2,4,4,256,256]{4,3,2,1,0:T(8,128)(2,1)S(1)}) custom-call(bf16[272,256]{1,0:T(8,128)(2,1)S(1)} %pad_maximum_fusion.2.a_ref, bf16[256,256]{1,0:T(8,128)(2,1)S(1)} %bitcast.92), custom_call_target="tpu_custom_call" | custom-call | tf_op jit(solution)/shard_map/pallas_call | solution.py:114
  84.6 0.0 copy-start.17
  84.6 1.3 shard_map.247
  85.9 0.9 copy-done
  86.8 1.4 copy-done.1
  88.2 0.3 copy.48
  88.5 0.2 fusion.60
  88.7 1.3 fusion.2
  90.1 0.5 fusion.3
  90.6 0.1 pad_maximum_fusion.refs_0_
  90.8 0.8 copy.36
  91.6 0.1 copy.37
  91.6 0.0 copy-start.14
  91.7 22.2 %shard_map.248 = (bf16[2,128,2304]{2,1,0:T(8,128)(2,1)S(1)}, bf16[576,1024]{1,0:T(8,128)(2,1)S(1)}) custom-call(bf16[2,128,2304]{2,1,0:T(8,128)(2,1)S(1)} %pad_maximum_fusion.refs_0_, bf16[4,576,256]{2,1,0:T(8,128)(2,1)S(1)} %bitcast.87), custom_call_target="tpu_custom_call" | custom-call | flops 1000 | bytes 1000 | tf_op jit(solution)/shard_map/pallas_call | solution.py:195
  113.8 0.3 fusion.7
  114.2 0.7 multiply_reduce_fusion
  114.9 0.3 copy-done.6
  115.3 0.3 multiply_convert_fusion.2.x_ref
  115.5 21.2 %shard_map.249 = (f32[2,128,2304]{2,1,0:T(8,128)S(1)}, f32[2,128,2304]{2,1,0:T(8,128)S(1)}, bf16[2,128,2304]{2,1,0:T(8,128)(2,1)S(1)}, bf16[2,128,2304]{2,1,0:T(8,128)(2,1)S(1)}) custom-call(bf16[2,128,2304]{2,1,0:T(8,128)(2,1)S(1)} %multiply_convert_fusion.2.x_ref, bf16[2304,2304]{1,0:T(8,128)(2,1)} %wg_ref.3, bf16[2304,2304]{1,0:T(8,128)(2,1)} %wu_ref.3, ...), custom_call_target="tpu_custom_call" | custom-call | flops 1000 | bytes 1000 | tf_op jit(solution)/shard_map/pallas_call | solution.py:328
  136.8 20.1 %shard_map.250 = (bf16[2,128,2304]{2,1,0:T(8,128)(2,1)S(1)}, bf16[1024,512]{1,0:T(8,128)(2,1)S(1)}) custom-call(bf16[2,128,2304]{2,1,0:T(8,128)(2,1)S(1)} %get-tuple-element.49.refs_0_, bf16[256,512]{1,0:T(8,128)(2,1)S(1)} %bitcast.91), custom_call_target="tpu_custom_call" | custom-call | flops 1000 | bytes 1000 | tf_op jit(solution)/shard_map/pallas_call | solution.py:195
  157.0 0.3 fusion.12
  157.3 0.8 fusion.19
  158.1 2.0 fusion.6
  160.2 26.3 %shard_map.251 = (bf16[2,128,2304]{2,1,0:T(8,128)(2,1)S(1)}, bf16[2,128,2304]{2,1,0:T(8,128)(2,1)S(1)}, bf16[2,128,2304]{2,1,0:T(8,128)(2,1)S(1)}) custom-call(bf16[2,128,2304]{2,1,0:T(8,128)(2,1)S(1)} %get-tuple-element.85.g_ref, f32[2,128,2304]{2,1,0:T(8,128)S(1)} %get-tuple-element.51.gate_ref, f32[2,128,2304]{2,1,0:T(8,128)S(1)} %get-tuple-element.52.up_ref, ...), custom_call_target="tpu_custom_call" | custom-call | flops 1000 | bytes 1000 | tf_op jit(solution)/shard_map/pallas_call | solution.py:380
  186.5 1.0 copy-done.8
  187.5 1.0 copy-done.9
  188.5 1.0 copy-done.10
  189.5 0.6 broadcast_in_dim.22.refs_1_
  190.1 0.6 broadcast_in_dim.23.refs_2_
  190.7 0.6 copy.38
  191.3 1.1 copy.39
  192.5 0.6 copy.40
  193.1 1.1 copy.41
  194.2 191.4 %shard_map.252 = (f32[256,256]{1,0:T(8,128)}, f32[256,256]{1,0:T(8,128)}, f32[2,256,256]{2,1,0:T(8,128)}, f32[2,128,2304]{2,1,0:T(8,128)}, bf16[2,4,288,256]{3,2...) custom-call(bf16[2,128,2304]{2,1,0:T(8,128)(2,1)} %copy-done.10, ...), custom_call_target="tpu_custom_call" | custom-call | tf_op jit(solution)/shard_map/pallas_call | solution.py:627
  385.6 0.6 broadcast_in_dim.24.refs_5_
  386.2 1.4 pad_maximum_fusion.5.refs_6_
  387.6 117.0 %shard_map.253 = (bf16[2,128,2304]{2,1,0:T(8,128)(2,1)}, f32[72,2304]{1,0:T(8,128)}, f32[72,2304]{1,0:T(8,128)}, f32[72,2304]{1,0:T(8,128)}, f32[72,1536]{1,0:T(8,128)}, /*index=5*/f32[72,128]{1,0:T(8,128)}) custom-call(f32[256,256]{1,0:T(8,128)} %get-tuple-element.58.refs_0_, f32[256,256]{1,0:T(8,128)} %get-tuple-element.59.refs_1_, ...), custom_call_target="tpu_custom_call" | custom-call | tf_op jit(solution)/shard_map/pallas_call | solution.py:846
  504.6 1.8 multiply_bitcast_fusion.1
  506.4 1.7 slice_multiply_fusion.1
  508.1 2.0 broadcast_multiply_fusion.1
  510.1 1.2 multiply_bitcast_fusion
  511.3 0.7 slice_reduce_fusion
  512.0 1.0 copy.50
  (74 shorter events, 0.4 us)
Async XLA Ops:
  0.6 3.4 copy-start.16
  10.7 2.7 copy-start.32
  10.7 2.7 copy-start.33
  10.7 3.0 copy-start.19
  13.3 1.4 copy-start.23
  13.3 1.4 copy-start.24
  13.4 71.2 %copy-start.3 = (bf16[2,256,256]{2,1,0:T(8,128)(2,1)}, bf16[2,256,256]{2,1,0:T(8,128)(2,1)S(1)}, u32[]{:S(2)}) copy-start(bf16[2,256,256]{2,1,0:T(8,128)(2,1)S(1)} %pad_maximum_fusion.1.q_ref.refs_3_) | copy-start | bytes 786436
  13.6 71.0 %copy-start.4 = (f32[2,256,1]{2,1,0:T(8,128)}, f32[2,256,1]{2,1,0:T(8,128)S(1)}, u32[]{:S(2)}) copy-start(f32[2,256,1]{2,1,0:T(8,128)S(1)} %copy.34.t_ref.refs_5_) | copy-start | bytes 6148
  14.4 1.3 copy-start.18
  84.6 2.3 copy-start
  84.6 3.6 copy-start.1
  84.6 4.1 copy-start.17
  88.2 1.9 copy-start.5
  88.2 1.9 copy-start.12
  88.5 1.6 copy-start.20
  91.6 22.5 %copy-start.14 = (bf16[2,128,2304]{2,1,0:T(8,128)(2,1)S(1)}, bf16[2,128,2304]{2,1,0:T(8,128)(2,1)}, u32[]{:S(2)}) copy-start(bf16[2,128,2304]{2,1,0:T(8,128)(2,1)} %refs_11_.1) | copy-start | bytes 3538948
  91.7 22.5 %copy-start.30 = (f32[2304]{0:T(1024)S(1)}, f32[2304]{0:T(1024)}, u32[]{:S(2)}) copy-start(f32[2304]{0:T(1024)} %param.27) | copy-start | bytes 27652
  113.8 1.1 copy-start.2
  113.8 1.4 copy-start.6
  114.2 1.1 copy-start.29
  115.2 42.9 %copy-start.13 = (f32[2,128,2304]{2,1,0:T(8,128)}, f32[2,128,2304]{2,1,0:T(8,128)S(1)}, u32[]{:S(2)}) copy-start(f32[2,128,2304]{2,1,0:T(8,128)S(1)} %get-tuple-element.84.refs_7_) | copy-start | bytes 7077892
  115.5 21.3 %copy-start.21 = (bf16[2,2,128,256]{3,1,2,0:T(2,128)(2,1)S(1)}, bf16[2,2,128,256]{3,1,2,0:T(2,128)(2,1)}, u32[]{:S(2)}) copy-start(bf16[2,2,128,256]{3,1,2,0:T(2,128)(2,1)} %copy-done.20) | copy-start | bytes 786436
  136.7 21.4 %copy-start.7 = (bf16[2,128,2304]{2,1,0:T(8,128)(2,1)}, bf16[2,128,2304]{2,1,0:T(8,128)(2,1)S(1)}, u32[]{:S(2)}) copy-start(bf16[2,128,2304]{2,1,0:T(8,128)(2,1)S(1)} %get-tuple-element.57) | copy-start | bytes 3538948
  136.8 20.5 %copy-start.15 = (bf16[2,128,2304]{2,1,0:T(8,128)(2,1)S(1)}, bf16[2,128,2304]{2,1,0:T(8,128)(2,1)}, u32[]{:S(2)}) copy-start(bf16[2,128,2304]{2,1,0:T(8,128)(2,1)} %refs_9_.2) | copy-start | bytes 3538948
  136.8 20.5 %copy-start.28 = (f32[2304]{0:T(1024)S(1)}, f32[2304]{0:T(1024)}, u32[]{:S(2)}) copy-start(f32[2304]{0:T(1024)} %param.29) | copy-start | bytes 27652
  157.0 3.2 copy-start.11
  186.5 1.0 copy-start.8
  187.5 1.0 copy-start.9
  188.5 1.0 copy-start.10
  194.2 191.4 %copy-start.31 = (f32[2304]{0:T(1024)S(1)}, f32[2304]{0:T(1024)}, u32[]{:S(2)}) copy-start(f32[2304]{0:T(1024)} %param.26) | copy-start | bytes 27652
  504.5 5.5 %copy-start.25 = (f32[72,2304]{1,0:T(8,128)S(1)}, f32[72,2304]{1,0:T(8,128)}, u32[]{:S(2)}) copy-start(f32[72,2304]{1,0:T(8,128)} %get-tuple-element.74) | copy-start | bytes 1990660
  504.6 5.5 %copy-start.26 = (f32[72,2304]{1,0:T(8,128)S(1)}, f32[72,2304]{1,0:T(8,128)}, u32[]{:S(2)}) copy-start(f32[72,2304]{1,0:T(8,128)} %get-tuple-element.75) | copy-start | bytes 1990660
  504.6 6.7 %copy-start.27 = (f32[72,128]{1,0:T(8,128)S(1)}, f32[72,128]{1,0:T(8,128)}, u32[]{:S(2)}) copy-start(f32[72,128]{1,0:T(8,128)} %get-tuple-element.76) | copy-start | bytes 110596
  506.4 5.6 %copy-start.22 = (bf16[2,128,2304]{2,1,0:T(8,128)(2,1)S(1)}, bf16[2,128,2304]{2,1,0:T(8,128)(2,1)}, u32[]{:S(2)}) copy-start(bf16[2,128,2304]{2,1,0:T(8,128)(2,1)} %get-tuple-element.121) | copy-start | bytes 3538948

commit v3 on v2

v3 whole, which is shorter than its diff:
```python
import functools

import jax
import jax.numpy as jnp
from jax import lax
from jax.experimental import pallas as pl
from jax.experimental.pallas import tpu as pltpu
from jax.sharding import PartitionSpec as P

D = 2304
HEADS = 8
HD = 256
FF = 9216

CAP = 50.0
EPS = 1e-06
LEVEL_SCALE = 1.0 / 74.0
WIDTHS = (8, 4, 2)

MESH = pl.DeviceIdType.MESH
VMEM = pltpu.VMEM
BF = jnp.bfloat16
F32 = jnp.float32
SEQ = 4096
ROWS = 128
TAGROW = 256
MASKED = -2.0


def place_of():
    b = lax.axis_index("blk")
    t = lax.axis_index("tensor")
    return b % 4, (b // 4) % 4, b // 16, t // 2, t % 2


def device_at(x, y, z, zh, c):
    return ((z * 4 + y) * 4 + x, zh * 2 + c)


def greet(peers):
    barrier = pltpu.get_barrier_semaphore()
    for peer in peers:
        pl.semaphore_signal(barrier, inc=1, device_id=peer, device_id_type=MESH)
    pl.semaphore_wait(barrier, len(peers))


def send(src, dst, ssem, rsem, peer):
    copy = pltpu.make_async_remote_copy(
        src_ref=src, dst_ref=dst, send_sem=ssem, recv_sem=rsem, device_id=peer, device_id_type=MESH
    )
    copy.start()
    return copy


def params(collective_id=None, limit=60):
    if collective_id is None:
        return pltpu.CompilerParams(vmem_limit_bytes=limit << 20)
    return pltpu.CompilerParams(
        vmem_limit_bytes=limit << 20, collective_id=collective_id, has_side_effects=True
    )


def whole(space=VMEM):
    return pl.BlockSpec(memory_space=space)


CHUNK = 4
KEYS = CHUNK * ROWS


def nt(left, right):
    return lax.dot_general(left, right, (((1,), (1,)), ((), ())), preferred_element_type=F32)


def tn(left, right):
    return lax.dot_general(left, right, (((0,), (0,)), ((), ())), preferred_element_type=F32)


def nn(left, right):
    return jnp.dot(left, right, preferred_element_type=F32)


def load_chunk(ref, step):
    zi, k = step // 4, step % 4
    keys = ref[zi, k, :, :ROWS, :].reshape(KEYS, HD)
    values = ref[zi, k, :, ROWS : 2 * ROWS, :].reshape(KEYS, HD)
    tags = ref[zi, k, :, TAGROW : TAGROW + 16, :ROWS].astype(F32)
    tag_row = jnp.concatenate([tags[i, 0:1, :] for i in range(CHUNK)], axis=1)
    return keys, values, tag_row


def allowed(key_place, tag_row, query_tag, query_place):
    ok = (key_place <= query_place) & (tag_row == query_tag)
    return ok | (key_place == query_place)


def query_places():
    row = lax.broadcasted_iota(jnp.int32, (2 * ROWS, 1), 0)
    return lax.axis_index("blk") * ROWS + row % ROWS


def poster(ssem, rsem, copies):
    def post(src, dst, peer):
        k = len(copies)
        copies.append(send(src, dst, ssem.at[k], rsem.at[k], peer))
        return copies[k]

    return post


def loader(sem, copies):
    def load(src, dst):
        copy = pltpu.make_async_copy(src, dst, sem.at[len(copies)])
        copy.start()
        copies.append(copy)
        return copy

    return load


def arrive(copies):
    for copy in copies:
        copy.wait_recv()


def turn(values, cosine, sine):
    half = HD // 2
    first, second = values[:, :half], values[:, half:]
    return jnp.concatenate([first * cosine - second * sine, second * cosine + first * sine], axis=1)


def fill_turned(dst, value, m):
    turned = value.T
    for zi in range(2):
        for k in range(4):
            at = (zi * 4 + k) * 288
            dst[zi, k, :, m * ROWS : (m + 1) * ROWS] = turned[at : at + 288]


HALF = ROWS // 2
STEP_ROWS = 32


class Summed:
    def __init__(self, post, part, t1, th, t2, c, mate, far):
        self.post, self.part, self.t1, self.th, self.t2 = post, part, t1, th, t2
        self.c, self.mate, self.far = c, mate, far
        self.pieces = [pl.ds(k * STEP_ROWS, STEP_ROWS) for k in range(HALF // STEP_ROWS)]

    def rows(self, core, k):
        return pl.ds(pl.multiple_of(core * HALF + k * STEP_ROWS, STEP_ROWS), STEP_ROWS)

    def start(self, i):
        other = 1 - self.c
        return [
            self.post(self.part.at[i, self.rows(other, k)], self.t1.at[i, r], self.mate)
            for k, r in enumerate(self.pieces)
        ]

    def across(self, i, one):
        sent = []
        for k, r in enumerate(self.pieces):
            one[k].wait_recv()
            own = self.part[i, self.rows(self.c, k)].astype(F32)
            self.th[i, r] = (own + self.t1[i, r].astype(F32)).astype(BF)
            sent.append(self.post(self.th.at[i, r], self.t2.at[i, r], self.far))
        return sent

    def back(self, i, two, dst, m):
        sent = []
        for k, r in enumerate(self.pieces):
            two[k].wait_recv()
            rows = self.rows(self.c, k)
            dst[m, rows] = (self.th[i, r].astype(F32) + self.t2[i, r].astype(F32)).astype(BF)
            sent.append(self.post(dst.at[m, rows], dst.at[m, rows], self.mate))
        return sent


CUT = 144


def front_kernel(
    gain_in, gain_out, gain_ffn, cos_ref, sin_ref, tags, tag_ref,
    tok_in, wq_in, wk_in, wv_in, wo_in,
    middle, branch, ffn_in, q_ref, att, lse_ref, ft, all_a, all_b, dn_land, ca_land,
    tok, wq, wk, wv, wo, normed, dn, flat, ga, gb, acc, mass, part, t1, th, t2,
    lsem, ssem, rsem,
    scale_in, scale_mid,
):
    x, y, z, zh, c = place_of()
    block = lax.axis_index("blk")
    xi = [(x + j) % 4 for j in (1, 2, 3)]
    yi = [(y + j) % 4 for j in (1, 2, 3)]
    xs = [device_at(i, y, z, zh, c) for i in xi]
    ys = [device_at(x, i, z, zh, c) for i in yi]
    zp = device_at(x, y, 1 - z, zh, c)
    mate = device_at(x, y, z, zh, 1 - c)
    far = device_at(x, y, z, 1 - zh, c)
    copies, local = [], []
    post = poster(ssem, rsem, copies)
    load = loader(lsem, local)
    loads = [
        load(*pair)
        for pair in ((tok_in, tok), (wk_in, wk), (wv_in, wv), (wq_in, wq), (wo_in, wo))
    ]
    greet(xs + ys + [zp, mate, far])

    loads[0].wait()
    for m in range(2):

        def slab(i, carry):
            r = pl.ds(pl.multiple_of(i * 16, 16), 16)
            v = tok[m, r].astype(F32)
            q = lax.rsqrt(jnp.mean(v * v, axis=-1, keepdims=True) + EPS)
            normed[m, r] = (v * q * gain_in[...]).astype(BF)
            return carry

        lax.fori_loop(0, ROWS // 16, slab, 0)
    loads[1].wait()
    loads[2].wait()
    cosine, sine = cos_ref[...], sin_ref[...]
    for m, held in ((0, ga), (1, gb)):
        a, b = wk[...], wv[...]
        if m == 1:
            a, b = narrow(a), narrow(b)
        held[z, y, x, :ROWS] = turn(nn(normed[m], a) * scale_in, cosine, sine).astype(BF)
        held[z, y, x, ROWS : 2 * ROWS] = (nn(normed[m], b) * scale_in).astype(BF)
        held[z, y, x, TAGROW:] = tags[m]

    levels = (z, 1 - z)

    def at_a(level, along_x, along_y, part=None):
        ref = ga.at[level, along_y, along_x]
        return ref if part is None else ref.at[part]

    def at_b(level, along_y, along_x, part=None):
        ref = gb.at[level, along_y, along_x]
        return ref if part is None else ref.at[part]

    first_half, last_half = pl.ds(0, CUT), pl.ds(CUT, TAGROW + 16 - CUT)
    sides = (
        (at_a, x, xi, xs, y, yi, ys),
        (at_b, y, yi, ys, x, xi, xs),
    )

    def line(side, level, second, pair=None):
        if side == 0:
            return ga.at[level, second] if pair is None else ga.at[level, second, pair]
        return gb.at[level, :, second] if pair is None else gb.at[level, pair, second]

    across = []
    for at, one, places, devices, two, _, _ in sides:
        own = at(z, one, two)
        across.append(post(own, own, zp))
    near = {}

    def send_near(side, k):
        at, one, places, devices, two, _, _ = sides[side]
        own = at(levels[k], one, two)
        near[side, k] = [post(own, own, devices[j]) for j in (0, 2)]

    relays = {}

    def relay_near(side, k):
        at, one, places, devices, two, _, _ = sides[side]
        sent = near[side, k]
        sent[0].wait_recv()
        piece = at(levels[k], places[2], two, first_half)
        relays[side, k] = [post(piece, piece, devices[0])]
        sent[1].wait_recv()
        piece = at(levels[k], places[0], two, last_half)
        relays[side, k].append(post(piece, piece, devices[2]))

    lines = {}

    def send_line(side, k):
        _, _, _, _, two, _, devices = sides[side]
        arrive(relays[side, k])
        own = line(side, levels[k], two)
        lines[side, k] = [post(own, own, devices[j]) for j in (0, 2)]

    passed = {}

    def relay_line(side, k):
        _, _, _, _, _, places, devices = sides[side]
        sent = lines[side, k]
        sent[0].wait_recv()
        piece = line(side, levels[k], places[2], pl.ds(0, 2))
        passed[side, k] = [post(piece, piece, devices[0])]
        sent[1].wait_recv()
        piece = line(side, levels[k], places[0], pl.ds(2, 2))
        passed[side, k].append(post(piece, piece, devices[2]))

    both = (0, 1)
    for side in both:
        send_near(side, 0)
    loads[3].wait()
    for m in range(2):
        a = wq[...] if m == 0 else narrow(wq[...])
        wide = nn(normed[m], a) * scale_in
        for h in range(2):
            turned = turn(wide[:, h * HD : (h + 1) * HD], cosine, sine)
            q_ref[m, h * ROWS : (h + 1) * ROWS] = turned.astype(BF)
        fill_turned(dn, normed[m], m)
    arrive(across)
    for side in both:
        send_near(side, 1)
    for k in both:
        for side in both:
            relay_near(side, k)

    acc[...] = jnp.zeros_like(acc)
    mass[...] = jnp.zeros_like(mass)
    where = query_places()
    lane = lax.broadcasted_iota(jnp.int32, (2 * ROWS, KEYS), 1)

    def attend(side, k, second):
        level = levels[k]
        if side == 0:
            held, begin, key_place = ga.at[level, second], level * 16 + second * 4, lane
            stride = 1
        else:
            held, begin, key_place = gb.at[level, :, second], level * 16 + second, lane % ROWS + lane // ROWS * (4 * ROWS)
            stride = 4

        @pl.when(begin <= block)
        def _():
            keys = held[:, :ROWS, :].reshape(KEYS, HD)
            values = held[:, ROWS : 2 * ROWS, :].reshape(KEYS, HD)
            tag = held[:, TAGROW : TAGROW + 16, :ROWS].astype(F32)
            tag_row = jnp.concatenate([tag[i, 0:1, :] for i in range(CHUNK)], axis=1)
            bent = jnp.tanh(nt(q_ref[side], keys) * (HD ** (-0.5) / CAP))
            ok = allowed(key_place + begin * ROWS, tag_row, tag_ref[side], where)
            e = jnp.where(ok, jnp.exp(CAP * bent), 0.0)
            mass[side] += jnp.sum(e, axis=-1, keepdims=True)
            acc[side] += nn(e.astype(BF), values)

    for k in both:
        for side in both:
            send_line(side, k)
    for k in both:
        for side in both:
            attend(side, k, sides[side][4])
    for k in both:
        for side in both:
            relay_line(side, k)
    for k in both:
        for side in both:
            attend(side, k, sides[side][5][0])
            attend(side, k, sides[side][5][2])
    for side in both:
        for k in both:
            arrive(passed[side, k])
            attend(side, k, sides[side][5][1])
    load(ga, all_a)
    load(gb, all_b)

    band_y = pl.ds(pl.multiple_of(y * 256, 256), 256)
    sums = Summed(post, part, t1, th, t2, c, mate, far)
    carried = []
    loads[4].wait()

    def project(m):
        out = acc[m] / mass[m]
        att[m] = out
        lse_ref[m] = jnp.log(mass[m])
        low = out.astype(BF)
        flat[m] = jnp.concatenate([low[:ROWS], low[ROWS:]], axis=1)
        a = wo[...] if m == 0 else narrow(wo[...])
        part[m] = (nn(flat[m], a) * scale_mid).astype(BF)

    def spread(m):
        rows = pl.ds(pl.multiple_of(y * 256, 256) + m * ROWS, ROWS)
        load(flat.at[m], ca_land.at[rows])
        return [post(flat.at[m], ca_land.at[rows], ys[j]) for j in range(3)]

    def norms(m):
        def slab(i, carry):
            r = pl.ds(pl.multiple_of(i * 16, 16), 16)
            v = branch[m, r].astype(F32)
            q = lax.rsqrt(jnp.mean(v * v, axis=-1, keepdims=True) + EPS)
            mid = tok[m, r].astype(F32) + v * q * gain_out[...]
            middle[m, r] = mid
            q = lax.rsqrt(jnp.mean(mid * mid, axis=-1, keepdims=True) + EPS)
            ffn_in[m, r] = (mid * q * gain_ffn[...]).astype(BF)
            return carry

        lax.fori_loop(0, ROWS // 16, slab, 0)
        fill_turned(ft, ffn_in[m], m)

    project(0)
    one = sums.start(0)
    carried += [post(dn.at[:, yi[j]], dn_land.at[:, :, band_y], ys[j]) for j in range(3)]
    load(dn.at[:, y], dn_land.at[:, :, band_y])
    two0 = sums.across(0, one)
    project(1)
    one = sums.start(1)
    two1 = sums.across(1, one)
    carried += spread(0)
    carried += spread(1)
    three = sums.back(0, two0, branch, 0)
    arrive(three)
    norms(0)
    three = sums.back(1, two1, branch, 1)
    arrive(three)
    norms(1)
    arrive(carried)
    for copy in local[5:]:
        copy.wait()
    for copy in copies:
        copy.wait_send()


def front(gain_in, gain_out, gain_ffn, cosine, sine, tags, tag, tok, wq, wk, wv, wo, scale_in, scale_mid):
    def kernel(*refs):
        front_kernel(*refs, scale_in, scale_mid)

    any_ = whole(pl.ANY)
    both = (2, ROWS, D)
    heads = (2, 2 * ROWS, HD)
    kv = (2, 4, 4, TAGROW + 16, HD)
    turned = (2, 4, 288, 2 * ROWS)
    sems = 34 + 2 * 3 * (HALF // STEP_ROWS) + 9
    return pl.pallas_call(
        kernel,
        out_shape=[
            jax.ShapeDtypeStruct(both, F32),
            jax.ShapeDtypeStruct(both, BF),
            jax.ShapeDtypeStruct(both, BF),
            jax.ShapeDtypeStruct(heads, BF),
            jax.ShapeDtypeStruct(heads, F32),
            jax.ShapeDtypeStruct((2, 2 * ROWS, 1), F32),
            jax.ShapeDtypeStruct(turned, BF),
            jax.ShapeDtypeStruct(kv, BF),
            jax.ShapeDtypeStruct(kv, BF),
            jax.ShapeDtypeStruct((2, 288, 1024), BF),
            jax.ShapeDtypeStruct((1024, 2 * HD), BF),
        ],
        in_specs=[whole()] * 7 + [any_] * 5,
        out_specs=[whole()] * 7 + [any_] * 4,
        scratch_shapes=[
            VMEM(both, BF),
            VMEM(wq.shape, BF),
            VMEM(wk.shape, BF),
            VMEM(wv.shape, BF),
            VMEM(wo.shape, BF),
            VMEM(both, BF),
            VMEM(turned, BF),
            VMEM((2, ROWS, 2 * HD), BF),
            VMEM(kv, BF),
            VMEM(kv, BF),
            VMEM(heads, F32),
            VMEM((2, 2 * ROWS, 1), F32),
            VMEM(both, BF),
            VMEM((2, HALF, D), BF),
            VMEM((2, HALF, D), BF),
            VMEM((2, HALF, D), BF),
            pltpu.SemaphoreType.DMA((10,)),
            pltpu.SemaphoreType.DMA((sems,)),
            pltpu.SemaphoreType.DMA((sems,)),
        ],
        compiler_params=params(1, 60),
    )(gain_in, gain_out, gain_ffn, cosine, sine, tags, tag, tok, wq, wk, wv, wo)


FTILE = 256
ROOT = (2.0 / 3.141592653589793) ** 0.5
CUBE = 0.044715


def narrow(codes):
    level = codes * BF(1.0 / 16.0) + BF(1.0 / 32.0)
    level = (level + BF(192.0)) - BF(192.0)
    return jnp.minimum(level, BF(7.0)) * BF(16.0)


def ffn_kernel(
    x_ref, gain_ref, wg_in, wu_in, wd_in, middle_in, up_in, dg_own,
    out_ref, dgate_ref, dup_ref, total_ref, gains, ch, dd_land, dg_land,
    wg, wu, wd, middle, upstream, gate_s, up_s, hid, acc, part, low, dd,
    t1, th, t2, down_sum,
    wsem, lsem, ssem, rsem,
    scale_in, scale_out,
):
    x, y, z, zh, c = place_of()
    xi = [(x + j) % 4 for j in (1, 2, 3)]
    yi = [(y + j) % 4 for j in (1, 2, 3)]
    xs = [device_at(i, y, z, zh, c) for i in xi]
    ys = [device_at(x, i, z, zh, c) for i in yi]
    mate = device_at(x, y, z, zh, 1 - c)
    far = device_at(x, y, z, 1 - zh, c)
    tiles = wg.shape[1] // FTILE
    copies, local = [], []
    post = poster(ssem, rsem, copies)

    def load(src, dst):
        copy = pltpu.make_async_copy(src, dst, lsem.at[len(local)])
        copy.start()
        local.append(copy)
        return copy

    def weight_copies(t):
        span = pl.ds(pl.multiple_of(t * FTILE, FTILE), FTILE)
        return (
            pltpu.make_async_copy(wg_in.at[:, span], wg.at[:, span], wsem.at[0, t]),
            pltpu.make_async_copy(wu_in.at[:, span], wu.at[:, span], wsem.at[1, t]),
            pltpu.make_async_copy(wd_in.at[span], wd.at[span], wsem.at[2, t]),
        )

    def start_weights(t, carry):
        for copy in weight_copies(t):
            copy.start()
        return carry

    lax.fori_loop(0, tiles, start_weights, 0)
    loads = [load(middle_in, middle), load(up_in, upstream)]
    greet(xs + ys + [mate, far])
    band_x = pl.ds(pl.multiple_of(x * 256, 256), 256)
    band_y = pl.ds(pl.multiple_of(y * 256, 256), 256)
    carried = [post(dg_own.at[xi[j]], dg_land.at[:, band_x], xs[j]) for j in range(3)]
    load(dg_own.at[x], dg_land.at[:, band_x])

    def forward(m, first, last, wait=False):
        def body(t, carry):
            span = pl.ds(pl.multiple_of(t * FTILE, FTILE), FTILE)
            if wait:
                for copy in weight_copies(t):
                    copy.wait()
            a, b, d = wg[:, span], wu[:, span], wd[span]
            if m == 1:
                a, b, d = narrow(a), narrow(b), narrow(d)
            gate = nn(x_ref[m], a) * scale_in
            up = nn(x_ref[m], b) * scale_in
            gate_s[m, :, span] = gate
            up_s[m, :, span] = up
            bent = jnp.tanh(ROOT * (gate + CUBE * gate * gate * gate))
            hidden = (0.5 * gate * (1.0 + bent) * up).astype(BF)
            hid[m, :, span] = hidden
            acc[...] += nn(hidden, d)
            return carry

        lax.fori_loop(first, last, body, 0)

    def backward(m, first, last):
        def body(t, carry):
            span = pl.ds(pl.multiple_of(t * FTILE, FTILE), FTILE)
            a, b, d = wg[:, span], wu[:, span], wd[span]
            if m == 1:
                a, b, d = narrow(a), narrow(b), narrow(d)
            grad = nt(low[m], d) * scale_out
            v, u = gate_s[m, :, span], up_s[m, :, span]
            bent = jnp.tanh(ROOT * (v + CUBE * v * v * v))
            half = 0.5 * (1.0 + bent)
            slope = half + 0.5 * v * (1.0 - bent * bent) * (ROOT * (1.0 + 3.0 * CUBE * v * v))
            dgate = (grad * u * slope).astype(BF)
            dup = (grad * (v * half)).astype(BF)
            dgate_ref[m, :, span] = dgate
            dup_ref[m, :, span] = dup
            acc[...] += nt(dgate, a) + nt(dup, b)
            return carry

        lax.fori_loop(first, last, body, 0)

    pieces = [pl.ds(k * STEP_ROWS, STEP_ROWS) for k in range(HALF // STEP_ROWS)]

    def at_rows(core, k):
        return pl.ds(pl.multiple_of(core * HALF + k * STEP_ROWS, STEP_ROWS), STEP_ROWS)

    def sum_start(i, m):
        return [post(part.at[i, at_rows(1 - c, k)], t1.at[i, r], mate) for k, r in enumerate(pieces)]

    def sum_across(i, one):
        sent = []
        for k, r in enumerate(pieces):
            one[k].wait_recv()
            th[i, r] = (part[i, at_rows(c, k)].astype(F32) + t1[i, r].astype(F32)).astype(BF)
            sent.append(post(th.at[i, r], t2.at[i, r], far))
        return sent

    def sum_back(i, two, dst, m):
        sent = []
        for k, r in enumerate(pieces):
            two[k].wait_recv()
            dst[m, at_rows(c, k)] = (th[i, r].astype(F32) + t2[i, r].astype(F32)).astype(BF)
            sent.append(post(dst.at[m, at_rows(c, k)], dst.at[m, at_rows(c, k)], mate))
        return sent

    def arrive(sent):
        for copy in sent:
            copy.wait_recv()

    def spread_hidden(m):
        rows = pl.ds(pl.multiple_of(y * 256, 256) + m * ROWS, ROWS)
        load(hid.at[m], ch.at[rows])
        return [post(hid.at[m], ch.at[rows], ys[j]) for j in (0, 2)]

    def relay_hidden(m, sent):
        for j, copy in zip((0, 2), sent):
            copy.wait_recv()
            source = yi[2] if j == 0 else yi[0]
            begin = pl.multiple_of(source * 256, 256) + m * ROWS + (0 if j == 0 else HALF)
            rows = pl.ds(begin, HALF)
            carried.append(post(ch.at[rows], ch.at[rows], ys[j]))

    def norm(m, sums):
        def slab(i, carry):
            r = pl.ds(pl.multiple_of(i * 16, 16), 16)
            v = down_sum[m, r].astype(F32)
            du = upstream[m, r].astype(F32)
            q = lax.rsqrt(jnp.mean(v * v, axis=-1, keepdims=True) + EPS)
            gain = gain_ref[...]
            out_ref[m, r] = (middle[m, r] + v * q * gain).astype(BF)
            lifted = du * gain
            back = q * lifted - v * (q * q * q * jnp.mean(lifted * v, axis=-1, keepdims=True))
            low[m, r] = back.astype(BF)
            return carry + jnp.sum(du * v * q, axis=0, keepdims=True)

        return lax.fori_loop(0, ROWS // 16, slab, sums)

    def turn_down(m):
        turned = low[m].T
        for zi in range(2):
            for k in range(4):
                at = (zi * 4 + k) * 288
                dd[zi, k, :, m * ROWS : (m + 1) * ROWS] = turned[at : at + 288]

    acc[...] = jnp.zeros_like(acc)
    forward(0, 0, tiles, True)
    part[0] = (acc[...] * scale_out).astype(BF)
    one = sum_start(0, 0)
    hidden0 = spread_hidden(0)
    acc[...] = jnp.zeros_like(acc)
    forward(1, 0, 2)
    two = sum_across(0, one)
    forward(1, 2, tiles)
    part[1] = (acc[...] * scale_out).astype(BF)
    one = sum_start(1, 1)
    hidden1 = spread_hidden(1)
    three = sum_back(0, two, down_sum, 0)
    two = sum_across(1, one)
    arrive(three)
    for copy in loads:
        copy.wait()
    sums = norm(0, jnp.zeros((1, D), F32))
    relay_hidden(0, hidden0)
    acc[...] = jnp.zeros_like(acc)
    backward(0, 0, tiles)
    part[2] = (acc[...] * scale_in).astype(BF)
    one = sum_start(2, 0)
    three = sum_back(1, two, down_sum, 1)
    two = sum_across(2, one)
    arrive(three)
    gains[...] = norm(1, sums)
    relay_hidden(1, hidden1)
    turn_down(0)
    turn_down(1)
    carried += [post(dd.at[:, yi[j]], dd_land.at[:, :, band_y], ys[j]) for j in range(3)]
    load(dd.at[:, y], dd_land.at[:, :, band_y])
    acc[...] = jnp.zeros_like(acc)
    backward(1, 0, tiles)
    part[3] = (acc[...] * scale_in).astype(BF)
    one = sum_start(3, 1)
    three = sum_back(2, two, total_ref, 0)
    two = sum_across(3, one)
    arrive(three)
    three = sum_back(3, two, total_ref, 1)
    arrive(three)
    arrive(carried)
    for copy in local[2:]:
        copy.wait()
    for copy in copies:
        copy.wait_send()


def ffn(x, gain, wg, wu, wd, middle, up, dg, scale_in, scale_out):
    def kernel(*refs):
        ffn_kernel(*refs, scale_in, scale_out)

    any_ = whole(pl.ANY)
    both = (2, ROWS, D)
    tiles = wg.shape[1] // FTILE
    sems = 3 + 4 * 3 * (HALF // STEP_ROWS) + 8 + 3
    return pl.pallas_call(
        kernel,
        out_shape=[
            jax.ShapeDtypeStruct(both, BF),
            jax.ShapeDtypeStruct(both, BF),
            jax.ShapeDtypeStruct(both, BF),
            jax.ShapeDtypeStruct(both, BF),
            jax.ShapeDtypeStruct((1, D), F32),
            jax.ShapeDtypeStruct((1024, D), BF),
            jax.ShapeDtypeStruct((2, 288, 1024), BF),
            jax.ShapeDtypeStruct((PART, 1024), BF),
        ],
        in_specs=[whole()] * 2 + [any_] * 6,
        out_specs=[whole()] * 5 + [any_] * 3,
        scratch_shapes=[
            VMEM(wg.shape, BF),
            VMEM(wu.shape, BF),
            VMEM(wd.shape, BF),
            VMEM(both, F32),
            VMEM(both, BF),
            VMEM(both, F32),
            VMEM(both, F32),
            VMEM(both, BF),
            VMEM((ROWS, D), F32),
            VMEM((4, ROWS, D), BF),
            VMEM(both, BF),
            VMEM((2, 4, 288, 2 * ROWS), BF),
            VMEM((4, HALF, D), BF),
            VMEM((4, HALF, D), BF),
            VMEM((4, HALF, D), BF),
            VMEM(both, BF),
            pltpu.SemaphoreType.DMA((3, tiles)),
            pltpu.SemaphoreType.DMA((6,)),
            pltpu.SemaphoreType.DMA((sems,)),
            pltpu.SemaphoreType.DMA((sems,)),
        ],
        compiler_params=params(5, 63),
    )(x, gain, wg, wu, wd, middle, up, dg)


PART = 576
SHARE = 72


PIECES = 4


def total_start(post, p_ref, r1, rows, c, mate):
    return [post(p_ref.at[1 - c, r], r1.at[r], mate) for r in rows]


def total_across(post, p_ref, r1, h, r2, rows, c, far, one):
    two = []
    for k, r in enumerate(rows):
        one[k].wait_recv()
        h[r] = (p_ref[c, r].astype(F32) + r1[r].astype(F32)).astype(BF)
        two.append(post(h.at[r], r2.at[r], far))
    return two


def total_end(post, o_ref, h, r2, rows, c, mate, two):
    three = []
    for k, r in enumerate(rows):
        two[k].wait_recv()
        o_ref[c, r] = (h[r].astype(F32) + r2[r].astype(F32)).astype(BF)
        three.append(post(o_ref.at[c, r], o_ref.at[c, r], mate))
    for copy in three:
        copy.wait_recv()


def piece_rows():
    size = ROWS // PIECES
    return [pl.ds(k * size, size) for k in range(PIECES)]


def norm_grad(v, gain, grad):
    q = lax.rsqrt(jnp.mean(v * v, axis=-1, keepdims=True) + EPS)
    lifted = grad * gain
    back = q * lifted - v * (q * q * q * jnp.mean(lifted * v, axis=-1, keepdims=True))
    return back, jnp.sum(grad * v * q, axis=0, keepdims=True)


def mid_kernel(
    total_ref, gain_mid, gain_out, q_ref, lse_ref, tag_ref, att_ref,
    middle_in, branch_in, up_in, wo_in, k_in, v_in, cg_own, cu_own, du,
    key_out, value_out, dq_ref, mgrad, bt, gains, cg, cu, du_land,
    middle, branch, upstream, wo, k_ref, v_ref, blow, g_ref, dk, dv,
    r1a, r1b, s1a, s1b, r2a, r2b, s2a, s2b, r3a, r3b,
    lsem, ssem, rsem,
    scale,
):
    x, y, z, zh, c = place_of()
    xi = [(x + j) % 4 for j in (1, 2, 3)]
    yi = [(y + j) % 4 for j in (1, 2, 3)]
    xs = [device_at(i, y, z, zh, c) for i in xi]
    ys = [device_at(x, i, z, zh, c) for i in yi]
    zp = device_at(x, y, 1 - z, zh, c)
    copies, local = [], []
    post = poster(ssem, rsem, copies)

    def load(src, dst):
        copy = pltpu.make_async_copy(src, dst, lsem.at[len(local)])
        copy.start()
        local.append(copy)
        return copy

    loads = [
        load(*pair)
        for pair in (
            (middle_in, middle), (branch_in, branch), (up_in, upstream), (wo_in, wo), (k_in, k_ref), (v_in, v_ref),
        )
    ]
    greet(xs + ys + [zp])
    band_x = pl.ds(pl.multiple_of(x * 256, 256), 256)
    band_y = pl.ds(pl.multiple_of(y * 256, 256), 256)
    gate_sent = [post(cg_own, cg.at[band_x], xs[j]) for j in (0, 2)]
    up_sent = [post(cu_own, cu.at[band_y], ys[j]) for j in (0, 2)]
    carried = [post(du.at[:, yi[j]], du_land.at[:, :, band_y], ys[j]) for j in range(3)]
    for pair in (
        (du.at[:, y], du_land.at[:, :, band_y]), (cg_own, cg.at[band_x]), (cu_own, cu.at[band_y]),
    ):
        load(*pair)
    for copy in loads[:4]:
        copy.wait()

    zero = jnp.zeros((1, D), F32)
    for m in range(2):

        def slab(i, carry):
            sum_mid, sum_out = carry
            r = pl.ds(pl.multiple_of(i * 16, 16), 16)
            back, more = norm_grad(middle[m, r], gain_mid[...], total_ref[m, r].astype(F32))
            grad = upstream[m, r].astype(F32) + back
            mgrad[m, r] = grad
            back, most = norm_grad(branch[m, r].astype(F32), gain_out[...], grad)
            blow[m, r] = back.astype(BF)
            return sum_mid + more, sum_out + most

        sums = lax.fori_loop(0, ROWS // 16, slab, (zero, zero) if m == 0 else sums)
    gains[0:1] = sums[1]
    gains[1:2] = sums[0]
    for m in range(2):
        weight = wo[...] if m == 0 else narrow(wo[...])
        wide = (nt(blow[m], weight) * scale).astype(BF)
        g_ref[m, :ROWS] = wide[:, :HD]
        g_ref[m, ROWS:] = wide[:, HD:]
        turned = blow[m].T
        for zi in range(2):
            for k in range(4):
                at = (zi * 4 + k) * 288
                bt[zi, k, :, m * ROWS : (m + 1) * ROWS] = turned[at : at + 288]

    for j, k in ((0, 0), (2, 1)):
        for sent, land, places, devices in ((gate_sent, cg, xi, xs), (up_sent, cu, yi, ys)):
            sent[k].wait_recv()
            begin = pl.multiple_of(places[2 - j] * 256, 256) + k * ROWS
            relayed = pl.ds(begin, ROWS)
            carried.append(post(land.at[relayed], land.at[relayed], devices[j]))

    loads[4].wait()
    loads[5].wait()
    limit = lax.axis_index("blk") // CHUNK + 1
    where = query_places()
    lane = lax.broadcasted_iota(jnp.int32, (2 * ROWS, KEYS), 1)
    for m in range(2):
        q = q_ref[m]
        g = g_ref[m]
        tag = tag_ref[m]
        lse = lse_ref[m]
        off = jnp.sum(g.astype(F32) * att_ref[m], axis=-1, keepdims=True)
        span = slice(m * ROWS, (m + 1) * ROWS)

        def step(i, dq):
            keys, values, tag_row = load_chunk(k_ref if m == 0 else v_ref, i)
            bent = jnp.tanh(nt(q, keys) * (HD ** (-0.5) / CAP))
            ok = allowed(i * KEYS + lane, tag_row, tag, where)
            p = jnp.where(ok, jnp.exp(CAP * bent - lse), 0.0)
            dp = nt(g, values)
            ds = (p * (dp - off) * (1.0 - bent * bent) * HD ** (-0.5)).astype(BF)
            dk[i // 4, i % 4, :, span, :] = tn(ds, q).astype(BF).reshape(CHUNK, ROWS, HD)
            dv[i // 4, i % 4, :, span, :] = tn(p.astype(BF), g).astype(BF).reshape(CHUNK, ROWS, HD)
            return dq + nn(ds, keys)

        dq_ref[m] = lax.fori_loop(0, limit, step, jnp.zeros((2 * ROWS, HD), F32))

        def blank(i, carry):
            dk[i // 4, i % 4, :, span, :] = jnp.zeros((CHUNK, ROWS, HD), BF)
            dv[i // 4, i % 4, :, span, :] = jnp.zeros((CHUNK, ROWS, HD), BF)
            return carry

        lax.fori_loop(limit, SEQ // KEYS, blank, 0)

    one_a = [post(dk.at[:, :, xi[j]], r1a.at[j], xs[j]) for j in range(3)]
    one_b = [post(dv.at[:, yi[j]], r1b.at[j], ys[j]) for j in range(3)]
    for copy in one_a:
        copy.wait_recv()

    def add_a(i, carry):
        zi, k = i // 4, i % 4
        out = dk[zi, k, x].astype(F32)
        for j in range(3):
            out = out + r1a[j, zi, k].astype(F32)
        s1a[zi, k] = out.astype(BF)
        return carry

    lax.fori_loop(0, 8, add_a, 0)
    two_a = [post(s1a.at[:, yi[j]], r2a.at[j], ys[j]) for j in range(3)]
    for copy in one_b:
        copy.wait_recv()

    def add_b(i, carry):
        zi, k = i // 4, i % 4
        out = dv[zi, y, k].astype(F32)
        for j in range(3):
            out = out + r1b[j, zi, k].astype(F32)
        s1b[zi, k] = out.astype(BF)
        return carry

    lax.fori_loop(0, 8, add_b, 0)
    two_b = [post(s1b.at[:, xi[j]], r2b.at[j], xs[j]) for j in range(3)]

    def second(arrivals, own, mine, land, half):
        for copy in arrivals:
            copy.wait_recv()
        for zi in range(2):
            out = own[zi, mine].astype(F32)
            for j in range(3):
                out = out + land[j, zi].astype(F32)
            half[zi] = out.astype(BF)

    second(two_a, s1a, y, r2a, s2a)
    three_a = post(s2a.at[1 - z], r3a, zp)
    second(two_b, s1b, x, r2b, s2b)
    three_b = post(s2b.at[1 - z], r3b, zp)
    three_a.wait_recv()
    key_out[...] = s2a[z].astype(F32) + r3a[...].astype(F32)
    three_b.wait_recv()
    value_out[...] = s2b[z].astype(F32) + r3b[...].astype(F32)
    for copy in carried:
        copy.wait_recv()
    for copy in local[6:]:
        copy.wait()
    for copy in copies:
        copy.wait_send()


def mid(total_in, gain_mid, gain_out, q, lse, tag, att, middle, branch, up, wo, k, v, cg, cu, du, scale):
    def kernel(*refs):
        mid_kernel(*refs, scale)

    any_ = whole(pl.ANY)
    tile = (2 * ROWS, HD)
    wide = (4 * 2 * ROWS, D)
    sems = 4 + 3 + 4 + 6 + 6 + 2
    return pl.pallas_call(
        kernel,
        out_shape=[
            jax.ShapeDtypeStruct(tile, F32),
            jax.ShapeDtypeStruct(tile, F32),
            jax.ShapeDtypeStruct((2,) + tile, F32),
            jax.ShapeDtypeStruct((2, ROWS, D), F32),
            jax.ShapeDtypeStruct((2, 4, 288, 2 * ROWS), BF),
            jax.ShapeDtypeStruct((2, D), F32),
            jax.ShapeDtypeStruct(wide, BF),
            jax.ShapeDtypeStruct(wide, BF),
            jax.ShapeDtypeStruct((2, 288, 1024), BF),
        ],
        in_specs=[whole()] * 7 + [any_] * 9,
        out_specs=[whole()] * 6 + [any_] * 3,
        scratch_shapes=[
            VMEM(middle.shape, F32),
            VMEM(branch.shape, BF),
            VMEM(up.shape, BF),
            VMEM(wo.shape, BF),
            VMEM(k.shape, BF),
            VMEM(v.shape, BF),
            VMEM((2, ROWS, D), BF),
            VMEM((2,) + tile, BF),
            VMEM((2, 4, 4) + tile, BF),
            VMEM((2, 4, 4) + tile, BF),
            VMEM((3, 2, 4) + tile, BF),
            VMEM((3, 2, 4) + tile, BF),
            VMEM((2, 4) + tile, BF),
            VMEM((2, 4) + tile, BF),
            VMEM((3, 2) + tile, BF),
            VMEM((3, 2) + tile, BF),
            VMEM((2,) + tile, BF),
            VMEM((2,) + tile, BF),
            VMEM(tile, BF),
            VMEM(tile, BF),
            pltpu.SemaphoreType.DMA((9,)),
            pltpu.SemaphoreType.DMA((sems,)),
            pltpu.SemaphoreType.DMA((sems,)),
        ],
        compiler_params=params(2, 62),
    )(total_in, gain_mid, gain_out, q, lse, tag, att, middle, branch, up, wo, k, v, cg, cu, du)


def end_kernel(
    key_ref, value_ref, dq_ref, cos_ref, sin_ref, gain_in, gains_in,
    bt, wq_in, wk_in, wv_in, tok_in, mgrad_in, dg_in, cg_in, du_in, cu_in, dd_in, ch_in, dn_in, ca_in,
    igrad, og, ou, od, oq, on,
    wq, wk, wv, tok, mgrad, dg, c0, dd, c1, dn, ca, db, cq,
    part, t1, th, t2, total_ref, gpad, gb, rgb,
    pg, pu, pd, pq, pn, rg, ru, rd, rq, rn, sg, su, sd, sq, sn, zg, zu, zd, zq, zn,
    lsem, ssem, rsem,
    scale,
):
    x, y, z, zh, c = place_of()
    xi = [(x + j) % 4 for j in (1, 2, 3)]
    yi = [(y + j) % 4 for j in (1, 2, 3)]
    xs = [device_at(i, y, z, zh, c) for i in xi]
    ys = [device_at(x, i, z, zh, c) for i in yi]
    zp = device_at(x, y, 1 - z, zh, c)
    mate = device_at(x, y, z, zh, 1 - c)
    far = device_at(x, y, z, 1 - zh, c)
    copies, local = [], []
    post = poster(ssem, rsem, copies)

    def load(src, dst):
        copy = pltpu.make_async_copy(src, dst, lsem.at[len(local)])
        copy.start()
        local.append(copy)
        return copy

    band_y = pl.ds(pl.multiple_of(y * 256, 256), 256)
    weights = [load(*pair) for pair in ((wq_in, wq), (wk_in, wk), (wv_in, wv))]
    got_g = [load(dg_in, dg), load(cg_in, c0)]
    got_u = [load(du_in, dd), load(cu_in, c1)]
    got_t = [load(tok_in, tok), load(mgrad_in, mgrad)]
    got_q = [load(dn_in, dn), load(ca_in, ca), load(bt.at[:, y], db.at[:, :, band_y])]
    greet(xs + ys + [zp, mate, far])
    got_q_far = [post(bt.at[:, yi[j]], db.at[:, :, band_y], ys[j]) for j in range(3)]

    for m in range(2):
        r = slice(m * ROWS, (m + 1) * ROWS)
        own = pl.ds(pl.multiple_of(y * 256, 256) + m * ROWS, ROWS)
        cosine, sine = cos_ref[...], -sin_ref[...]
        for h in range(2):
            turned = turn(dq_ref[m, h * ROWS : (h + 1) * ROWS], cosine, sine)
            cq[own, h * HD : (h + 1) * HD] = turned.astype(BF)
        cq[own, 2 * HD : 3 * HD] = turn(key_ref[r], cosine, sine).astype(BF)
        cq[own, 3 * HD :] = value_ref[r].astype(BF)
    got_q_far += [post(cq.at[band_y], cq.at[band_y], ys[j]) for j in range(3)]
    for copy in weights:
        copy.wait()
    for m in range(2):
        own = pl.ds(pl.multiple_of(y * 256, 256) + m * ROWS, ROWS)
        a, b, v = wq[...], wk[...], wv[...]
        if m == 1:
            a, b, v = narrow(a), narrow(b), narrow(v)
        out = nt(cq[own, : 2 * HD], a) + nt(cq[own, 2 * HD : 3 * HD], b) + nt(cq[own, 3 * HD :], v)
        part[m] = (out * scale).astype(BF)
    rows = piece_rows()
    one = total_start(post, part, t1, rows, c, mate)
    two = total_across(post, part, t1, th, t2, rows, c, far, one)

    def multiply(left, right, out_ref, width, base, tile):
        def body(t, carry):
            cols = pl.ds(pl.multiple_of(t * tile, tile), tile)
            outs = pl.ds(pl.multiple_of(base + t * tile, 256), tile)
            out = nn(left[...].reshape(PART, 1024), right[:, cols])
            out_ref[:, :, :, outs] = out.reshape(2, 4, SHARE, tile).astype(BF)
            return carry

        lax.fori_loop(0, width // tile, body, 0)

    def spread(p, land, along):
        if along == "y":
            return [post(p.at[:, yi[j]], land.at[j], ys[j]) for j in range(3)]
        return [post(p.at[:, xi[j]], land.at[j], xs[j]) for j in range(3)]

    def reduce(p, land, half, own, arrivals, across):
        for copy in arrivals:
            copy.wait_recv()

        def body(t, carry):
            cols = pl.ds(pl.multiple_of(t * 128, 128), 128)
            for zi in range(2):
                out = p[zi, own, :, cols].astype(F32)
                for j in range(3):
                    out = out + land[j, zi, :, cols].astype(F32)
                half[zi, :, cols] = out.astype(BF)
            return carry

        lax.fori_loop(0, half.shape[-1] // 128, body, 0)
        return post(half.at[1 - z], across, zp)

    def finish(copy, half, across, out):
        copy.wait_recv()
        out[...] = half[z].astype(F32) + across[...].astype(F32)

    for copy in got_g:
        copy.wait()
    multiply(dg, c0, pg, D, 0, 768)
    two_g = spread(pg, rg, "y")
    got_d = [load(ch_in, c0)]
    for copy in got_u:
        copy.wait()
    multiply(dd, c1, pu, D, 0, 768)
    two_u = spread(pu, ru, "x")
    got_d.append(load(dd_in, dd))
    total_end(post, total_ref, th, t2, rows, c, mate, two)

    for copy in got_t:
        copy.wait()
    sums = jnp.zeros((1, D), F32)
    for m in range(2):

        def slab(i, carry):
            r = pl.ds(pl.multiple_of(i * 16, 16), 16)
            back, more = norm_grad(tok[m, r].astype(F32), gain_in[...], total_ref[m, r].astype(F32))
            igrad[m, r] = (mgrad[m, r] + back).astype(BF)
            return carry + more

        sums = lax.fori_loop(0, ROWS // 16, slab, sums)
    gpad[...] = jnp.zeros_like(gpad)
    gpad[0:1] = sums
    gpad[1:4] = gains_in[...]
    turned = gpad[...].T.astype(BF)
    for zi in range(2):
        for k in range(4):
            at = (zi * 4 + k) * 288
            gb[zi, k] = turned[at : at + 288]
    gains_far = [post(gb.at[:, yi[j]], rgb.at[j], ys[j]) for j in range(3)]

    for copy in got_d:
        copy.wait()
    multiply(dd, c0, pd, D, 0, 768)
    two_d = spread(pd, rd, "x")
    for copy in got_q:
        copy.wait()
    for copy in got_q_far:
        copy.wait_recv()
    multiply(dn, cq, pq, 1024, 0, 512)
    multiply(db, ca, pq, 512, 1024, 512)
    two_q = spread(pq, rq, "x")
    out = gb[:, y].astype(F32)
    for j in range(3):
        gains_far[j].wait_recv()
        out = out + rgb[j].astype(F32)
    pn[...] = out.reshape(2, 4, SHARE, 128).astype(BF)
    two_n = spread(pn, rn, "x")
    three_g = reduce(pg, rg, sg, y, two_g, zg)
    three_u = reduce(pu, ru, su, x, two_u, zu)
    finish(three_g, sg, zg, og)
    finish(three_u, su, zu, ou)
    three_d = reduce(pd, rd, sd, x, two_d, zd)
    three_q = reduce(pq, rq, sq, x, two_q, zq)
    three_n = reduce(pn, rn, sn, x, two_n, zn)
    finish(three_d, sd, zd, od)
    finish(three_q, sq, zq, oq)
    finish(three_n, sn, zn, on)
    for copy in copies:
        copy.wait_send()


def end(key, value, dq, cosine, sine, gain_in, gains, bt, wq, wk, wv, tok, mgrad, dg, cg, du, cu, dd, ch, dn, ca, scale):
    def kernel(*refs):
        end_kernel(*refs, scale)

    widths = (D, D, D, 1536, 128)
    sems = 6 + 12 + 3 + 15 + 5
    return pl.pallas_call(
        kernel,
        out_shape=[jax.ShapeDtypeStruct((2, ROWS, D), BF)]
        + [jax.ShapeDtypeStruct((SHARE, w), F32) for w in widths],
        in_specs=[whole()] * 7 + [whole(pl.ANY)] * 14,
        out_specs=[whole()] * 6,
        scratch_shapes=[
            VMEM(wq.shape, BF),
            VMEM(wk.shape, BF),
            VMEM(wv.shape, BF),
            VMEM(tok.shape, BF),
            VMEM(mgrad.shape, F32),
            VMEM(dg.shape, BF),
            VMEM(cg.shape, BF),
            VMEM(dd.shape, BF),
            VMEM(ch.shape, BF),
            VMEM(dn.shape, BF),
            VMEM(ca.shape, BF),
            VMEM((2, 288, 1024), BF),
            VMEM((1024, 1024), BF),
            VMEM((2, ROWS, D), BF),
            VMEM((ROWS, D), BF),
            VMEM((ROWS, D), BF),
            VMEM((ROWS, D), BF),
            VMEM((2, ROWS, D), BF),
            VMEM((128, D), F32),
            VMEM((2, 4, 288, 128), BF),
            VMEM((3, 2, 288, 128), BF),
        ]
        + [VMEM((2, 4, SHARE, w), BF) for w in widths]
        + [VMEM((3, 2, SHARE, w), BF) for w in widths]
        + [VMEM((2, SHARE, w), BF) for w in widths]
        + [VMEM((SHARE, w), BF) for w in widths]
        + [
            pltpu.SemaphoreType.DMA((14,)),
            pltpu.SemaphoreType.DMA((sems,)),
            pltpu.SemaphoreType.DMA((sems,)),
        ],
        compiler_params=params(3, 63),
    )(key, value, dq, cosine, sine, gain_in, gains, bt, wq, wk, wv, tok, mgrad, dg, cg, du, cu, dd, ch, dn, ca)


def shards(
    inputs,
    out_grad,
    segment_ids,
    keep_mask,
    query_codes,
    key_codes,
    value_codes,
    output_codes,
    gate_codes,
    up_codes,
    down_codes,
    norm_attn_in,
    norm_attn_out,
    norm_ffn_in,
    norm_ffn_out,
):
    rows = inputs.shape[1]
    place = lax.axis_index("blk") * rows + jnp.arange(rows, dtype=jnp.int32)
    freqs = 10000.0 ** (-jnp.arange(HD // 2, dtype=F32) * 2.0 / HD)
    angles = place.astype(F32)[:, None] * freqs[None, :]
    cosine = jnp.cos(angles)
    sine = jnp.sin(angles)
    in_scale = LEVEL_SCALE * D ** (-0.5)
    mid_scale = LEVEL_SCALE * (HEADS * HD) ** (-0.5)
    ff_scale = LEVEL_SCALE * FF ** (-0.5)

    def both(left):
        return left.reshape(2 * rows, left.shape[-1])

    key_tag = jnp.where(keep_mask == 1, segment_ids, -1).astype(BF)
    key_tag = jnp.concatenate([key_tag, jnp.zeros_like(key_tag)], axis=1)
    key_tag = jnp.broadcast_to(key_tag[:, None, :], (2, 16, 2 * rows))
    tag = segment_ids.astype(F32)
    tag = jnp.concatenate([tag, tag], axis=1)[:, :, None]
    (
        middle, branch, ffn_in, queries, attended, lse, ffn_turned, blocks_a, blocks_b, d_normed, all_attended,
    ) = front(
        norm_attn_in[None], norm_attn_out[None], norm_ffn_in[None], cosine, sine, key_tag, tag,
        inputs, query_codes, key_codes, value_codes, output_codes, in_scale, mid_scale,
    )
    out_rows, gate_low, up_low, ffn_in_grad, gain_ffn_out, ch, d_down, d_gate = ffn(
        ffn_in, norm_ffn_out[None], gate_codes, up_codes, down_codes, middle, out_grad,
        ffn_turned.reshape(8, 4, SHARE, 2 * rows).transpose(1, 0, 2, 3).reshape(4, PART, 2 * rows),
        in_scale, ff_scale,
    )
    key_rot, value_grad, query_rot, middle_grad, d_branch, gains, cg, cu, d_up = mid(
        ffn_in_grad, norm_ffn_in[None], norm_attn_out[None], queries, lse, tag, attended,
        middle, branch, out_grad, output_codes, blocks_a, blocks_b,
        both(gate_low), both(up_low), ffn_turned, mid_scale,
    )
    gains = jnp.concatenate([gains, gain_ffn_out])
    input_grad, g_gate, g_up, g_down, g_rest, g_gains = end(
        key_rot, value_grad, query_rot, cosine, sine, norm_attn_in[None], gains,
        d_branch, query_codes, key_codes, value_codes, inputs, middle_grad,
        d_gate, cg, d_up, cu, d_down, ch, d_normed, all_attended, in_scale,
    )
    return (
        out_rows,
        input_grad,
        g_rest[:, :512] * in_scale,
        g_rest[:, 512:768] * in_scale,
        g_rest[:, 768:1024] * in_scale,
        g_rest[:, 1024:1536].T * mid_scale,
        g_gate * in_scale,
        g_up * in_scale,
        g_down.T * ff_scale,
        g_gains[:, 0],
        g_gains[:, 1],
        g_gains[:, 2],
        g_gains[:, 3],
    )


def solution(mesh):
    placed = (
        P(None, "blk", None),
        P(None, "blk", None),
        P(None, "blk"),
        P(None, "blk"),
        P(None, "tensor"),
        P(None, "tensor"),
        P(None, "tensor"),
        P("tensor", None),
        P(None, "tensor"),
        P(None, "tensor"),
        P("tensor", None),
        P(),
        P(),
        P(),
        P(),
    )
    return jax.shard_map(
        shards,
        mesh=mesh,
        in_specs=placed,
        out_specs=(
            P(None, "blk", None),
            P(None, "blk", None),
            P("blk", "tensor"),
            P("blk", "tensor"),
            P("blk", "tensor"),
            P("tensor", "blk"),
            P("blk", "tensor"),
            P("blk", "tensor"),
            P("tensor", "blk"),
            P("blk"),
            P("blk"),
            P("blk"),
            P("blk"),
        ),
        check_vma=False,
    )
```

time: 516 us -> 428 us (0.83)
  Pallas kernels: 467 us -> 401 us
  other arithmetic: 17.4 us -> 8.49 us
  matrix products: 7.08 us -> 0 us
  local copies, waits for them, and re-layouts: 19.9 us -> 14.1 us
    pallas_call x1, Pallas kernels: 191 us -> 123 us  [mid(): pl.pallas_call(kernel, out_shape=[jax.ShapeDtypeStruct(tile, F32), jax.Sh...]
    pallas_call x6 -> x2, Pallas kernels: 159 us -> 173 us  [the longest x1 88.3 us: front(): pl.pallas_call(kernel, out_shape=[jax.ShapeDtypeStruct(both, F32), jax.Sh...]
    pallas_call x1, Pallas kernels: 117 us -> 106 us  [end(): pl.pallas_call(kernel, out_shape=[jax.ShapeDtypeStruct((2, ROWS, D), BF)]...]
    dot_general x8 -> x0, matrix products: 7.08 us -> none  [nn(): return jnp.dot(left, right, preferred_element_type=F32)]
where the time goes in v3:
time: 428 us; the launch traced here: 424 us
  Pallas kernels  401 us (94%)
  local copies, waits for them, and re-layouts  14.1 us (3%)
  other arithmetic  8.49 us (2%)
    pallas_call x1, Pallas kernels, mid(): pl.pallas_call(kernel, out_shape=[jax.ShapeDtypeStruct(tile, F32), jax.Sh...  123 us
    pallas_call x1, Pallas kernels, end(): pl.pallas_call(kernel, out_shape=[jax.ShapeDtypeStruct((2, ROWS, D), BF)]...  106 us
    pallas_call x1, Pallas kernels, front(): pl.pallas_call(kernel, out_shape=[jax.ShapeDtypeStruct(both, F32), jax.Sh...  88.3 us
    pallas_call x1, Pallas kernels, ffn(): pl.pallas_call(kernel, out_shape=[jax.ShapeDtypeStruct(both, BF), jax.Sha...  84.4 us

profile of v3, /device:TPU:1, one launch (start us, length us, event | category | flops | bytes accessed | tf_op | source)
XLA Modules:
  0.0 424.3 jit_solution(15091894127342047733)
XLA Ops:
  0.7 0.8 fusion.1
  1.5 1.3 broadcast_in_dim.16.refs_0_.refs_5_
  2.8 1.3 broadcast_in_dim.32.refs_1_.refs_2_
  4.1 1.3 broadcast_in_dim.33.refs_2_.refs_1_
  5.4 1.3 broadcast_in_dim.37.refs_1_
  6.7 0.6 broadcast_in_dim.35.refs_5_
  7.3 1.0 multiply_sine_fusion
  8.3 0.9 copy.29.refs_6_.refs_5_
  9.1 88.3 %shard_map.246 = (f32[2,128,2304]{2,1,0:T(8,128)}, bf16[2,128,2304]{2,1,0:T(8,128)(2,1)}, bf16[2,128,2304]{2,1,0:T(8,128)(2,1)}, bf16[2,256,256]{2,1,0:T(8,128)(...) custom-call(f32[1,2304]{1,0:T(1,128)} %broadcast_in_dim.16.refs_0_.r, ...), custom_call_target="tpu_custom_call" | custom-call | tf_op jit(solution)/shard_map/pallas_call | solution.py:424
  97.4 2.4 copy.30
  99.8 84.4 %shard_map.247 = (bf16[2,128,2304]{2,1,0:T(8,128)(2,1)}, bf16[2,128,2304]{2,1,0:T(8,128)(2,1)}, bf16[2,128,2304]{2,1,0:T(8,128)(2,1)}, bf16[2,128,2304]{2,1,0:T(...) custom-call(bf16[2,128,2304]{2,1,0:T(8,128)(2,1)} %get-tuple-element, ...), custom_call_target="tpu_custom_call" | custom-call | tf_op jit(solution)/shard_map/pallas_call | solution.py:683
  184.1 0.0 copy-start.5
  184.1 122.6 %shard_map.248 = (f32[256,256]{1,0:T(8,128)}, f32[256,256]{1,0:T(8,128)}, f32[2,256,256]{2,1,0:T(8,128)}, f32[2,128,2304]{2,1,0:T(8,128)}, bf16[2,4,288,256]{3,2...) custom-call(bf16[2,128,2304]{2,1,0:T(8,128)(2,1)} %get-tuple-element, ...), custom_call_target="tpu_custom_call" | custom-call | tf_op jit(solution)/shard_map/pallas_call | solution.py:937
  306.8 0.0 copy-done.5
  306.8 1.4 pad_maximum_fusion.refs_6_
  308.2 105.7 %shard_map.249 = (bf16[2,128,2304]{2,1,0:T(8,128)(2,1)}, f32[72,2304]{1,0:T(8,128)}, f32[72,2304]{1,0:T(8,128)}, f32[72,2304]{1,0:T(8,128)}, f32[72,1536]{1,0:T(8,128)}, /*index=5*/f32[72,128]{1,0:T(8,128)}) custom-call(f32[256,256]{1,0:T(8,128)} %get-tuple-element.60.refs_0_, f32[256,256]{1,0:T(8,128)} %get-tuple-element.61.refs_1_, ...), custom_call_target="tpu_custom_call" | custom-call | tf_op jit(solution)/shard_map/pallas_call | solution.py:1146
  413.9 0.0 copy-start.2
  413.9 0.0 copy-start.3
  413.9 0.0 copy-start.4
  413.9 1.7 slice_reduce_fusion
  415.6 1.6 slice_multiply_fusion.1
  417.2 1.7 multiply_bitcast_fusion.1
  418.9 0.0 copy-done.2
  418.9 0.9 broadcast_multiply_fusion.1
  419.8 0.0 copy-done.3
  419.8 0.0 copy-done.4
  419.8 0.0 copy-start
  419.8 1.2 multiply_bitcast_fusion
  421.0 0.6 copy-done
  421.6 0.0 copy-start.1
  421.6 1.0 copy.34
  422.6 0.7 copy-done.1
  423.3 1.0 copy.35
  (4 shorter events, 0.0 us)
Async XLA Ops:
  184.1 122.7 %copy-start.5 = (f32[1,2304]{1,0:T(1,128)S(1)}, f32[1,2304]{1,0:T(1,128)}, u32[]{:S(2)}) copy-start(f32[1,2304]{1,0:T(1,128)} %get-tuple-element.64) | copy-start | bytes 27652
  413.9 5.1 %copy-start.2 = (f32[72,2304]{1,0:T(8,128)S(1)}, f32[72,2304]{1,0:T(8,128)}, u32[]{:S(2)}) copy-start(f32[72,2304]{1,0:T(8,128)} %get-tuple-element.77) | copy-start | bytes 1990660
  413.9 6.0 %copy-start.3 = (f32[72,2304]{1,0:T(8,128)S(1)}, f32[72,2304]{1,0:T(8,128)}, u32[]{:S(2)}) copy-start(f32[72,2304]{1,0:T(8,128)} %get-tuple-element.78) | copy-start | bytes 1990660
  413.9 5.9 %copy-start.4 = (f32[72,2304]{1,0:T(8,128)S(1)}, f32[72,2304]{1,0:T(8,128)}, u32[]{:S(2)}) copy-start(f32[72,2304]{1,0:T(8,128)} %get-tuple-element.79) | copy-start | bytes 1990660
  419.8 1.8 copy-start
  421.6 1.7 copy-start.1
